TPU v7x, 512 devices: a whole 4x4x16 slice. The times are simulated.
512 devices in a mesh: gx: 8 (over y, z_hi), gy: 8 (over z_lo), gz: 8 (over x, core).
Axes of the slice: x: 4, y: 4, z: 16 (z_hi: 2, z_lo: 8; z = z_hi * 8 + z_lo), core: 2. Of those that a mesh axis runs over, the one named last changes fastest.
Arguments:
- tokens: bfloat16 [1024, 8192], P('gx', 'gz'), may hold values from -6 to 6
- gate_weight: bfloat16 [8192, 14336], P('gz', ('gx', 'gy')), may hold values from -0.0625 to 0.0625
- up_weight: bfloat16 [8192, 14336], P('gz', ('gx', 'gy')), may hold values from -0.0625 to 0.0625
- down_weight: bfloat16 [14336, 8192], P(('gx', 'gy'), 'gz'), may hold values from -0.046875 to 0.046875
- out_grad: bfloat16 [1024, 8192], P('gx', 'gz'), may hold values from -6 to 6
Outputs:
- output: bfloat16 [1024, 8192], P('gx', 'gz')
- input_grad: bfloat16 [1024, 8192], P('gx', 'gz')
- gate_grad: bfloat16 [8192, 14336], P('gz', ('gx', 'gy'))
- up_grad: bfloat16 [8192, 14336], P('gz', ('gx', 'gy'))
- down_grad: bfloat16 [14336, 8192], P(('gx', 'gy'), 'gz')
All inputs are finite; a program needn't handle non-finite values.
Results may differ from a plain program's by a relative error of at most 0.025.
Values may be sent and summed in bfloat16 or wider, within the bound.
No kernel may reach another device: no remote copies, remote signals or barrier semaphores. Data moves between devices by JAX's collectives and lax.ppermute only.
A program may use at most 64 MiB of HBM per device.

v0:
```python
import jax
import jax.numpy as jnp
from jax import lax
from jax.sharding import Mesh
from jax.sharding import PartitionSpec as P

GX = ("gx_0", "gx_1")
GX_GY = ("gx_0", "gx_1", "gy")


def side_by_side(arrays, axis, dim, along):
    both = jnp.concatenate(arrays, axis=along)
    out, at, finished = (lax.psum_scatter(both, axis, scatter_dimension=dim, tiled=True), 0, [])
    for a in arrays:
        finished.append(lax.slice_in_dim(out, at, at + a.shape[along], axis=along))
        at += a.shape[along]
    return tuple(finished)


def copy_for_each(shard, axis):
    devices = lax.axis_size(axis)
    return lax.all_to_all(
        jnp.broadcast_to(shard[None], (devices, *shard.shape)), axis, 0, 0, tiled=True
    )


def in_order(tiles, dim):
    tiles = jnp.moveaxis(tiles, 0, dim)
    shape = tiles.shape
    return tiles.reshape(*shape[:dim], shape[dim] * shape[dim + 1], *shape[dim + 2 :])


def collect(shard, axis, dim):
    tiles = copy_for_each(shard, axis)
    return in_order(tiles, dim)


def gathered_by_axis(shard, axes, dim):
    if not axes:
        return shard
    nearer = lax.all_gather(shard, axes[-1], axis=dim, tiled=True)
    return gathered_by_axis(nearer, axes[:-1], dim)


def of_everyone(shard, axis):
    everything = copy_for_each(shard, axis)
    return jnp.sum(everything.astype(jnp.float32), axis=0)


def cut_along(shard, dim, devices):
    before, after = (shard.shape[:dim], shard.shape[dim + 1 :])
    return jnp.moveaxis(shard.reshape(*before, devices, -1, *after), dim, 0)


def summed_on_arrival(shard, axis, dim):
    devices = lax.axis_size(axis)
    tiles = lax.all_to_all(cut_along(shard, dim, devices), axis, 0, 0, tiled=True)
    return jnp.sum(tiles.astype(jnp.float32), axis=0)


def sent_together(arrays, axis, dim, along):
    widths = [a.shape[along] for a in arrays]
    both = jnp.concatenate(arrays, axis=along)
    out = lax.all_gather(both, axis, axis=dim, tiled=True)
    return tuple(jnp.split(out, [sum(widths[:k]) for k in range(1, len(widths))], axis=along))


def contract_rows(left, right):
    return lax.dot_general(
        left, right, (((0,), (0,)), ((), ())), preferred_element_type=jnp.float32
    )


def contract_cols(left, right):
    return lax.dot_general(
        left, right, (((1,), (1,)), ((), ())), preferred_element_type=jnp.float32
    )


def activate(gate, upward):
    sigmoid = jax.nn.sigmoid(gate)
    hidden = (gate * sigmoid * upward).astype(jnp.bfloat16)
    return (hidden, sigmoid)


def backward_gates(dhidden, gate, upward, sigmoid):
    dgate = (dhidden * upward * sigmoid * (1.0 + gate * (1.0 - sigmoid))).astype(jnp.bfloat16)
    dupward = (dhidden * gate * sigmoid).astype(jnp.bfloat16)
    return (dgate, dupward)


def body(tokens, gate_weight, up_weight, down_weight, out_grad):
    all_tokens = lax.all_gather(tokens, GX, axis=0, tiled=True)
    gate_part = jnp.dot(all_tokens, gate_weight, preferred_element_type=jnp.float32)
    up_part = jnp.dot(all_tokens, up_weight, preferred_element_type=jnp.float32)
    gate, upward = tuple(
        (
            part.astype(jnp.float32)
            for part in side_by_side(
                (gate_part.astype(jnp.bfloat16), up_part.astype(jnp.bfloat16)), "gz", 0, 1
            )
        )
    )
    hidden_own, sigmoid = activate(gate, upward)
    hidden_all = collect(hidden_own, "gz", 0)
    hidden_mine = lax.all_to_all(hidden_all, GX, split_axis=0, concat_axis=1, tiled=True)
    output_part = jnp.dot(
        hidden_mine, gathered_by_axis(down_weight, GX, 0), preferred_element_type=jnp.float32
    )
    output = (
        of_everyone(output_part.astype(jnp.bfloat16), "gy").astype(jnp.float32).astype(jnp.bfloat16)
    )
    all_grad = lax.all_gather(out_grad, GX, axis=0, tiled=True)
    dhidden_part = contract_cols(all_grad, down_weight)
    dhidden = summed_on_arrival(dhidden_part.astype(jnp.bfloat16), "gz", 0)
    dgate_own, dup_own = backward_gates(dhidden, gate, upward, sigmoid)
    dgate_all, dup_all = sent_together((dgate_own, dup_own), "gz", 0, 1)
    input_part = lax.psum_scatter(
        (contract_cols(dgate_all, gate_weight) + contract_cols(dup_all, up_weight)).astype(
            jnp.bfloat16
        ),
        GX,
        scatter_dimension=0,
        tiled=True,
    )
    input_grad = of_everyone(input_part, "gy").astype(jnp.float32).astype(jnp.bfloat16)
    gate_grad = contract_rows(all_tokens, dgate_all).astype(jnp.bfloat16)
    up_grad = contract_rows(all_tokens, dup_all).astype(jnp.bfloat16)
    down_grad = contract_rows(hidden_all, all_grad).astype(jnp.bfloat16)
    return (output, input_grad, gate_grad, up_grad, down_grad)


def solution(mesh):
    finer = Mesh(
        mesh.devices.reshape(4, 2, mesh.shape["gy"], mesh.shape["gz"]), ("gx_0", "gx_1", "gy", "gz")
    )
    in_specs = (P(GX, "gz"), P("gz", GX_GY), P("gz", GX_GY), P(GX_GY, "gz"), P(GX, "gz"))
    out_specs = (P(GX, "gz"), P(GX, "gz"), P("gz", GX_GY), P("gz", GX_GY), P(GX_GY, "gz"))
    return jax.shard_map(body, mesh=finer, in_specs=in_specs, out_specs=out_specs, check_vma=False)
```

profile of v0, /device:TPU:2, one launch (start us, length us, event | category | flops | bytes accessed | tf_op | source)
XLA Modules:
  0.0 693.5 jit_solution(4162685620083025210)
XLA Ops:
  7.2 0.0 copy-start
  7.2 0.0 all-gather.4.cloned.1.call-start
  7.2 0.7 all-gather.4.cloned.1.call-update
  7.9 0.0 all-gather.8.cloned.1.call-start
  8.0 0.7 all-gather.8.cloned.1.call-update
  8.7 0.0 reduce-scatter.7.cloned.1.call-start
  8.7 123.5 %all-gather.4.cloned.1.call-done = bf16[1024,1024]{1,0:T(8,128)(2,1)} async-done(((bf16[128,1024]{1,0:T(8,128)(2,1)}), bf16[1024,1024]{1,0:T(8,128)(2,1)}) %all-gather.4.cloned.1.call-update) | async-done | bytes 2097168 | tf_op jit(solution)/shard_map/all_gather | solution.py:93
  132.2 0.0 copy-start.3
  132.2 2.6 convolution_convert_fusion.4
  134.8 0.0 copy-done
  134.8 0.0 copy-done.3
  134.8 0.8 convolution_convert_fusion.5
  135.6 0.0 copy-start.2
  135.6 0.1 pad_maximum_fusion
  135.7 1.3 copy.16
  137.0 0.0 reduce-scatter.7.cloned.1.call-update
  137.0 0.0 all-gather.6.cloned.1.call-start
  137.0 0.0 copy-done.2
  137.1 23.9 %all_gather.16 = bf16[448,1024]{1,0:T(8,128)(2,1)} all-gather(bf16[224,1024]{1,0:T(8,128)(2,1)S(1)} %copy-done.2), channel_id=1, replica_groups=mesh['gx_0'=4,'gx_1'=2,'gy'=8,'gz'=8] {'gx_1'}, dimensions={0}, use_global_device_ids=true | all-gather | bytes 1376256 | tf_op jit(solution)/shard_map/all_gather | solution.py:41
  160.9 0.0 all-gather.6.cloned.1.call-update
  161.0 110.2 %all-gather.8.cloned.1.call-done = bf16[1024,1024]{1,0:T(8,128)(2,1)} async-done(((bf16[128,1024]{1,0:T(8,128)(2,1)}), bf16[1024,1024]{1,0:T(8,128)(2,1)}) %all-gather.8.cloned.1.call-update) | async-done | bytes 2097168 | tf_op jit(solution)/shard_map/all_gather | solution.py:113
  271.2 2.4 fusion
  273.6 0.1 copy.27
  273.7 12.8 %all_to_all.36 = bf16[8,128,224]{1,2,0:T(8,128)(2,1)S(1)} all-to-all(bf16[8,128,224]{1,2,0:T(8,128)(2,1)S(1)} %bitcast.34), channel_id=1, replica_groups=mesh['gx_0'=4,'gx_1'=2,'gy'=8,'gz'=8] {'gz'}, dimensions={0} | all-to-all | bytes 917504 | tf_op jit(solution)/shard_map/all_to_all | solution.py:57
  286.5 0.1 convert_reduce_fusion
  286.5 19.3 %reduce-scatter.7.cloned.1.call-done = bf16[128,448]{1,0:T(8,128)(2,1)} async-done(((bf16[1024,448]{1,0:T(8,128)(2,1)}), bf16[128,448]{1,0:T(8,128)(2,1)}) %reduce-scatter.7.cloned.1.call-update) | async-done | bytes 114704
  305.8 1.1 fusion.20
  306.9 0.1 copy.18
  307.0 0.1 copy.19
  307.1 0.1 fusion.13
  307.2 0.1 broadcast_in_dim.6
  307.3 14.9 %all_to_all.37 = bf16[8,128,224]{1,2,0:T(8,128)(2,1)} all-to-all(bf16[8,128,224]{1,2,0:T(8,128)(2,1)S(1)} %broadcast_in_dim.6), channel_id=1, replica_groups=mesh['gx_0'=4,'gx_1'=2,'gy'=8,'gz'=8] {'gz'}, dimensions={0} | all-to-all | bytes 917504 | tf_op jit(solution)/shard_map/all_to_all | solution.py:22
  322.1 14.5 %all-to-all-start.1 = ((bf16[8,128,224]{1,2,0:T(8,128)(2,1)}), bf16[8,128,224]{1,2,0:T(8,128)(2,1)S(1)}, u32[]{:S(2)}, u32[]{:S(2)}) async-start(bf16[8,128,224]{1,2,0:T(8,128)(2,1)} %all_to_all.37), calls=%async_computation.1 | async-start | bytes 917504 | tf_op jit(solution)/shard_map/all_to_all | solution.py:106
  336.6 29.5 %all-gather.6.cloned.1.call-done = bf16[1792,1024]{1,0:T(8,128)(2,1)} async-done(((bf16[448,1024]{1,0:T(8,128)(2,1)}), bf16[1792,1024]{1,0:T(8,128)(2,1)}) %all-gather.6.cloned.1.call-update) | async-done | bytes 3670032 | tf_op jit(solution)/shard_map/all_gather | solution.py:41
  366.1 0.0 all-to-all-done.1
  366.1 2.7 convolution_convert_fusion.6
  368.9 1.6 broadcast_in_dim.7
  370.5 10.0 %all-to-all-start.2 = ((bf16[8,128,1024]{2,1,0:T(8,128)(2,1)}), bf16[8,128,1024]{2,1,0:T(8,128)(2,1)S(1)}, u32[]{:S(2)}, u32[]{:S(2)}) async-start(bf16[8,128,1024]{2,1,0:T(8,128)(2,1)} %broadcast_in_dim.7), calls=%async_computation.2 | async-start | bytes 4194304 | tf_op jit(solution)/shard_map/all_to_all | solution.py:22
  380.5 0.0 reduce-scatter.5.cloned.1.call-start
  380.5 14.3 %all_gather.19 = bf16[1024,448]{0,1:T(8,128)(2,1)S(1)} all-gather(bf16[128,448]{0,1:T(8,128)(2,1)S(1)} %pad_maximum_fusion.1), channel_id=1, replica_groups=mesh['gx_0'=4,'gx_1'=2,'gy'=8,'gz'=8] {'gz'}, dimensions={0}, use_global_device_ids=true | all-gather | bytes 1032192 | tf_op jit(solution)/shard_map/all_gather | solution.py:64
  394.8 0.0 copy-start.1
  394.8 0.8 fusion.8
  395.6 0.3 copy-done.1
  395.8 2.1 add_convert_fusion
  398.0 0.0 reduce-scatter.5.cloned.1.call-update
  398.0 184.5 %reduce-scatter.5.cloned.1.call-done = bf16[128,1024]{1,0:T(8,128)(2,1)} async-done(((bf16[1024,1024]{1,0:T(8,128)(2,1)}), bf16[128,1024]{1,0:T(8,128)(2,1)}) %reduce-scatter.5.cloned.1.call-update) | async-done | bytes 262160 | tf_op jit(solution)/shard_map/reduce_scatter | solution.py:118
  582.5 0.0 all-to-all-done.2
  582.5 2.6 broadcast_in_dim.8
  585.0 4.3 all-to-all-start.4
  589.4 0.0 copy-start.4
  589.4 3.2 fusion.1
  592.6 0.0 copy-done.4
  592.6 0.0 copy-start.5
  592.6 1.4 fusion.2
  594.0 0.2 copy-done.5
  594.2 2.4 convolution_convert_fusion
  596.6 1.1 reduce_sum.33
  597.7 86.6 %all-to-all-done.4 = bf16[8,128,1024]{2,1,0:T(8,128)(2,1)} async-done(((bf16[8,128,1024]{2,1,0:T(8,128)(2,1)}), bf16[8,128,1024]{2,1,0:T(8,128)(2,1)}, u32[]{:S(2)}, u32[]{:S(2)}) %all-to-all-start.4) | async-done | bytes 2097184 | tf_op jit(solution)/shard_map/all_to_all | solution.py:22
  684.3 2.7 reduce_sum.35
  (1 shorter events, 0.0 us)
Async XLA Ops:
  7.2 127.6 %copy-start = (bf16[1024,224]{0,1:T(8,128)(2,1)S(1)}, bf16[1024,224]{0,1:T(8,128)(2,1)}, u32[]{:S(2)}) copy-start(bf16[1024,224]{0,1:T(8,128)(2,1)} %param.6) | copy-start | bytes 1376260
  7.2 125.0 %all-gather.4.cloned.1.call-start = ((), (), s32[]{:S(2)}) async-start(), calls=%async_computation.7 | async-start | bytes 2359296 | tf_op jit(solution)/shard_map/all_gather | solution.py:93
  7.9 263.3 %all-gather.8.cloned.1.call-start = ((), (), s32[]{:S(2)}) async-start(), calls=%async_computation.9 | async-start | bytes 2359296 | tf_op jit(solution)/shard_map/all_gather | solution.py:113
  8.7 297.1 %reduce-scatter.7.cloned.1.call-start = ((), (), s32[]{:S(2)}) async-start(), calls=%async_computation.11 | async-start | bytes 1179648
  132.2 2.6 copy-start.3
  135.6 1.4 copy-start.2
  137.0 229.1 %all-gather.6.cloned.1.call-start = ((), (), s32[]{:S(2)}) async-start(), calls=%async_computation.8 | async-start | bytes 4587520 | tf_op jit(solution)/shard_map/all_gather | solution.py:41
  322.1 44.0 %all-to-all-start.1 = ((bf16[8,128,224]{1,2,0:T(8,128)(2,1)}), bf16[8,128,224]{1,2,0:T(8,128)(2,1)S(1)}, u32[]{:S(2)}, u32[]{:S(2)}) async-start(bf16[8,128,224]{1,2,0:T(8,128)(2,1)} %all_to_all.37), calls=%async_computation.1 | async-start | bytes 917504 | tf_op jit(solution)/shard_map/all_to_all | solution.py:106
  370.5 212.0 %all-to-all-start.2 = ((bf16[8,128,1024]{2,1,0:T(8,128)(2,1)}), bf16[8,128,1024]{2,1,0:T(8,128)(2,1)S(1)}, u32[]{:S(2)}, u32[]{:S(2)}) async-start(bf16[8,128,1024]{2,1,0:T(8,128)(2,1)} %broadcast_in_dim.7), calls=%async_computation.2 | async-start | bytes 4194304 | tf_op jit(solution)/shard_map/all_to_all | solution.py:22
  380.5 202.0 %reduce-scatter.5.cloned.1.call-start = ((), (), s32[]{:S(2)}) async-start(), calls=%async_computation.10 | async-start | bytes 2359296 | tf_op jit(solution)/shard_map/reduce_scatter | solution.py:118
  394.8 1.0 copy-start.1
  585.0 99.2 %all-to-all-start.4 = ((bf16[8,128,1024]{2,1,0:T(8,128)(2,1)}), bf16[8,128,1024]{2,1,0:T(8,128)(2,1)}, u32[]{:S(2)}, u32[]{:S(2)}) async-start(bf16[8,128,1024]{2,1,0:T(8,128)(2,1)} %broadcast_in_dim.8), calls=%async_computation.5 | async-start | bytes 4194304 | tf_op jit(solution)/shard_map/all_to_all | solution.py:22
  589.4 3.2 copy-start.4
  592.6 1.6 copy-start.5
Sparse Core Ops, SparseCore 0:
  11.2 120.9 all-gather.3
  135.4 135.7 all-gather.7
  274.0 31.7 reduce-scatter.6
  307.8 58.3 all-gather.5
  398.1 184.3 reduce-scatter.4
where the time goes:
time: 694 us
  waiting for transfers between devices  555 us (80%)
  blocking collectives  65.8 us (9%)
  starting transfers between devices  29.1 us (4%)
  matrix products  18.3 us (3%)
  between operations  13.9 us (2%)
  local copies, waits for them, and re-layouts  7.4 us (1%)
    reduce_scatter x1, waiting for transfers between devices, body(): lax.psum_scatter((contract_cols(dgate_all, gate_weight) + contract_cols(d...  184 us
    all_gather x1, waiting for transfers between devices, body(): all_tokens = lax.all_gather(tokens, GX, axis=0, tiled=True)  123 us
    all_gather x1, waiting for transfers between devices, body(): all_grad = lax.all_gather(out_grad, GX, axis=0, tiled=True)  110 us
    all_to_all x2, waiting for transfers between devices, copy_for_each(): lax.all_to_all(jnp.broadcast_to(shard[None], (devices, *shard.shape)), ax...  86.6 us
    all_gather x1, waiting for transfers between devices, gathered_by_axis(): nearer = lax.all_gather(shard, axes[-1], axis=dim, tiled=True)  29.5 us
    all_gather x1, blocking collectives, gathered_by_axis(): nearer = lax.all_gather(shard, axes[-1], axis=dim, tiled=True)  23.9 us
    unnamed x6, waiting for transfers between devices  20.7 us
    all_to_all x1, blocking collectives, copy_for_each(): lax.all_to_all(jnp.broadcast_to(shard[None], (devices, *shard.shape)), ax...  14.9 us
  transfers between devices with their start and end apart: 8, of which 6 were waited for; matrix products, arithmetic and copies ran while one was open for 3% of the time, Pallas kernels for 0%

commit v1 on v0

v1 whole, which is shorter than its diff:
```python
import jax
import jax.numpy as jnp
from jax import lax
from jax.sharding import Mesh
from jax.sharding import PartitionSpec as P

GZ = ("x", "c")
Z = ("zh", "zl")


def give_all(shard, axis):
    devices = lax.axis_size(axis)
    return lax.all_to_all(
        jnp.broadcast_to(shard[None], (devices, *shard.shape)), axis, 0, 0, tiled=True
    )


def exchange(tiles, axis):
    return lax.all_to_all(tiles, axis, 0, 0, tiled=True)


def total(tiles):
    return jnp.sum(tiles.astype(jnp.float32), axis=0)


def contract_rows(left, right):
    return lax.dot_general(
        left, right, (((0,), (0,)), ((), ())), preferred_element_type=jnp.float32
    )


def contract_cols(left, right):
    return lax.dot_general(
        left, right, (((1,), (1,)), ((), ())), preferred_element_type=jnp.float32
    )


def matmul(left, right):
    return jnp.dot(left, right, preferred_element_type=jnp.float32)


def finish(part):
    halves, ys, rows, width = part.shape
    by_y = exchange(jnp.swapaxes(part, 0, 1), "y")
    mine = total(by_y).astype(jnp.bfloat16)
    mine = jnp.where(lax.axis_index("zh") == 0, mine, mine[::-1])
    zl = lax.axis_size("zl")
    pieces = exchange(mine.reshape(halves * zl, rows // zl, width), Z)
    return give_all(total(pieces).astype(jnp.bfloat16), "zl").reshape(rows, width)


def body(tokens, gate_weight, up_weight, down_weight, out_grad):
    rows, width = tokens.shape
    hid = down_weight.shape[0]
    zl = lax.axis_size("zl")
    nz = 2 * zl
    cut = rows // zl
    at = lax.axis_index("zl") * cut
    own_tokens = give_all(tokens, "y").reshape(-1, width)
    thin = jnp.concatenate(
        [lax.dynamic_slice_in_dim(a, at, cut, 0) for a in (tokens, out_grad)], axis=0
    )
    far = lax.ppermute(thin, Z, [(i, (i + zl) % nz) for i in range(nz)])
    far_tokens = give_all(far[:cut], "zl").reshape(rows, width)
    far_tokens = give_all(far_tokens, "y").reshape(-1, width)
    own_grad = give_all(out_grad, "y").reshape(-1, width)
    far_grad = give_all(far[cut:], "zl").reshape(rows, width)
    far_grad = give_all(far_grad, "y").reshape(-1, width)

    def up_terms(some):
        return jnp.concatenate(
            [matmul(some, w).astype(jnp.bfloat16) for w in (gate_weight, up_weight)], axis=1
        )

    def spread(own, other):
        both = jnp.concatenate([own, other], axis=0)
        return both.reshape(8, -1, both.shape[1])

    pre = total(exchange(spread(up_terms(own_tokens), up_terms(far_tokens)), GZ))
    gate, upward = pre[:, :hid], pre[:, hid:]
    sigmoid = jax.nn.sigmoid(gate)
    hidden = (gate * sigmoid * upward).astype(jnp.bfloat16)
    hidden_all = give_all(hidden, GZ).reshape(-1, hid)
    output = finish(
        matmul(hidden_all, down_weight).astype(jnp.bfloat16).reshape(2, -1, rows, width)
    )
    dhidden = total(
        exchange(
            spread(
                contract_cols(own_grad, down_weight).astype(jnp.bfloat16),
                contract_cols(far_grad, down_weight).astype(jnp.bfloat16),
            ),
            GZ,
        )
    )
    dgate = (dhidden * upward * sigmoid * (1.0 + gate * (1.0 - sigmoid))).astype(jnp.bfloat16)
    dup = (dhidden * gate * sigmoid).astype(jnp.bfloat16)
    both = give_all(jnp.concatenate([dgate, dup], axis=1), GZ).reshape(-1, 2 * hid)
    dgate_all, dup_all = both[:, :hid], both[:, hid:]
    input_part = contract_cols(dgate_all, gate_weight) + contract_cols(dup_all, up_weight)
    input_grad = finish(input_part.astype(jnp.bfloat16).reshape(2, -1, rows, width))
    all_tokens = jnp.concatenate([own_tokens, far_tokens], axis=0)
    all_grad = jnp.concatenate([own_grad, far_grad], axis=0)
    gate_grad = contract_rows(all_tokens, dgate_all).astype(jnp.bfloat16)
    up_grad = contract_rows(all_tokens, dup_all).astype(jnp.bfloat16)
    down_grad = contract_rows(hidden_all, all_grad).astype(jnp.bfloat16)
    return (output, input_grad, gate_grad, up_grad, down_grad)


def solution(mesh):
    finer = Mesh(
        mesh.devices.reshape(4, 2, mesh.shape["gy"], 4, 2), ("y", "zh", "zl", "x", "c")
    )
    gx, ff = ("y", "zh"), ("y", "zh", "zl")
    in_specs = (P(gx, GZ), P(GZ, ff), P(GZ, ff), P(ff, GZ), P(gx, GZ))
    out_specs = (P(gx, GZ), P(gx, GZ), P(GZ, ff), P(GZ, ff), P(ff, GZ))
    return jax.shard_map(body, mesh=finer, in_specs=in_specs, out_specs=out_specs, check_vma=False)
```

time: 694 us -> 376 us (0.54)
  waiting for transfers between devices: 555 us -> 177 us
  starting transfers between devices: 29.1 us -> 87.2 us
  between operations: 13.9 us -> 0.98 us
  local copies, waits for them, and re-layouts: 7.4 us -> 15.8 us
    all_gather x3 -> x0, waiting for transfers between devices: 263 us -> none  [the longest x1 123 us: body(): all_tokens = lax.all_gather(tokens, GX, axis=0, tiled=True)]
    reduce_scatter x1 -> x0, waiting for transfers between devices: 184 us -> none  [body(): lax.psum_scatter((contract_cols(dgate_all, gate_weight) + contract_cols(d...]
    all_to_all x3 -> x13, waiting for transfers between devices: 86.6 us -> 174 us  [the longest x6 112 us: exchange(): return lax.all_to_all(tiles, axis, 0, 0, tiled=True)]
    all_to_all x3 -> x13, starting transfers between devices: 28.9 us -> 71.5 us  [the longest x6 37.8 us: exchange(): return lax.all_to_all(tiles, axis, 0, 0, tiled=True)]
    all_to_all x2 -> x3, blocking collectives: 27.6 us -> 66.2 us  [give_all(): lax.all_to_all(jnp.broadcast_to(shard[None], (devices, *shard.shape)), ax...]
    all_gather x2 -> x0, blocking collectives: 38.1 us -> none  [the longest x1 23.9 us: gathered_by_axis(): nearer = lax.all_gather(shard, axes[-1], axis=dim, tiled=True)]
    unnamed x6 -> x0, waiting for transfers between devices: 20.7 us -> none
    ppermute x0 -> x1, starting transfers between devices: none -> 15.7 us  [body(): far = lax.ppermute(thin, Z, [(i, (i + zl) % nz) for i in range(nz)])]
  transfers between devices with their start and end apart: 8 -> 14, of which waited for: 6 -> 13; matrix products, arithmetic and copies ran while one was open for 3% -> 8% of each run, Pallas kernels for 0% -> 0%
where the time goes in v1:
time: 376 us; the launch traced here: 373 us
  waiting for transfers between devices  177 us (47%)
  starting transfers between devices  87.2 us (23%)
  blocking collectives  66.2 us (18%)
  matrix products  17.2 us (5%)
  local copies, waits for them, and re-layouts  15.8 us (4%)
  other arithmetic  8.92 us (2%)
    all_to_all x6, waiting for transfers between devices, exchange(): return lax.all_to_all(tiles, axis, 0, 0, tiled=True)  112 us
    all_to_all x3, blocking collectives, give_all(): lax.all_to_all(jnp.broadcast_to(shard[None], (devices, *shard.shape)), ax...  66.2 us
    all_to_all x7, waiting for transfers between devices, give_all(): lax.all_to_all(jnp.broadcast_to(shard[None], (devices, *shard.shape)), ax...  61.5 us
    all_to_all x6, starting transfers between devices, exchange(): return lax.all_to_all(tiles, axis, 0, 0, tiled=True)  37.8 us
    all_to_all x7, starting transfers between devices, give_all(): lax.all_to_all(jnp.broadcast_to(shard[None], (devices, *shard.shape)), ax...  33.7 us
    ppermute x1, starting transfers between devices, body(): far = lax.ppermute(thin, Z, [(i, (i + zl) % nz) for i in range(nz)])  15.7 us
    dot_general x3, matrix products, contract_rows(): lax.dot_general(left, right, (((0,), (0,)), ((), ())), preferred_element_...  8.32 us
    broadcast_in_dim x10, local copies, waits for them, and re-layouts, give_all(): jnp.broadcast_to(shard[None], (devices, *shard.shape))  8.01 us
  transfers between devices with their start and end apart: 14, of which 13 were waited for; matrix products, arithmetic and copies ran while one was open for 8% of the time, Pallas kernels for 0%

profile of v1, /device:TPU:2, one launch (start us, length us, event | category | flops | bytes accessed | tf_op | source)
XLA Modules:
  0.0 373.2 jit_solution(12802697515472837060)
XLA Ops:
  0.7 1.1 broadcast_in_dim.24
  1.8 19.4 %all_to_all.80 = bf16[4,128,1024]{2,1,0:T(8,128)(2,1)S(1)} all-to-all(bf16[4,128,1024]{2,1,0:T(8,128)(2,1)S(1)} %broadcast_in_dim.24), channel_id=1, replica_groups=mesh['y'=4,'zh'=2,'zl'=8,'x'=4,'c'=2] {'y'}, dimensions={0} | all-to-all | bytes 2097152 | tf_op jit(solution)/shard_map/all_to_all | solution.py:13
  21.2 1.2 broadcast_in_dim.30
  22.4 3.5 all-to-all-start.8
  25.9 0.8 constant_dynamic-slice_fusion.1
  26.7 15.7 %collective-permute-start = (bf16[32,1024]{1,0:T(8,128)(2,1)S(1)}, bf16[32,1024]{1,0:T(8,128)(2,1)S(1)}, u32[]{:S(2)}, u32[]{:S(2)}) collective-permute-start(bf16[32,1024]{1,0:T(8,128)(2,1)S(1)} %pad_maximum_fusion.8), channel_id=1, source_target_pairs={{0,64},{8,72},{16,80},{24,88},{32,96},{40,104},{48,112},{56,120},{... | collective-permute-start | bytes 196616 | tf_op jit(solution)/shard_map/ppermute | solution.py:63
  42.4 3.2 collective-permute-done
  45.6 25.5 %all_to_all.81 = bf16[8,16,1024]{2,1,0:T(8,128)(2,1)S(1)} all-to-all(bf16[8,16,1024]{2,1,0:T(8,128)(2,1)S(1)} %broadcast_in_dim.31), channel_id=1, replica_groups=mesh['y'=4,'zh'=2,'zl'=8,'x'=4,'c'=2] {'zl'}, dimensions={0} | all-to-all | bytes 524288 | tf_op jit(solution)/shard_map/all_to_all | solution.py:13
  71.2 21.3 %all_to_all.82 = bf16[8,16,1024]{2,1,0:T(8,128)(2,1)S(1)} all-to-all(bf16[8,16,1024]{2,1,0:T(8,128)(2,1)S(1)} %broadcast_in_dim.25), channel_id=1, replica_groups=mesh['y'=4,'zh'=2,'zl'=8,'x'=4,'c'=2] {'zl'}, dimensions={0} | all-to-all | bytes 524288 | tf_op jit(solution)/shard_map/all_to_all | solution.py:13
  92.5 1.1 broadcast_in_dim.27
  93.6 4.2 %all-to-all-start.2 = ((bf16[4,128,1024]{2,1,0:T(8,128)(2,1)}), bf16[4,128,1024]{2,1,0:T(8,128)(2,1)}, u32[]{:S(2)}, u32[]{:S(2)}) async-start(bf16[4,128,1024]{2,1,0:T(8,128)(2,1)} %broadcast_in_dim.27), calls=%async_computation.2 | async-start | bytes 2097152 | tf_op jit(solution)/shard_map/all_to_all | solution.py:13
  97.9 0.5 convolution_convert_fusion.5
  98.4 10.4 %all-to-all-done.2 = bf16[4,128,1024]{2,1,0:T(8,128)(2,1)} async-done(((bf16[4,128,1024]{2,1,0:T(8,128)(2,1)}), bf16[4,128,1024]{2,1,0:T(8,128)(2,1)}, u32[]{:S(2)}, u32[]{:S(2)}) %all-to-all-start.2) | async-done | bytes 1048608 | tf_op jit(solution)/shard_map/all_to_all | solution.py:13
  108.8 1.1 broadcast_in_dim.33
  109.9 4.2 %all-to-all-start.10 = ((bf16[4,128,1024]{2,1,0:T(8,128)(2,1)}), bf16[4,128,1024]{2,1,0:T(8,128)(2,1)}, u32[]{:S(2)}, u32[]{:S(2)}) async-start(bf16[4,128,1024]{2,1,0:T(8,128)(2,1)} %broadcast_in_dim.33), calls=%async_computation.10 | async-start | bytes 2097152 | tf_op jit(solution)/shard_map/all_to_all | solution.py:13
  114.2 0.5 convolution_convert_fusion.6
  114.7 0.5 convolution_convert_fusion.2
  115.2 1.7 convolution_convert_fusion.3
  117.0 8.1 %all-to-all-done.10 = bf16[4,128,1024]{2,1,0:T(8,128)(2,1)} async-done(((bf16[4,128,1024]{2,1,0:T(8,128)(2,1)}), bf16[4,128,1024]{2,1,0:T(8,128)(2,1)}, u32[]{:S(2)}, u32[]{:S(2)}) %all-to-all-start.10) | async-done | bytes 1048608 | tf_op jit(solution)/shard_map/all_to_all | solution.py:13
  125.1 1.7 convolution_convert_fusion.1
  126.8 0.8 copy_bitcast_fusion.4
  127.7 4.8 %all-to-all-start.11 = ((bf16[8,128,224]{1,2,0:T(8,128)(2,1)}), bf16[8,128,224]{1,2,0:T(8,128)(2,1)S(1)}, u32[]{:S(2)}, u32[]{:S(2)}) async-start(bf16[8,128,224]{1,2,0:T(8,128)(2,1)} %copy_bitcast_fusion.4), calls=%async_computation.11 | async-start | bytes 917504 | tf_op jit(solution)/shard_map/all_to_all | solution.py:19
  132.5 1.7 convolution_convert_fusion.4
  134.2 1.1 copy_bitcast_fusion.3
  135.3 5.3 %all-to-all-done.11 = bf16[8,128,224]{1,2,0:T(8,128)(2,1)S(1)} async-done(((bf16[8,128,224]{1,2,0:T(8,128)(2,1)}), bf16[8,128,224]{1,2,0:T(8,128)(2,1)S(1)}, u32[]{:S(2)}, u32[]{:S(2)}) %all-to-all-start.11) | async-done | bytes 458784 | tf_op jit(solution)/shard_map/all_to_all | solution.py:19
  140.7 4.9 %all-to-all-start.3 = ((bf16[8,128,448]{1,2,0:T(8,128)(2,1)}), bf16[8,128,448]{1,2,0:T(8,128)(2,1)S(1)}, u32[]{:S(2)}, u32[]{:S(2)}) async-start(bf16[8,128,448]{1,2,0:T(8,128)(2,1)} %copy_bitcast_fusion.3), calls=%async_computation.3 | async-start | bytes 1835008 | tf_op jit(solution)/shard_map/all_to_all | solution.py:19
  145.7 13.0 %all-to-all-done.3 = bf16[8,128,448]{1,2,0:T(8,128)(2,1)S(1)} async-done(((bf16[8,128,448]{1,2,0:T(8,128)(2,1)}), bf16[8,128,448]{1,2,0:T(8,128)(2,1)S(1)}, u32[]{:S(2)}, u32[]{:S(2)}) %all-to-all-start.3) | async-done | bytes 917536 | tf_op jit(solution)/shard_map/all_to_all | solution.py:19
  158.9 0.8 broadcast_in_dim.28
  159.7 4.8 %all-to-all-start.4 = ((bf16[8,128,224]{1,2,0:T(8,128)(2,1)}), bf16[8,128,224]{1,2,0:T(8,128)(2,1)S(1)}, u32[]{:S(2)}, u32[]{:S(2)}) async-start(bf16[8,128,224]{1,2,0:T(8,128)(2,1)} %broadcast_in_dim.28), calls=%async_computation.4 | async-start | bytes 917504 | tf_op jit(solution)/shard_map/all_to_all | solution.py:13
  164.6 8.2 %all-to-all-done.4 = bf16[8,128,224]{1,2,0:T(8,128)(2,1)S(1)} async-done(((bf16[8,128,224]{1,2,0:T(8,128)(2,1)}), bf16[8,128,224]{1,2,0:T(8,128)(2,1)S(1)}, u32[]{:S(2)}, u32[]{:S(2)}) %all-to-all-start.4) | async-done | bytes 458784 | tf_op jit(solution)/shard_map/all_to_all | solution.py:13
  172.8 1.1 broadcast_in_dim.34
  173.8 4.9 %all-to-all-start.12 = ((bf16[8,128,448]{1,2,0:T(8,128)(2,1)}), bf16[8,128,448]{1,2,0:T(8,128)(2,1)S(1)}, u32[]{:S(2)}, u32[]{:S(2)}) async-start(bf16[8,128,448]{1,2,0:T(8,128)(2,1)} %broadcast_in_dim.34), calls=%async_computation.12 | async-start | bytes 1835008 | tf_op jit(solution)/shard_map/all_to_all | solution.py:13
  178.8 0.7 convolution_convert_fusion
  179.5 1.5 copy.54
  181.0 10.9 %all-to-all-done.12 = bf16[8,128,448]{1,2,0:T(8,128)(2,1)S(1)} async-done(((bf16[8,128,448]{1,2,0:T(8,128)(2,1)}), bf16[8,128,448]{1,2,0:T(8,128)(2,1)S(1)}, u32[]{:S(2)}, u32[]{:S(2)}) %all-to-all-start.12) | async-done | bytes 917536 | tf_op jit(solution)/shard_map/all_to_all | solution.py:13
  191.9 0.9 copy-done.1
  192.8 3.6 all-to-all-start.5
  196.4 1.4 copy_bitcast_fusion.2
  197.8 0.8 fusion.18
  198.6 0.3 copy-done.11
  198.8 0.8 add_convert_fusion
  199.6 1.5 copy.53
  201.1 21.6 %all-to-all-done.5 = bf16[4,2,128,1024]{3,2,1,0:T(8,128)(2,1)S(1)} async-done(((bf16[4,2,128,1024]{3,2,1,0:T(8,128)(2,1)}), bf16[4,2,128,1024]{3,2,1,0:T(8,128)(2,1)S(1)}, u32[]{:S(2)}, u32[]{:S(2)}) %all-to-all-start.5) | async-done | bytes 2097184 | tf_op jit(solution)/shard_map/all_to_all | solution.py:19
  222.7 4.5 %all-to-all-start.13 = ((bf16[4,2,128,1024]{3,2,1,0:T(8,128)(2,1)}), bf16[4,2,128,1024]{3,2,1,0:T(8,128)(2,1)}, u32[]{:S(2)}, u32[]{:S(2)}) async-start(bf16[4,2,128,1024]{3,2,1,0:T(8,128)(2,1)} %bitcast.61), calls=%async_computation.13 | async-start | bytes 4194304 | tf_op jit(solution)/shard_map/all_to_all | solution.py:19
  227.2 1.3 reduce_sum.67
  228.5 2.3 reverse_select_fusion.1
  230.7 21.9 %all-to-all-done.13 = bf16[4,2,128,1024]{3,2,1,0:T(8,128)(2,1)} async-done(((bf16[4,2,128,1024]{3,2,1,0:T(8,128)(2,1)}), bf16[4,2,128,1024]{3,2,1,0:T(8,128)(2,1)}, u32[]{:S(2)}, u32[]{:S(2)}) %all-to-all-start.13) | async-done | bytes 2097184 | tf_op jit(solution)/shard_map/all_to_all | solution.py:19
  252.7 12.6 %all-to-all-start.6 = ((bf16[16,16,1024]{2,1,0:T(8,128)(2,1)}), bf16[16,16,1024]{2,1,0:T(8,128)(2,1)S(1)}, u32[]{:S(2)}, u32[]{:S(2)}) async-start(bf16[16,16,1024]{2,1,0:T(8,128)(2,1)} %bitcast.5), calls=%async_computation.6 | async-start | bytes 1048576 | tf_op jit(solution)/shard_map/all_to_all | solution.py:19
  265.2 2.0 reduce_sum.70
  267.3 0.9 reverse_select_fusion
  268.2 23.0 %all-to-all-done.6 = bf16[16,16,1024]{2,1,0:T(8,128)(2,1)S(1)} async-done(((bf16[16,16,1024]{2,1,0:T(8,128)(2,1)}), bf16[16,16,1024]{2,1,0:T(8,128)(2,1)S(1)}, u32[]{:S(2)}, u32[]{:S(2)}) %all-to-all-start.6) | async-done | bytes 524320 | tf_op jit(solution)/shard_map/all_to_all | solution.py:19
  291.2 7.4 %all-to-all-start.14 = ((bf16[16,16,1024]{2,1,0:T(8,128)(2,1)}), bf16[16,16,1024]{2,1,0:T(8,128)(2,1)S(1)}, u32[]{:S(2)}, u32[]{:S(2)}) async-start(bf16[16,16,1024]{2,1,0:T(8,128)(2,1)} %bitcast.12), calls=%async_computation.14 | async-start | bytes 1048576 | tf_op jit(solution)/shard_map/all_to_all | solution.py:19
  298.7 27.3 %all-to-all-done.14 = bf16[16,16,1024]{2,1,0:T(8,128)(2,1)S(1)} async-done(((bf16[16,16,1024]{2,1,0:T(8,128)(2,1)}), bf16[16,16,1024]{2,1,0:T(8,128)(2,1)S(1)}, u32[]{:S(2)}, u32[]{:S(2)}) %all-to-all-start.14) | async-done | bytes 524320 | tf_op jit(solution)/shard_map/all_to_all | solution.py:19
  326.0 0.7 broadcast_in_dim.29
  326.8 6.9 %all-to-all-start.7 = ((bf16[8,16,1024]{2,1,0:T(8,128)(2,1)}), bf16[8,16,1024]{2,1,0:T(8,128)(2,1)S(1)}, u32[]{:S(2)}, u32[]{:S(2)}) async-start(bf16[8,16,1024]{2,1,0:T(8,128)(2,1)} %broadcast_in_dim.29), calls=%async_computation.7 | async-start | bytes 524288 | tf_op jit(solution)/shard_map/all_to_all | solution.py:13
  333.8 15.9 %all-to-all-done.7 = bf16[8,16,1024]{2,1,0:T(8,128)(2,1)S(1)} async-done(((bf16[8,16,1024]{2,1,0:T(8,128)(2,1)}), bf16[8,16,1024]{2,1,0:T(8,128)(2,1)S(1)}, u32[]{:S(2)}, u32[]{:S(2)}) %all-to-all-start.7) | async-done | bytes 262176 | tf_op jit(solution)/shard_map/all_to_all | solution.py:13
  349.7 0.7 broadcast_in_dim.35
  350.4 5.1 %all-to-all-start.15 = ((bf16[8,16,1024]{2,1,0:T(8,128)(2,1)}), bf16[8,16,1024]{2,1,0:T(8,128)(2,1)S(1)}, u32[]{:S(2)}, u32[]{:S(2)}) async-start(bf16[8,16,1024]{2,1,0:T(8,128)(2,1)} %broadcast_in_dim.35), calls=%async_computation.15 | async-start | bytes 524288 | tf_op jit(solution)/shard_map/all_to_all | solution.py:13
  355.5 3.0 fusion.8
  358.6 2.6 fusion.7
  361.2 2.6 fusion.6
  363.8 8.0 %all-to-all-done.15 = bf16[8,16,1024]{2,1,0:T(8,128)(2,1)S(1)} async-done(((bf16[8,16,1024]{2,1,0:T(8,128)(2,1)}), bf16[8,16,1024]{2,1,0:T(8,128)(2,1)S(1)}, u32[]{:S(2)}, u32[]{:S(2)}) %all-to-all-start.15) | async-done | bytes 262176 | tf_op jit(solution)/shard_map/all_to_all | solution.py:13
  371.8 0.7 copy.57
  372.5 0.7 copy.58
  (36 shorter events, 0.6 us)
Async XLA Ops:
  0.6 114.1 %copy-start = (bf16[224,1024]{1,0:T(8,128)(2,1)S(1)}, bf16[224,1024]{1,0:T(8,128)(2,1)}, u32[]{:S(2)}) copy-start(bf16[224,1024]{1,0:T(8,128)(2,1)} %param.8) | copy-start | bytes 1376260
  0.6 20.5 %copy-start.12 = (bf16[128,1024]{1,0:T(8,128)(2,1)S(1)}, bf16[128,1024]{1,0:T(8,128)(2,1)}, u32[]{:S(2)}) copy-start(bf16[128,1024]{1,0:T(8,128)(2,1)} %param.9) | copy-start | bytes 786436
  21.2 93.0 %copy-start.4 = (bf16[4,128,1024]{2,1,0:T(8,128)(2,1)}, bf16[4,128,1024]{2,1,0:T(8,128)(2,1)S(1)}, u32[]{:S(2)}) copy-start(bf16[4,128,1024]{2,1,0:T(8,128)(2,1)S(1)} %all_to_all.80) | copy-start | bytes 3145732
  22.4 23.2 %all-to-all-start.8 = ((bf16[4,128,1024]{2,1,0:T(8,128)(2,1)}), bf16[4,128,1024]{2,1,0:T(8,128)(2,1)S(1)}, u32[]{:S(2)}, u32[]{:S(2)}) async-start(bf16[4,128,1024]{2,1,0:T(8,128)(2,1)} %broadcast_in_dim.30), calls=%async_computation.8 | async-start | bytes 2097152 | tf_op jit(solution)/shard_map/all_to_all | solution.py:13
  26.7 18.9 %collective-permute-start = (bf16[32,1024]{1,0:T(8,128)(2,1)S(1)}, bf16[32,1024]{1,0:T(8,128)(2,1)S(1)}, u32[]{:S(2)}, u32[]{:S(2)}) collective-permute-start(bf16[32,1024]{1,0:T(8,128)(2,1)S(1)} %pad_maximum_fusion.8), channel_id=1, source_target_pairs={{0,64},{8,72},{16,80},{24,88},{32,96},{40,104},{48,112},{56,120},{... | collective-permute-start | bytes 196616 | tf_op jit(solution)/shard_map/ppermute | solution.py:63
  45.6 69.1 %copy-start.6 = (bf16[4,128,1024]{2,1,0:T(8,128)(2,1)}, bf16[4,128,1024]{2,1,0:T(8,128)(2,1)S(1)}, u32[]{:S(2)}) copy-start(bf16[4,128,1024]{2,1,0:T(8,128)(2,1)S(1)} %all-to-all-done.8) | copy-start | bytes 3145732
  71.1 26.7 %copy-start.9 = (bf16[1024,224]{0,1:T(8,128)(2,1)S(1)}, bf16[1024,224]{0,1:T(8,128)(2,1)}, u32[]{:S(2)}) copy-start(bf16[1024,224]{0,1:T(8,128)(2,1)} %param.7) | copy-start | bytes 1376260
  93.6 15.2 %all-to-all-start.2 = ((bf16[4,128,1024]{2,1,0:T(8,128)(2,1)}), bf16[4,128,1024]{2,1,0:T(8,128)(2,1)}, u32[]{:S(2)}, u32[]{:S(2)}) async-start(bf16[4,128,1024]{2,1,0:T(8,128)(2,1)} %broadcast_in_dim.27), calls=%async_computation.2 | async-start | bytes 2097152 | tf_op jit(solution)/shard_map/all_to_all | solution.py:13
  98.4 15.8 %copy-start.7 = (bf16[1024,224]{0,1:T(8,128)(2,1)S(1)}, bf16[1024,224]{0,1:T(8,128)(2,1)}, u32[]{:S(2)}) copy-start(bf16[1024,224]{0,1:T(8,128)(2,1)} %param.6) | copy-start | bytes 1376260
  109.9 15.2 %all-to-all-start.10 = ((bf16[4,128,1024]{2,1,0:T(8,128)(2,1)}), bf16[4,128,1024]{2,1,0:T(8,128)(2,1)}, u32[]{:S(2)}, u32[]{:S(2)}) async-start(bf16[4,128,1024]{2,1,0:T(8,128)(2,1)} %broadcast_in_dim.33), calls=%async_computation.10 | async-start | bytes 2097152 | tf_op jit(solution)/shard_map/all_to_all | solution.py:13
  114.2 1.0 copy-start.10
  127.7 13.0 %all-to-all-start.11 = ((bf16[8,128,224]{1,2,0:T(8,128)(2,1)}), bf16[8,128,224]{1,2,0:T(8,128)(2,1)S(1)}, u32[]{:S(2)}, u32[]{:S(2)}) async-start(bf16[8,128,224]{1,2,0:T(8,128)(2,1)} %copy_bitcast_fusion.4), calls=%async_computation.11 | async-start | bytes 917504 | tf_op jit(solution)/shard_map/all_to_all | solution.py:19
  140.7 18.0 %all-to-all-start.3 = ((bf16[8,128,448]{1,2,0:T(8,128)(2,1)}), bf16[8,128,448]{1,2,0:T(8,128)(2,1)S(1)}, u32[]{:S(2)}, u32[]{:S(2)}) async-start(bf16[8,128,448]{1,2,0:T(8,128)(2,1)} %copy_bitcast_fusion.3), calls=%async_computation.3 | async-start | bytes 1835008 | tf_op jit(solution)/shard_map/all_to_all | solution.py:19
  159.7 13.0 %all-to-all-start.4 = ((bf16[8,128,224]{1,2,0:T(8,128)(2,1)}), bf16[8,128,224]{1,2,0:T(8,128)(2,1)S(1)}, u32[]{:S(2)}, u32[]{:S(2)}) async-start(bf16[8,128,224]{1,2,0:T(8,128)(2,1)} %broadcast_in_dim.28), calls=%async_computation.4 | async-start | bytes 917504 | tf_op jit(solution)/shard_map/all_to_all | solution.py:13
  172.8 6.7 %copy-start.2 = (bf16[8,128,224]{1,2,0:T(8,128)(2,1)}, bf16[8,128,224]{1,2,0:T(8,128)(2,1)S(1)}, u32[]{:S(2)}) copy-start(bf16[8,128,224]{1,2,0:T(8,128)(2,1)S(1)} %all-to-all-done.4) | copy-start | bytes 1376260
  173.8 18.0 %all-to-all-start.12 = ((bf16[8,128,448]{1,2,0:T(8,128)(2,1)}), bf16[8,128,448]{1,2,0:T(8,128)(2,1)S(1)}, u32[]{:S(2)}, u32[]{:S(2)}) async-start(bf16[8,128,448]{1,2,0:T(8,128)(2,1)} %broadcast_in_dim.34), calls=%async_computation.12 | async-start | bytes 1835008 | tf_op jit(solution)/shard_map/all_to_all | solution.py:13
  191.9 0.9 copy-start.1
  192.8 29.9 %all-to-all-start.5 = ((bf16[4,2,128,1024]{3,2,1,0:T(8,128)(2,1)}), bf16[4,2,128,1024]{3,2,1,0:T(8,128)(2,1)S(1)}, u32[]{:S(2)}, u32[]{:S(2)}) async-start(bf16[4,2,128,1024]{3,2,1,0:T(8,128)(2,1)} %bitcast.62), calls=%async_computation.5 | async-start | bytes 4194304 | tf_op jit(solution)/shard_map/all_to_all | solution.py:19
  196.4 1.4 copy-start.8
  197.8 1.0 copy-start.11
  222.7 30.0 %all-to-all-start.13 = ((bf16[4,2,128,1024]{3,2,1,0:T(8,128)(2,1)}), bf16[4,2,128,1024]{3,2,1,0:T(8,128)(2,1)}, u32[]{:S(2)}, u32[]{:S(2)}) async-start(bf16[4,2,128,1024]{3,2,1,0:T(8,128)(2,1)} %bitcast.61), calls=%async_computation.13 | async-start | bytes 4194304 | tf_op jit(solution)/shard_map/all_to_all | solution.py:19
  252.7 38.5 %all-to-all-start.6 = ((bf16[16,16,1024]{2,1,0:T(8,128)(2,1)}), bf16[16,16,1024]{2,1,0:T(8,128)(2,1)S(1)}, u32[]{:S(2)}, u32[]{:S(2)}) async-start(bf16[16,16,1024]{2,1,0:T(8,128)(2,1)} %bitcast.5), calls=%async_computation.6 | async-start | bytes 1048576 | tf_op jit(solution)/shard_map/all_to_all | solution.py:19
  268.2 87.3 %copy-start.3 = (bf16[8,128,224]{1,2,0:T(8,128)(2,1)S(1)}, bf16[8,128,224]{1,2,0:T(8,128)(2,1)}, u32[]{:S(2)}) copy-start(bf16[8,128,224]{1,2,0:T(8,128)(2,1)} %copy-done.2) | copy-start | bytes 1376260
  291.2 34.8 %all-to-all-start.14 = ((bf16[16,16,1024]{2,1,0:T(8,128)(2,1)}), bf16[16,16,1024]{2,1,0:T(8,128)(2,1)S(1)}, u32[]{:S(2)}, u32[]{:S(2)}) async-start(bf16[16,16,1024]{2,1,0:T(8,128)(2,1)} %bitcast.12), calls=%async_computation.14 | async-start | bytes 1048576 | tf_op jit(solution)/shard_map/all_to_all | solution.py:19
  326.8 22.9 %all-to-all-start.7 = ((bf16[8,16,1024]{2,1,0:T(8,128)(2,1)}), bf16[8,16,1024]{2,1,0:T(8,128)(2,1)S(1)}, u32[]{:S(2)}, u32[]{:S(2)}) async-start(bf16[8,16,1024]{2,1,0:T(8,128)(2,1)} %broadcast_in_dim.29), calls=%async_computation.7 | async-start | bytes 524288 | tf_op jit(solution)/shard_map/all_to_all | solution.py:13
  350.4 21.4 %all-to-all-start.15 = ((bf16[8,16,1024]{2,1,0:T(8,128)(2,1)}), bf16[8,16,1024]{2,1,0:T(8,128)(2,1)S(1)}, u32[]{:S(2)}, u32[]{:S(2)}) async-start(bf16[8,16,1024]{2,1,0:T(8,128)(2,1)} %broadcast_in_dim.35), calls=%async_computation.15 | async-start | bytes 524288 | tf_op jit(solution)/shard_map/all_to_all | solution.py:13
  355.5 3.1 copy-start.5

commit v2 on v1

v2 whole, which is shorter than its diff:
```python
import jax
import jax.numpy as jnp
from jax import lax
from jax.experimental import pallas as pl
from jax.experimental.pallas import tpu as pltpu
from jax.sharding import Mesh
from jax.sharding import PartitionSpec as P

GZ = ("x", "c")
Z = ("zh", "zl")
HALVING = (0, 1, 2)
LANES = 256


def give_all(shard, axis):
    devices = lax.axis_size(axis)
    return lax.all_to_all(
        jnp.broadcast_to(shard[None], (devices, *shard.shape)), axis, 0, 0, tiled=True
    )


def exchange(tiles, axis):
    return lax.all_to_all(tiles, axis, 0, 0, tiled=True)


def total(tiles):
    return jnp.sum(tiles.astype(jnp.float32), axis=0)


def to_y(block, d):
    n = lax.axis_size("y")
    return lax.ppermute(block, "y", [(i, (i + d) % n) for i in range(n)])


def of_ys(shard):
    blocks = [shard]
    for d in (1, 2, 3):
        blocks.append(to_y(shard, -d))
    return blocks


def across(shard):
    zl = lax.axis_size("zl")
    nz, step = 2 * zl, zl // 2
    return lax.ppermute(
        shard, Z, [(i, (i - step if i % zl < step else i + step) % nz) for i in range(nz)]
    )


def to_bit(block, bit):
    return lax.ppermute(block, "zl", [(i, i ^ (1 << bit)) for i in range(lax.axis_size("zl"))])


def halved(tiles, bit):
    pairs = tiles.reshape(-1, 2, *tiles.shape[1:])
    got = to_bit(pairs[:, 1], bit)
    return pairs[:, 0].astype(jnp.float32) + got.astype(jnp.float32)


def contract_rows(left, right):
    return lax.dot_general(
        left, right, (((0,), (0,)), ((), ())), preferred_element_type=jnp.float32
    )


def contract_cols(left, right):
    return lax.dot_general(
        left, right, (((1,), (1,)), ((), ())), preferred_element_type=jnp.float32
    )


def matmul(left, right):
    return jnp.dot(left, right, preferred_element_type=jnp.float32)


def own_kernel(zl, tokens, grad, out):
    for r in range(out.shape[0]):
        s = jnp.bitwise_xor(zl[0], r)
        out[r, 0] = tokens[s]
        out[r, 1] = grad[s]


def terms_kernel(b0, b1, b2, b3, wide, down, out):
    n, _, cut, width = b0.shape
    rows = n * cut
    for k, b in enumerate((b0, b1, b2, b3)):
        t = b[:, 0].reshape(rows, width)
        g = b[:, 1].reshape(rows, width)
        at = pl.ds(k * rows, rows)
        out[at, : 2 * LANES] = matmul(t, wide[...]).astype(jnp.bfloat16)
        out[at, 2 * LANES :] = contract_cols(g, down[...]).astype(jnp.bfloat16)


def leave_kernel(acts, wide, down, *outs):
    rows = acts.shape[0] // 4
    n, _, cut, width = outs[0].shape
    for d, out in enumerate(outs):
        at = pl.ds(d * rows, rows)
        o = matmul(acts[at, :LANES], down[...]).astype(jnp.bfloat16)
        out[:, 0] = o.reshape(n, cut, width)
        i = contract_cols(acts[at, LANES:], wide[...]).astype(jnp.bfloat16)
        out[:, 1] = i.reshape(n, cut, width)


def sum_kernel(a, b, c, d, out):
    f32 = jnp.float32
    out[...] = (
        a[...].astype(f32) + b[...].astype(f32) + c[...].astype(f32) + d[...].astype(f32)
    ).astype(jnp.bfloat16)


def work(tokens, gate_weight, up_weight, down_weight, out_grad):
    rows, width = tokens.shape
    hid = down_weight.shape[0]
    zl = lax.axis_size("zl")
    cut = rows // zl
    block = jax.ShapeDtypeStruct((zl, 2, cut, width), jnp.bfloat16)
    more = LANES - hid
    vmem = pl.BlockSpec(memory_space=pltpu.VMEM)
    own = pl.pallas_call(
        own_kernel,
        out_shape=block,
        in_specs=[pl.BlockSpec(memory_space=pltpu.SMEM), vmem, vmem],
        name="own",
    )(
        lax.axis_index("zl").astype(jnp.int32).reshape(1),
        *(a.reshape(zl, cut, width) for a in (tokens, out_grad)),
    )
    wide = jnp.concatenate(
        [jnp.pad(w, ((0, 0), (0, more))) for w in (gate_weight, up_weight)], axis=1
    )
    down = jnp.pad(down_weight, ((0, more), (0, 0)))
    far = across(own[:1])
    own = of_ys(own)
    for bit in HALVING[::-1]:
        got = to_bit(far, bit)
        far = jnp.stack([far, got], axis=1).reshape(-1, *far.shape[1:])
    far = of_ys(far)

    def terms(blocks):
        made = pl.pallas_call(
            terms_kernel,
            out_shape=jax.ShapeDtypeStruct((4 * rows, 3 * LANES), jnp.bfloat16),
            name="terms",
        )(*blocks, wide, down)
        made = exchange(made.reshape(8, rows // 2, -1), GZ)
        return total(made)

    def gates(pre):
        gate, upward, dhidden = (pre[:, k * LANES : (k + 1) * LANES] for k in range(3))
        sigmoid = jax.nn.sigmoid(gate)
        hidden = (gate * sigmoid * upward).astype(jnp.bfloat16)
        dgate = (dhidden * upward * sigmoid * (1.0 + gate * (1.0 - sigmoid))).astype(jnp.bfloat16)
        dup = (dhidden * gate * sigmoid).astype(jnp.bfloat16)
        acts = jnp.concatenate([hidden, dgate, dup], axis=1)
        acts = give_all(acts, GZ)
        return acts.reshape(4 * rows, -1)

    def leave(acts):
        parts = pl.pallas_call(leave_kernel, out_shape=[block] * 4, name="leave")(acts, wide, down)
        back = [to_y(parts[d], d) for d in (1, 2, 3)]
        mine = pl.pallas_call(sum_kernel, out_shape=block, name="add")(parts[0], *back)
        return mine

    own_acts = gates(terms(own))
    far_acts = gates(terms(far))
    own_sum = leave(own_acts)
    far_sum = leave(far_acts)
    for bit in HALVING:
        own_sum = halved(own_sum.astype(jnp.bfloat16), bit)
        far_sum = halved(far_sum.astype(jnp.bfloat16), bit)
    own_sum, far_sum = own_sum[0], far_sum[0].astype(jnp.bfloat16)
    far_sum = across(far_sum)
    ends = (own_sum + far_sum.astype(jnp.float32)).astype(jnp.bfloat16)
    ends = give_all(ends, "zl")
    output, input_grad = (ends[:, k].reshape(rows, width) for k in range(2))

    all_tokens, all_grad = (
        jnp.concatenate([b[:, k].reshape(rows, width) for b in own + far], axis=0)
        for k in range(2)
    )
    acts = jnp.concatenate([own_acts, far_acts], axis=0)
    hidden, dgate, dup = (acts[:, k * LANES : k * LANES + hid] for k in range(3))
    gate_grad = contract_rows(all_tokens, dgate).astype(jnp.bfloat16)
    up_grad = contract_rows(all_tokens, dup).astype(jnp.bfloat16)
    down_grad = contract_rows(hidden, all_grad).astype(jnp.bfloat16)
    return (output, input_grad, gate_grad, up_grad, down_grad)


def solution(mesh):
    finer = Mesh(
        mesh.devices.reshape(4, 2, mesh.shape["gy"], 4, 2), ("y", "zh", "zl", "x", "c")
    )
    gx, ff = ("y", "zh"), ("y", "zh", "zl")
    in_specs = (P(gx, GZ), P(GZ, ff), P(GZ, ff), P(ff, GZ), P(gx, GZ))
    out_specs = (P(gx, GZ), P(gx, GZ), P(GZ, ff), P(GZ, ff), P(ff, GZ))
    return jax.shard_map(work, mesh=finer, in_specs=in_specs, out_specs=out_specs, check_vma=False)
```

time: 376 us -> 290 us (0.77)
  the two profiles are of different devices: /device:TPU:2 before, /device:TPU:26 now
where the time goes in v2:
time: 290 us; the launch traced here: 288 us
  starting transfers between devices  129 us (44%)
  waiting for transfers between devices  94.5 us (33%)
  local copies, waits for them, and re-layouts  30.3 us (10%)
  Pallas kernels  23.9 us (8%)
  matrix products  6.08 us (2%)
    ppermute x12, starting transfers between devices, to_y(): return lax.ppermute(block, 'y', [(i, (i + d) % n) for i in range(n)])  41.3 us
    ppermute x9, starting transfers between devices, to_bit(): lax.ppermute(block, 'zl', [(i, i ^ 1 << bit) for i in range(lax.axis_size...  36.4 us
    all_to_all x3, waiting for transfers between devices, give_all(): lax.all_to_all(jnp.broadcast_to(shard[None], (devices, *shard.shape)), ax...  27.9 us
    ppermute x12, waiting for transfers between devices, to_y(): return lax.ppermute(block, 'y', [(i, (i + d) % n) for i in range(n)])  26 us
    ppermute x9, waiting for transfers between devices, to_bit(): lax.ppermute(block, 'zl', [(i, i ^ 1 << bit) for i in range(lax.axis_size...  23.2 us
    all_to_all x3, starting transfers between devices, give_all(): lax.all_to_all(jnp.broadcast_to(shard[None], (devices, *shard.shape)), ax...  21.8 us
    ppermute x2, starting transfers between devices, across(): lax.ppermute(shard, Z, [(i, (i - step if i % zl < step else i + step) % n...  20.3 us
    unnamed x60, local copies, waits for them, and re-layouts  14.8 us
  transfers between devices with their start and end apart: 28, of which 17 were waited for; matrix products, arithmetic and copies ran while one was open for 11% of the time, Pallas kernels for 8%

profile of v2, /device:TPU:26, one launch (start us, length us, event | category | flops | bytes accessed | tf_op | source)
XLA Modules:
  0.0 288.3 jit_solution(15823621385922051853)
XLA Ops:
  0.7 2.0 own.1.b0
  3.5 12.7 %collective-permute-start.9 = (bf16[1,2,16,1024]{3,2,1,0:T(8,128)(2,1)S(1)}, bf16[1,2,16,1024]{3,2,1,0:T(8,128)(2,1)S(1)}, u32[]{:S(2)}, u32[]{:S(2)}) collective-permute-start(bf16[1,2,16,1024]{3,2,1,0:T(8,128)(2,1)S(1)} %slice.169), channel_id=1, source_target_pairs={{0,96},{8,104},{16,112},{24,120},{32,64},{40,72},{48,80},{56,88},{... | collective-permute-start | bytes 196616 | tf_op jit(solution)/shard_map/ppermute | solution.py:45
  16.2 5.6 %collective-permute-done.9 = bf16[1,2,16,1024]{3,2,1,0:T(8,128)(2,1)S(1)} collective-permute-done((bf16[1,2,16,1024]{3,2,1,0:T(8,128)(2,1)S(1)}, bf16[1,2,16,1024]{3,2,1,0:T(8,128)(2,1)S(1)}, u32[]{:S(2)}, u32[]{:S(2)}) %collective-permute-start.9) | collective-permute-done | bytes 65568 | tf_op jit(solution)/shard_map/ppermute | solution.py:45
  21.8 6.2 %collective-permute-start.10 = (bf16[1,2,16,1024]{3,2,1,0:T(8,128)(2,1)S(1)}, bf16[1,2,16,1024]{3,2,1,0:T(8,128)(2,1)S(1)}, u32[]{:S(2)}, u32[]{:S(2)}) collective-permute-start(bf16[1,2,16,1024]{3,2,1,0:T(8,128)(2,1)S(1)} %collective-permute-done.9), channel_id=1, source_target_pairs={{0,32},{8,40},{16,48},{24,56},{32,0},{40,8},{48,16},{56,24},{1,33}... | collective-permute-start | bytes 196616 | tf_op jit(solution)/shard_map/ppermute | solution.py:51
  27.9 6.3 %collective-permute-done.10 = bf16[1,2,16,1024]{3,2,1,0:T(8,128)(2,1)S(1)} collective-permute-done((bf16[1,2,16,1024]{3,2,1,0:T(8,128)(2,1)S(1)}, bf16[1,2,16,1024]{3,2,1,0:T(8,128)(2,1)S(1)}, u32[]{:S(2)}, u32[]{:S(2)}) %collective-permute-start.10) | collective-permute-done | bytes 65568 | tf_op jit(solution)/shard_map/ppermute | solution.py:51
  34.2 1.9 collective-permute-start.11
  36.2 2.7 collective-permute-start
  38.8 2.9 collective-permute-start.1
  41.7 4.1 %collective-permute-start.2 = (bf16[8,2,16,1024]{3,2,1,0:T(8,128)(2,1)}, bf16[8,2,16,1024]{3,2,1,0:T(8,128)(2,1)S(1)}, u32[]{:S(2)}, u32[]{:S(2)}) collective-permute-start(bf16[8,2,16,1024]{3,2,1,0:T(8,128)(2,1)} %own.1.b0), channel_id=1, source_target_pairs={{0,128},{128,256},{256,384},{384,0},{1,129},{129,257},{257,385},{3... | collective-permute-start | bytes 1572872 | tf_op jit(solution)/shard_map/ppermute | solution.py:32
  45.8 2.7 collective-permute-start.12
  49.9 1.2 fusion.2.wide
  51.1 3.1 %collective-permute-done.12 = bf16[4,2,16,1024]{3,2,1,0:T(8,128)(2,1)S(1)} collective-permute-done((bf16[4,2,16,1024]{3,2,1,0:T(8,128)(2,1)S(1)}, bf16[4,2,16,1024]{3,2,1,0:T(8,128)(2,1)S(1)}, u32[]{:S(2)}, u32[]{:S(2)}) %collective-permute-start.12) | collective-permute-done | bytes 262176 | tf_op jit(solution)/shard_map/ppermute | solution.py:51
  54.2 2.3 collective-permute-start.13
  56.5 4.1 %collective-permute-start.14 = (bf16[8,2,16,1024]{3,2,1,0:T(8,128)(2,1)S(1)}, bf16[8,2,16,1024]{3,2,1,0:T(8,128)(2,1)S(1)}, u32[]{:S(2)}, u32[]{:S(2)}) collective-permute-start(bf16[8,2,16,1024]{3,2,1,0:T(8,128)(2,1)S(1)} %bitcast.118), channel_id=1, source_target_pairs={{0,256},{128,384},{256,0},{384,128},{1,257},{129,385},{257,1},{385... | collective-permute-start | bytes 1572872 | tf_op jit(solution)/shard_map/ppermute | solution.py:32
  60.9 4.1 %collective-permute-start.15 = (bf16[8,2,16,1024]{3,2,1,0:T(8,128)(2,1)S(1)}, bf16[8,2,16,1024]{3,2,1,0:T(8,128)(2,1)S(1)}, u32[]{:S(2)}, u32[]{:S(2)}) collective-permute-start(bf16[8,2,16,1024]{3,2,1,0:T(8,128)(2,1)S(1)} %bitcast.119), channel_id=1, source_target_pairs={{0,128},{128,256},{256,384},{384,0},{1,129},{129,257},{257,385},{3... | collective-permute-start | bytes 1572872 | tf_op jit(solution)/shard_map/ppermute | solution.py:32
  65.1 3.2 %collective-permute-done.2.b3 = bf16[8,2,16,1024]{3,2,1,0:T(8,128)(2,1)S(1)} collective-permute-done((bf16[8,2,16,1024]{3,2,1,0:T(8,128)(2,1)}, bf16[8,2,16,1024]{3,2,1,0:T(8,128)(2,1)S(1)}, u32[]{:S(2)}, u32[]{:S(2)}) %collective-permute-start.2) | collective-permute-done | bytes 524320 | tf_op jit(solution)/shard_map/ppermute | solution.py:32
  69.1 4.2 %terms.2 = bf16[512,768]{1,0:T(8,128)(2,1)} custom-call(bf16[8,2,16,1024]{3,2,1,0:T(8,128)(2,1)} %own.1.b0, bf16[8,2,16,1024]{3,2,1,0:T(8,128)(2,1)} %collective-permute-done.b1, bf16[8,2,16,1024]{3,2,1,0:T(8,128)(2,1)} %collective-permute-done.1.b2, bf16[8,2,16,1024]{3,2,1,0:T(8,128)(2,1)} %copy-done.14, bf16[1024,512]{1,0:T(8,128)(2,1)} %fusion.2.wide, ...), custom_call_target="tpu_custom_call" | custom-call | tf_op jit(solution)/shard_map/terms/pallas_call | solution.py:141
  73.3 4.8 %all-to-all-start = ((bf16[8,64,768]{2,1,0:T(8,128)(2,1)}), bf16[8,64,768]{2,1,0:T(8,128)(2,1)S(1)}, u32[]{:S(2)}, u32[]{:S(2)}) async-start(bf16[8,64,768]{2,1,0:T(8,128)(2,1)} %bitcast.122), calls=%async_computation | async-start | bytes 1572864 | tf_op jit(solution)/shard_map/all_to_all | solution.py:23
  80.5 3.1 %collective-permute-done.13.b1 = bf16[8,2,16,1024]{3,2,1,0:T(8,128)(2,1)S(1)} collective-permute-done((bf16[8,2,16,1024]{3,2,1,0:T(8,128)(2,1)S(1)}, bf16[8,2,16,1024]{3,2,1,0:T(8,128)(2,1)S(1)}, u32[]{:S(2)}, u32[]{:S(2)}) %collective-permute-start.13) | collective-permute-done | bytes 524320 | tf_op jit(solution)/shard_map/ppermute | solution.py:32
  83.7 2.6 collective-permute-done.15.b3
  87.0 4.2 %terms.3 = bf16[512,768]{1,0:T(8,128)(2,1)} custom-call(bf16[8,2,16,1024]{3,2,1,0:T(8,128)(2,1)} %bitcast.121, bf16[8,2,16,1024]{3,2,1,0:T(8,128)(2,1)} %copy-done.12, bf16[8,2,16,1024]{3,2,1,0:T(8,128)(2,1)} %copy-done.10, bf16[8,2,16,1024]{3,2,1,0:T(8,128)(2,1)} %copy-done.8, bf16[1024,512]{1,0:T(8,128)(2,1)} %fusion.2.wide, bf16[256,1024]{1,0:T(8,128)(2,1)} %pad.13.down), custom_call_target="tpu_custom_call" | custom-call | tf_op jit(solution)/shard_map/terms/pallas_call | solution.py:141
  91.3 4.8 %all-to-all-start.2 = ((bf16[8,64,768]{2,1,0:T(8,128)(2,1)}), bf16[8,64,768]{2,1,0:T(8,128)(2,1)S(1)}, u32[]{:S(2)}, u32[]{:S(2)}) async-start(bf16[8,64,768]{2,1,0:T(8,128)(2,1)} %bitcast.123), calls=%async_computation.2 | async-start | bytes 1572864 | tf_op jit(solution)/shard_map/all_to_all | solution.py:23
  96.1 1.9 fusion.30
  98.1 9.6 %all-to-all-done.2 = bf16[8,64,768]{2,1,0:T(8,128)(2,1)S(1)} async-done(((bf16[8,64,768]{2,1,0:T(8,128)(2,1)}), bf16[8,64,768]{2,1,0:T(8,128)(2,1)S(1)}, u32[]{:S(2)}, u32[]{:S(2)}) %all-to-all-start.2) | async-done | bytes 786464 | tf_op jit(solution)/shard_map/all_to_all | solution.py:23
  108.7 4.9 %all-to-all-start.1 = ((bf16[8,64,768]{2,1,0:T(8,128)(2,1)}), bf16[8,64,768]{2,1,0:T(8,128)(2,1)S(1)}, u32[]{:S(2)}, u32[]{:S(2)}) async-start(bf16[8,64,768]{2,1,0:T(8,128)(2,1)} %broadcast_in_dim.6), calls=%async_computation.1 | async-start | bytes 1572864 | tf_op jit(solution)/shard_map/all_to_all | solution.py:17
  113.6 1.8 fusion.29
  115.6 9.7 %all-to-all-done.1 = bf16[8,64,768]{2,1,0:T(8,128)(2,1)S(1)} async-done(((bf16[8,64,768]{2,1,0:T(8,128)(2,1)}), bf16[8,64,768]{2,1,0:T(8,128)(2,1)S(1)}, u32[]{:S(2)}, u32[]{:S(2)}) %all-to-all-start.1) | async-done | bytes 786464 | tf_op jit(solution)/shard_map/all_to_all | solution.py:17
  126.3 4.9 %all-to-all-start.3 = ((bf16[8,64,768]{2,1,0:T(8,128)(2,1)}), bf16[8,64,768]{2,1,0:T(8,128)(2,1)S(1)}, u32[]{:S(2)}, u32[]{:S(2)}) async-start(bf16[8,64,768]{2,1,0:T(8,128)(2,1)} %broadcast_in_dim.7), calls=%async_computation.3 | async-start | bytes 1572864 | tf_op jit(solution)/shard_map/all_to_all | solution.py:17
  132.1 4.2 %leave.2 = (bf16[8,2,16,1024]{3,2,1,0:T(8,128)(2,1)}, bf16[8,2,16,1024]{3,2,1,0:T(8,128)(2,1)}, bf16[8,2,16,1024]{3,2,1,0:T(8,128)(2,1)}, bf16[8,2,16,1024]{3,2,1,0:T(8,128)(2,1)}) custom-call(bf16[512,768]{1,0:T(8,128)(2,1)} %bitcast.109, bf16[1024,512]{1,0:T(8,128)(2,1)} %fusion.2.wide, bf16[256,1024]{1,0:T(8,128)(2,1)} %pad.13.down), custom_call_target="tpu_custom_call" | custom-call | tf_op jit(solution)/shard_map/leave/pallas_call | solution.py:160
  136.3 4.6 %collective-permute-start.3 = (bf16[8,2,16,1024]{3,2,1,0:T(8,128)(2,1)}, bf16[8,2,16,1024]{3,2,1,0:T(8,128)(2,1)}, u32[]{:S(2)}, u32[]{:S(2)}) collective-permute-start(bf16[8,2,16,1024]{3,2,1,0:T(8,128)(2,1)} %get-tuple-element.14), channel_id=1, source_target_pairs={{0,128},{128,256},{256,384},{384,0},{1,129},{129,257},{257,385},{3... | collective-permute-start | bytes 1572872 | tf_op jit(solution)/shard_map/ppermute | solution.py:32
  140.9 1.7 constant_dynamic-update-slice_fusion.6
  142.6 1.7 constant_dynamic-update-slice_fusion.5
  144.3 4.2 %collective-permute-start.4 = (bf16[8,2,16,1024]{3,2,1,0:T(8,128)(2,1)}, bf16[8,2,16,1024]{3,2,1,0:T(8,128)(2,1)}, u32[]{:S(2)}, u32[]{:S(2)}) collective-permute-start(bf16[8,2,16,1024]{3,2,1,0:T(8,128)(2,1)} %get-tuple-element.15), channel_id=1, source_target_pairs={{0,256},{128,384},{256,0},{384,128},{1,257},{129,385},{257,1},{385... | collective-permute-start | bytes 1572872 | tf_op jit(solution)/shard_map/ppermute | solution.py:32
  148.5 1.9 collective-permute-start.5
  150.4 1.7 constant_dynamic-update-slice_fusion.4
  154.7 4.2 %leave.3 = (bf16[8,2,16,1024]{3,2,1,0:T(8,128)(2,1)}, bf16[8,2,16,1024]{3,2,1,0:T(8,128)(2,1)}, bf16[8,2,16,1024]{3,2,1,0:T(8,128)(2,1)}, bf16[8,2,16,1024]{3,2,1,0:T(8,128)(2,1)}) custom-call(bf16[512,768]{1,0:T(8,128)(2,1)} %bitcast.113, bf16[1024,512]{1,0:T(8,128)(2,1)} %fusion.2.wide, bf16[256,1024]{1,0:T(8,128)(2,1)} %pad.13.down), custom_call_target="tpu_custom_call" | custom-call | tf_op jit(solution)/shard_map/leave/pallas_call | solution.py:160
  158.9 5.1 %collective-permute-start.16 = (bf16[8,2,16,1024]{3,2,1,0:T(8,128)(2,1)}, bf16[8,2,16,1024]{3,2,1,0:T(8,128)(2,1)}, u32[]{:S(2)}, u32[]{:S(2)}) collective-permute-start(bf16[8,2,16,1024]{3,2,1,0:T(8,128)(2,1)} %get-tuple-element.18), channel_id=1, source_target_pairs={{0,128},{128,256},{256,384},{384,0},{1,129},{129,257},{257,385},{3... | collective-permute-start | bytes 1572872 | tf_op jit(solution)/shard_map/ppermute | solution.py:32
  164.0 1.9 collective-permute-start.17
  166.0 3.4 %collective-permute-start.18 = (bf16[8,2,16,1024]{3,2,1,0:T(8,128)(2,1)}, bf16[8,2,16,1024]{3,2,1,0:T(8,128)(2,1)}, u32[]{:S(2)}, u32[]{:S(2)}) collective-permute-start(bf16[8,2,16,1024]{3,2,1,0:T(8,128)(2,1)} %get-tuple-element.20), channel_id=1, source_target_pairs={{0,384},{128,0},{256,128},{384,256},{1,385},{129,1},{257,129},{385... | collective-permute-start | bytes 1572872 | tf_op jit(solution)/shard_map/ppermute | solution.py:32
  170.5 3.6 %collective-permute-done.5.d = bf16[8,2,16,1024]{3,2,1,0:T(8,128)(2,1)} collective-permute-done((bf16[8,2,16,1024]{3,2,1,0:T(8,128)(2,1)}, bf16[8,2,16,1024]{3,2,1,0:T(8,128)(2,1)}, u32[]{:S(2)}, u32[]{:S(2)}) %collective-permute-start.5) | collective-permute-done | bytes 524320 | tf_op jit(solution)/shard_map/ppermute | solution.py:32
  174.1 2.6 add.99
  176.7 1.0 slice_bitcast_fusion.2
  177.7 4.4 %collective-permute-start.6 = (bf16[4,2,16,1024]{3,2,1,0:T(8,128)(2,1)S(1)}, bf16[4,2,16,1024]{3,2,1,0:T(8,128)(2,1)S(1)}, u32[]{:S(2)}, u32[]{:S(2)}) collective-permute-start(bf16[4,2,16,1024]{3,2,1,0:T(8,128)(2,1)S(1)} %slice_bitcast_fusion.2), channel_id=1, source_target_pairs={{0,8},{8,0},{16,24},{24,16},{32,40},{40,32},{48,56},{56,48},{1,9},... | collective-permute-start | bytes 786440 | tf_op jit(solution)/shard_map/ppermute | solution.py:51
  182.2 3.1 %collective-permute-done.17.c = bf16[8,2,16,1024]{3,2,1,0:T(8,128)(2,1)} collective-permute-done((bf16[8,2,16,1024]{3,2,1,0:T(8,128)(2,1)}, bf16[8,2,16,1024]{3,2,1,0:T(8,128)(2,1)}, u32[]{:S(2)}, u32[]{:S(2)}) %collective-permute-start.17) | collective-permute-done | bytes 524320 | tf_op jit(solution)/shard_map/ppermute | solution.py:32
  185.3 10.0 %collective-permute-done.18.d = bf16[8,2,16,1024]{3,2,1,0:T(8,128)(2,1)} collective-permute-done((bf16[8,2,16,1024]{3,2,1,0:T(8,128)(2,1)}, bf16[8,2,16,1024]{3,2,1,0:T(8,128)(2,1)}, u32[]{:S(2)}, u32[]{:S(2)}) %collective-permute-start.18) | collective-permute-done | bytes 524320 | tf_op jit(solution)/shard_map/ppermute | solution.py:32
  195.3 2.6 add.100
  197.9 1.0 slice_bitcast_fusion
  198.9 4.4 %collective-permute-start.19 = (bf16[4,2,16,1024]{3,2,1,0:T(8,128)(2,1)S(1)}, bf16[4,2,16,1024]{3,2,1,0:T(8,128)(2,1)S(1)}, u32[]{:S(2)}, u32[]{:S(2)}) collective-permute-start(bf16[4,2,16,1024]{3,2,1,0:T(8,128)(2,1)S(1)} %slice_bitcast_fusion), channel_id=1, source_target_pairs={{0,8},{8,0},{16,24},{24,16},{32,40},{40,32},{48,56},{56,48},{1,9},... | collective-permute-start | bytes 786440 | tf_op jit(solution)/shard_map/ppermute | solution.py:51
  203.4 3.5 %collective-permute-start.7 = (bf16[2,2,16,1024]{3,2,1,0:T(8,128)(2,1)S(1)}, bf16[2,2,16,1024]{3,2,1,0:T(8,128)(2,1)S(1)}, u32[]{:S(2)}, u32[]{:S(2)}) collective-permute-start(bf16[2,2,16,1024]{3,2,1,0:T(8,128)(2,1)S(1)} %slice_bitcast_fusion.6), channel_id=1, source_target_pairs={{0,16},{8,24},{16,0},{24,8},{32,48},{40,56},{48,32},{56,40},{1,17}... | collective-permute-start | bytes 393224 | tf_op jit(solution)/shard_map/ppermute | solution.py:51
  207.0 5.6 %collective-permute-done.19 = bf16[4,2,16,1024]{3,2,1,0:T(8,128)(2,1)S(1)} collective-permute-done((bf16[4,2,16,1024]{3,2,1,0:T(8,128)(2,1)S(1)}, bf16[4,2,16,1024]{3,2,1,0:T(8,128)(2,1)S(1)}, u32[]{:S(2)}, u32[]{:S(2)}) %collective-permute-start.19) | collective-permute-done | bytes 262176 | tf_op jit(solution)/shard_map/ppermute | solution.py:51
  213.7 3.5 %collective-permute-start.20 = (bf16[2,2,16,1024]{3,2,1,0:T(8,128)(2,1)S(1)}, bf16[2,2,16,1024]{3,2,1,0:T(8,128)(2,1)S(1)}, u32[]{:S(2)}, u32[]{:S(2)}) collective-permute-start(bf16[2,2,16,1024]{3,2,1,0:T(8,128)(2,1)S(1)} %slice_bitcast_fusion.4), channel_id=1, source_target_pairs={{0,16},{8,24},{16,0},{24,8},{32,48},{40,56},{48,32},{56,40},{1,17}... | collective-permute-start | bytes 393224 | tf_op jit(solution)/shard_map/ppermute | solution.py:51
  217.3 5.9 %collective-permute-done.20 = bf16[2,2,16,1024]{3,2,1,0:T(8,128)(2,1)S(1)} collective-permute-done((bf16[2,2,16,1024]{3,2,1,0:T(8,128)(2,1)S(1)}, bf16[2,2,16,1024]{3,2,1,0:T(8,128)(2,1)S(1)}, u32[]{:S(2)}, u32[]{:S(2)}) %collective-permute-start.20) | collective-permute-done | bytes 131104 | tf_op jit(solution)/shard_map/ppermute | solution.py:51
  223.2 7.2 %collective-permute-start.21 = (bf16[1,2,16,1024]{3,2,1,0:T(8,128)(2,1)S(1)}, bf16[1,2,16,1024]{3,2,1,0:T(8,128)(2,1)S(1)}, u32[]{:S(2)}, u32[]{:S(2)}) collective-permute-start(bf16[1,2,16,1024]{3,2,1,0:T(8,128)(2,1)S(1)} %slice_bitcast_fusion.8), channel_id=1, source_target_pairs={{0,32},{8,40},{16,48},{24,56},{32,0},{40,8},{48,16},{56,24},{1,33}... | collective-permute-start | bytes 196616 | tf_op jit(solution)/shard_map/ppermute | solution.py:51
  230.5 2.5 collective-permute-start.8
  233.0 2.4 collective-permute-done.21
  235.4 7.5 %collective-permute-start.22 = (bf16[2,16,1024]{2,1,0:T(8,128)(2,1)S(1)}, bf16[2,16,1024]{2,1,0:T(8,128)(2,1)S(1)}, u32[]{:S(2)}, u32[]{:S(2)}) collective-permute-start(bf16[2,16,1024]{2,1,0:T(8,128)(2,1)S(1)} %fusion.20), channel_id=1, source_target_pairs={{0,96},{8,104},{16,112},{24,120},{32,64},{40,72},{48,80},{56,88},{... | collective-permute-start | bytes 196616 | tf_op jit(solution)/shard_map/ppermute | solution.py:45
  243.7 2.2 collective-permute-done.22
  246.8 11.9 %all-to-all-start.4 = ((bf16[8,2,16,1024]{3,2,1,0:T(8,128)(2,1)}), bf16[8,2,16,1024]{3,2,1,0:T(8,128)(2,1)}, u32[]{:S(2)}, u32[]{:S(2)}) async-start(bf16[8,2,16,1024]{3,2,1,0:T(8,128)(2,1)} %broadcast_in_dim.8), calls=%async_computation.4 | async-start | bytes 1048576 | tf_op jit(solution)/shard_map/all_to_all | solution.py:17
  258.8 1.8 constant_dynamic-update-slice_fusion.2
  262.3 3.2 %convolution_convert_fusion.2 = bf16[1024,224]{0,1:T(8,128)(2,1)} fusion(bf16[1024,1024]{1,0:T(8,128)(2,1)} %constant_dynamic-update-slice_fusion, bf16[512,768]{1,0:T(8,128)(2,1)S(1)} %bitcast.110, bf16[512,768]{1,0:T(8,128)(2,1)S(1)} %bitcast.114), kind=kOutput, calls=%fused_computation.12 | convolution fusion | flops 470908928 | bytes 4128768 | tf_op jit(solution)/shard_map/dot_general | solution.py:61
  265.5 1.5 convolution_convert_fusion.1
  266.9 1.4 convolution_convert_fusion
  268.3 18.1 %all-to-all-done.4 = bf16[8,2,16,1024]{3,2,1,0:T(8,128)(2,1)} async-done(((bf16[8,2,16,1024]{3,2,1,0:T(8,128)(2,1)}), bf16[8,2,16,1024]{3,2,1,0:T(8,128)(2,1)}, u32[]{:S(2)}, u32[]{:S(2)}) %all-to-all-start.4) | async-done | bytes 524320 | tf_op jit(solution)/shard_map/all_to_all | solution.py:17
  286.4 1.9 fusion.32
  (102 shorter events, 17.8 us)
Async XLA Ops:
  0.6 48.0 %copy-start.19 = (bf16[1024,224]{0,1:T(8,128)(2,1)S(1)}, bf16[1024,224]{0,1:T(8,128)(2,1)}, u32[]{:S(2)}) copy-start(bf16[1024,224]{0,1:T(8,128)(2,1)} %param.7) | copy-start | bytes 1376260
  0.6 48.2 %copy-start.20 = (bf16[1024,224]{0,1:T(8,128)(2,1)S(1)}, bf16[1024,224]{0,1:T(8,128)(2,1)}, u32[]{:S(2)}) copy-start(bf16[1024,224]{0,1:T(8,128)(2,1)} %param.6) | copy-start | bytes 1376260
  0.7 48.4 %copy-start.18 = (bf16[224,1024]{1,0:T(8,128)(2,1)S(1)}, bf16[224,1024]{1,0:T(8,128)(2,1)}, u32[]{:S(2)}) copy-start(bf16[224,1024]{1,0:T(8,128)(2,1)} %param.8) | copy-start | bytes 1376260
  3.5 18.3 %collective-permute-start.9 = (bf16[1,2,16,1024]{3,2,1,0:T(8,128)(2,1)S(1)}, bf16[1,2,16,1024]{3,2,1,0:T(8,128)(2,1)S(1)}, u32[]{:S(2)}, u32[]{:S(2)}) collective-permute-start(bf16[1,2,16,1024]{3,2,1,0:T(8,128)(2,1)S(1)} %slice.169), channel_id=1, source_target_pairs={{0,96},{8,104},{16,112},{24,120},{32,64},{40,72},{48,80},{56,88},{... | collective-permute-start | bytes 196616 | tf_op jit(solution)/shard_map/ppermute | solution.py:45
  21.8 12.4 %collective-permute-start.10 = (bf16[1,2,16,1024]{3,2,1,0:T(8,128)(2,1)S(1)}, bf16[1,2,16,1024]{3,2,1,0:T(8,128)(2,1)S(1)}, u32[]{:S(2)}, u32[]{:S(2)}) collective-permute-start(bf16[1,2,16,1024]{3,2,1,0:T(8,128)(2,1)S(1)} %collective-permute-done.9), channel_id=1, source_target_pairs={{0,32},{8,40},{16,48},{24,56},{32,0},{40,8},{48,16},{56,24},{1,33}... | collective-permute-start | bytes 196616 | tf_op jit(solution)/shard_map/ppermute | solution.py:51
  34.2 11.5 %collective-permute-start.11 = (bf16[2,2,16,1024]{3,2,1,0:T(8,128)(2,1)S(1)}, bf16[2,2,16,1024]{3,2,1,0:T(8,128)(2,1)S(1)}, u32[]{:S(2)}, u32[]{:S(2)}) collective-permute-start(bf16[2,2,16,1024]{3,2,1,0:T(8,128)(2,1)S(1)} %get-tuple-element.46), channel_id=1, source_target_pairs={{0,16},{8,24},{16,0},{24,8},{32,48},{40,56},{48,32},{56,40},{1,17}... | collective-permute-start | bytes 393224 | tf_op jit(solution)/shard_map/ppermute | solution.py:51
  36.2 24.8 %collective-permute-start = (bf16[8,2,16,1024]{3,2,1,0:T(8,128)(2,1)}, bf16[8,2,16,1024]{3,2,1,0:T(8,128)(2,1)}, u32[]{:S(2)}, u32[]{:S(2)}) collective-permute-start(bf16[8,2,16,1024]{3,2,1,0:T(8,128)(2,1)} %own.1.b0), channel_id=1, source_target_pairs={{0,384},{128,0},{256,128},{384,256},{1,385},{129,1},{257,129},{385... | collective-permute-start | bytes 1572872 | tf_op jit(solution)/shard_map/ppermute | solution.py:32
  38.8 26.2 %collective-permute-start.1 = (bf16[8,2,16,1024]{3,2,1,0:T(8,128)(2,1)}, bf16[8,2,16,1024]{3,2,1,0:T(8,128)(2,1)}, u32[]{:S(2)}, u32[]{:S(2)}) collective-permute-start(bf16[8,2,16,1024]{3,2,1,0:T(8,128)(2,1)} %own.1.b0), channel_id=1, source_target_pairs={{0,256},{128,384},{256,0},{384,128},{1,257},{129,385},{257,1},{385... | collective-permute-start | bytes 1572872 | tf_op jit(solution)/shard_map/ppermute | solution.py:32
  41.7 26.6 %collective-permute-start.2 = (bf16[8,2,16,1024]{3,2,1,0:T(8,128)(2,1)}, bf16[8,2,16,1024]{3,2,1,0:T(8,128)(2,1)S(1)}, u32[]{:S(2)}, u32[]{:S(2)}) collective-permute-start(bf16[8,2,16,1024]{3,2,1,0:T(8,128)(2,1)} %own.1.b0), channel_id=1, source_target_pairs={{0,128},{128,256},{256,384},{384,0},{1,129},{129,257},{257,385},{3... | collective-permute-start | bytes 1572872 | tf_op jit(solution)/shard_map/ppermute | solution.py:32
  45.8 8.3 %collective-permute-start.12 = (bf16[4,2,16,1024]{3,2,1,0:T(8,128)(2,1)S(1)}, bf16[4,2,16,1024]{3,2,1,0:T(8,128)(2,1)S(1)}, u32[]{:S(2)}, u32[]{:S(2)}) collective-permute-start(bf16[4,2,16,1024]{3,2,1,0:T(8,128)(2,1)S(1)} %bitcast.143), channel_id=1, source_target_pairs={{0,8},{8,0},{16,24},{24,16},{32,40},{40,32},{48,56},{56,48},{1,9},... | collective-permute-start | bytes 786440 | tf_op jit(solution)/shard_map/ppermute | solution.py:51
  54.2 25.5 %copy-start.5 = (bf16[4,2,2,16,1024]{4,3,2,1,0:T(8,128)(2,1)}, bf16[4,2,2,16,1024]{4,3,2,1,0:T(8,128)(2,1)S(1)}, u32[]{:S(2)}) copy-start(bf16[4,2,2,16,1024]{4,3,2,1,0:T(8,128)(2,1)S(1)} %copy.34) | copy-start | bytes 1572868
  54.2 23.9 %copy-start.4 = (bf16[8,2,16,1024]{3,2,1,0:T(8,128)(2,1)S(1)}, bf16[8,2,16,1024]{3,2,1,0:T(8,128)(2,1)}, u32[]{:S(2)}) copy-start(bf16[8,2,16,1024]{3,2,1,0:T(8,128)(2,1)} %own.1.b0) | copy-start | bytes 1572868
  54.2 29.4 %collective-permute-start.13 = (bf16[8,2,16,1024]{3,2,1,0:T(8,128)(2,1)S(1)}, bf16[8,2,16,1024]{3,2,1,0:T(8,128)(2,1)S(1)}, u32[]{:S(2)}, u32[]{:S(2)}) collective-permute-start(bf16[8,2,16,1024]{3,2,1,0:T(8,128)(2,1)S(1)} %bitcast.117), channel_id=1, source_target_pairs={{0,384},{128,0},{256,128},{384,256},{1,385},{129,1},{257,129},{385... | collective-permute-start | bytes 1572872 | tf_op jit(solution)/shard_map/ppermute | solution.py:32
  56.5 27.1 %collective-permute-start.14 = (bf16[8,2,16,1024]{3,2,1,0:T(8,128)(2,1)S(1)}, bf16[8,2,16,1024]{3,2,1,0:T(8,128)(2,1)S(1)}, u32[]{:S(2)}, u32[]{:S(2)}) collective-permute-start(bf16[8,2,16,1024]{3,2,1,0:T(8,128)(2,1)S(1)} %bitcast.118), channel_id=1, source_target_pairs={{0,256},{128,384},{256,0},{384,128},{1,257},{129,385},{257,1},{385... | collective-permute-start | bytes 1572872 | tf_op jit(solution)/shard_map/ppermute | solution.py:32
  60.9 25.3 %collective-permute-start.15 = (bf16[8,2,16,1024]{3,2,1,0:T(8,128)(2,1)S(1)}, bf16[8,2,16,1024]{3,2,1,0:T(8,128)(2,1)S(1)}, u32[]{:S(2)}, u32[]{:S(2)}) collective-permute-start(bf16[8,2,16,1024]{3,2,1,0:T(8,128)(2,1)S(1)} %bitcast.119), channel_id=1, source_target_pairs={{0,128},{128,256},{256,384},{384,0},{1,129},{129,257},{257,385},{3... | collective-permute-start | bytes 1572872 | tf_op jit(solution)/shard_map/ppermute | solution.py:32
  68.3 0.8 copy-start.14
  73.3 17.9 %all-to-all-start = ((bf16[8,64,768]{2,1,0:T(8,128)(2,1)}), bf16[8,64,768]{2,1,0:T(8,128)(2,1)S(1)}, u32[]{:S(2)}, u32[]{:S(2)}) async-start(bf16[8,64,768]{2,1,0:T(8,128)(2,1)} %bitcast.122), calls=%async_computation | async-start | bytes 1572864 | tf_op jit(solution)/shard_map/all_to_all | solution.py:23
  83.6 2.6 copy-start.12
  83.7 2.6 copy-start.10
  86.2 0.8 copy-start.8
  91.3 16.5 %all-to-all-start.2 = ((bf16[8,64,768]{2,1,0:T(8,128)(2,1)}), bf16[8,64,768]{2,1,0:T(8,128)(2,1)S(1)}, u32[]{:S(2)}, u32[]{:S(2)}) async-start(bf16[8,64,768]{2,1,0:T(8,128)(2,1)} %bitcast.123), calls=%async_computation.2 | async-start | bytes 1572864 | tf_op jit(solution)/shard_map/all_to_all | solution.py:23
  108.7 16.6 %all-to-all-start.1 = ((bf16[8,64,768]{2,1,0:T(8,128)(2,1)}), bf16[8,64,768]{2,1,0:T(8,128)(2,1)S(1)}, u32[]{:S(2)}, u32[]{:S(2)}) async-start(bf16[8,64,768]{2,1,0:T(8,128)(2,1)} %broadcast_in_dim.6), calls=%async_computation.1 | async-start | bytes 1572864 | tf_op jit(solution)/shard_map/all_to_all | solution.py:17
  115.4 15.8 %copy-start.15 = (bf16[8,2,16,1024]{3,2,1,0:T(8,128)(2,1)S(1)}, bf16[8,2,16,1024]{3,2,1,0:T(8,128)(2,1)}, u32[]{:S(2)}) copy-start(bf16[8,2,16,1024]{3,2,1,0:T(8,128)(2,1)} %copy-done.14) | copy-start | bytes 1572868
  125.3 6.7 %copy-start = (bf16[8,64,768]{2,1,0:T(8,128)(2,1)}, bf16[8,64,768]{2,1,0:T(8,128)(2,1)S(1)}, u32[]{:S(2)}) copy-start(bf16[8,64,768]{2,1,0:T(8,128)(2,1)S(1)} %all-to-all-done.1) | copy-start | bytes 2359300
  126.3 27.5 %all-to-all-start.3 = ((bf16[8,64,768]{2,1,0:T(8,128)(2,1)}), bf16[8,64,768]{2,1,0:T(8,128)(2,1)S(1)}, u32[]{:S(2)}, u32[]{:S(2)}) async-start(bf16[8,64,768]{2,1,0:T(8,128)(2,1)} %broadcast_in_dim.7), calls=%async_computation.3 | async-start | bytes 1572864 | tf_op jit(solution)/shard_map/all_to_all | solution.py:17
  132.0 20.1 %copy-start.17 = (bf16[8,1,16,1024]{3,2,1,0:T(8,128)(2,1)S(1)}, bf16[8,1,16,1024]{3,2,1,0:T(8,128)(2,1)}, u32[]{:S(2)}) copy-start(bf16[8,1,16,1024]{3,2,1,0:T(8,128)(2,1)} %get-tuple-element.28) | copy-start | bytes 786436
  136.3 16.5 %copy-start.6 = (bf16[1024,1024]{1,0:T(8,128)(2,1)S(1)}, bf16[1024,1024]{1,0:T(8,128)(2,1)}, u32[]{:S(2)}) copy-start(bf16[1024,1024]{1,0:T(8,128)(2,1)} %constant_dynamic-update-slice_fusion.15) | copy-start | bytes 6291460
  136.3 29.7 %collective-permute-start.3 = (bf16[8,2,16,1024]{3,2,1,0:T(8,128)(2,1)}, bf16[8,2,16,1024]{3,2,1,0:T(8,128)(2,1)}, u32[]{:S(2)}, u32[]{:S(2)}) collective-permute-start(bf16[8,2,16,1024]{3,2,1,0:T(8,128)(2,1)} %get-tuple-element.14), channel_id=1, source_target_pairs={{0,128},{128,256},{256,384},{384,0},{1,129},{129,257},{257,385},{3... | collective-permute-start | bytes 1572872 | tf_op jit(solution)/shard_map/ppermute | solution.py:32
  144.3 26.2 %collective-permute-start.4 = (bf16[8,2,16,1024]{3,2,1,0:T(8,128)(2,1)}, bf16[8,2,16,1024]{3,2,1,0:T(8,128)(2,1)}, u32[]{:S(2)}, u32[]{:S(2)}) collective-permute-start(bf16[8,2,16,1024]{3,2,1,0:T(8,128)(2,1)} %get-tuple-element.15), channel_id=1, source_target_pairs={{0,256},{128,384},{256,0},{384,128},{1,257},{129,385},{257,1},{385... | collective-permute-start | bytes 1572872 | tf_op jit(solution)/shard_map/ppermute | solution.py:32
  148.5 25.6 %collective-permute-start.5 = (bf16[8,2,16,1024]{3,2,1,0:T(8,128)(2,1)}, bf16[8,2,16,1024]{3,2,1,0:T(8,128)(2,1)}, u32[]{:S(2)}, u32[]{:S(2)}) collective-permute-start(bf16[8,2,16,1024]{3,2,1,0:T(8,128)(2,1)} %get-tuple-element.16), channel_id=1, source_target_pairs={{0,384},{128,0},{256,128},{384,256},{1,385},{129,1},{257,129},{385... | collective-permute-start | bytes 1572872 | tf_op jit(solution)/shard_map/ppermute | solution.py:32
  153.8 0.9 copy-start.2
  158.9 23.2 %collective-permute-start.16 = (bf16[8,2,16,1024]{3,2,1,0:T(8,128)(2,1)}, bf16[8,2,16,1024]{3,2,1,0:T(8,128)(2,1)}, u32[]{:S(2)}, u32[]{:S(2)}) collective-permute-start(bf16[8,2,16,1024]{3,2,1,0:T(8,128)(2,1)} %get-tuple-element.18), channel_id=1, source_target_pairs={{0,128},{128,256},{256,384},{384,0},{1,129},{129,257},{257,385},{3... | collective-permute-start | bytes 1572872 | tf_op jit(solution)/shard_map/ppermute | solution.py:32
  164.0 21.3 %collective-permute-start.17 = (bf16[8,2,16,1024]{3,2,1,0:T(8,128)(2,1)}, bf16[8,2,16,1024]{3,2,1,0:T(8,128)(2,1)}, u32[]{:S(2)}, u32[]{:S(2)}) collective-permute-start(bf16[8,2,16,1024]{3,2,1,0:T(8,128)(2,1)} %get-tuple-element.19), channel_id=1, source_target_pairs={{0,256},{128,384},{256,0},{384,128},{1,257},{129,385},{257,1},{385... | collective-permute-start | bytes 1572872 | tf_op jit(solution)/shard_map/ppermute | solution.py:32
  166.0 29.4 %collective-permute-start.18 = (bf16[8,2,16,1024]{3,2,1,0:T(8,128)(2,1)}, bf16[8,2,16,1024]{3,2,1,0:T(8,128)(2,1)}, u32[]{:S(2)}, u32[]{:S(2)}) collective-permute-start(bf16[8,2,16,1024]{3,2,1,0:T(8,128)(2,1)} %get-tuple-element.20), channel_id=1, source_target_pairs={{0,384},{128,0},{256,128},{384,256},{1,385},{129,1},{257,129},{385... | collective-permute-start | bytes 1572872 | tf_op jit(solution)/shard_map/ppermute | solution.py:32
  169.4 12.7 %copy-start.16 = (bf16[8,1,16,1024]{3,2,1,0:T(8,128)(2,1)S(1)}, bf16[8,1,16,1024]{3,2,1,0:T(8,128)(2,1)}, u32[]{:S(2)}) copy-start(bf16[8,1,16,1024]{3,2,1,0:T(8,128)(2,1)} %get-tuple-element.27) | copy-start | bytes 786436
  176.7 26.7 %copy-start.7 = (bf16[8,2,16,1024]{3,2,1,0:T(8,128)(2,1)S(1)}, bf16[8,2,16,1024]{3,2,1,0:T(8,128)(2,1)}, u32[]{:S(2)}) copy-start(bf16[8,2,16,1024]{3,2,1,0:T(8,128)(2,1)} %add.99) | copy-start | bytes 1572868
  177.7 25.6 %collective-permute-start.6 = (bf16[4,2,16,1024]{3,2,1,0:T(8,128)(2,1)S(1)}, bf16[4,2,16,1024]{3,2,1,0:T(8,128)(2,1)S(1)}, u32[]{:S(2)}, u32[]{:S(2)}) collective-permute-start(bf16[4,2,16,1024]{3,2,1,0:T(8,128)(2,1)S(1)} %slice_bitcast_fusion.2), channel_id=1, source_target_pairs={{0,8},{8,0},{16,24},{24,16},{32,40},{40,32},{48,56},{56,48},{1,9},... | collective-permute-start | bytes 786440 | tf_op jit(solution)/shard_map/ppermute | solution.py:51
  197.9 45.0 %copy-start.13 = (bf16[8,2,16,1024]{3,2,1,0:T(8,128)(2,1)S(1)}, bf16[8,2,16,1024]{3,2,1,0:T(8,128)(2,1)}, u32[]{:S(2)}) copy-start(bf16[8,2,16,1024]{3,2,1,0:T(8,128)(2,1)} %copy-done.12) | copy-start | bytes 1572868
  198.9 13.7 %collective-permute-start.19 = (bf16[4,2,16,1024]{3,2,1,0:T(8,128)(2,1)S(1)}, bf16[4,2,16,1024]{3,2,1,0:T(8,128)(2,1)S(1)}, u32[]{:S(2)}, u32[]{:S(2)}) collective-permute-start(bf16[4,2,16,1024]{3,2,1,0:T(8,128)(2,1)S(1)} %slice_bitcast_fusion), channel_id=1, source_target_pairs={{0,8},{8,0},{16,24},{24,16},{32,40},{40,32},{48,56},{56,48},{1,9},... | collective-permute-start | bytes 786440 | tf_op jit(solution)/shard_map/ppermute | solution.py:51
  203.4 13.8 %collective-permute-start.7 = (bf16[2,2,16,1024]{3,2,1,0:T(8,128)(2,1)S(1)}, bf16[2,2,16,1024]{3,2,1,0:T(8,128)(2,1)S(1)}, u32[]{:S(2)}, u32[]{:S(2)}) collective-permute-start(bf16[2,2,16,1024]{3,2,1,0:T(8,128)(2,1)S(1)} %slice_bitcast_fusion.6), channel_id=1, source_target_pairs={{0,16},{8,24},{16,0},{24,8},{32,48},{40,56},{48,32},{56,40},{1,17}... | collective-permute-start | bytes 393224 | tf_op jit(solution)/shard_map/ppermute | solution.py:51
  213.7 45.1 %copy-start.11 = (bf16[8,2,16,1024]{3,2,1,0:T(8,128)(2,1)S(1)}, bf16[8,2,16,1024]{3,2,1,0:T(8,128)(2,1)}, u32[]{:S(2)}) copy-start(bf16[8,2,16,1024]{3,2,1,0:T(8,128)(2,1)} %copy-done.10) | copy-start | bytes 1572868
  213.7 9.5 %collective-permute-start.20 = (bf16[2,2,16,1024]{3,2,1,0:T(8,128)(2,1)S(1)}, bf16[2,2,16,1024]{3,2,1,0:T(8,128)(2,1)S(1)}, u32[]{:S(2)}, u32[]{:S(2)}) collective-permute-start(bf16[2,2,16,1024]{3,2,1,0:T(8,128)(2,1)S(1)} %slice_bitcast_fusion.4), channel_id=1, source_target_pairs={{0,16},{8,24},{16,0},{24,8},{32,48},{40,56},{48,32},{56,40},{1,17}... | collective-permute-start | bytes 393224 | tf_op jit(solution)/shard_map/ppermute | solution.py:51
  223.2 12.1 %collective-permute-start.21 = (bf16[1,2,16,1024]{3,2,1,0:T(8,128)(2,1)S(1)}, bf16[1,2,16,1024]{3,2,1,0:T(8,128)(2,1)S(1)}, u32[]{:S(2)}, u32[]{:S(2)}) collective-permute-start(bf16[1,2,16,1024]{3,2,1,0:T(8,128)(2,1)S(1)} %slice_bitcast_fusion.8), channel_id=1, source_target_pairs={{0,32},{8,40},{16,48},{24,56},{32,0},{40,8},{48,16},{56,24},{1,33}... | collective-permute-start | bytes 196616 | tf_op jit(solution)/shard_map/ppermute | solution.py:51
  230.5 13.2 %collective-permute-start.8 = (bf16[1,2,16,1024]{3,2,1,0:T(8,128)(2,1)S(1)}, bf16[1,2,16,1024]{3,2,1,0:T(8,128)(2,1)S(1)}, u32[]{:S(2)}, u32[]{:S(2)}) collective-permute-start(bf16[1,2,16,1024]{3,2,1,0:T(8,128)(2,1)S(1)} %slice_bitcast_fusion.10), channel_id=1, source_target_pairs={{0,32},{8,40},{16,48},{24,56},{32,0},{40,8},{48,16},{56,24},{1,33}... | collective-permute-start | bytes 196616 | tf_op jit(solution)/shard_map/ppermute | solution.py:51
  235.4 10.5 %collective-permute-start.22 = (bf16[2,16,1024]{2,1,0:T(8,128)(2,1)S(1)}, bf16[2,16,1024]{2,1,0:T(8,128)(2,1)S(1)}, u32[]{:S(2)}, u32[]{:S(2)}) collective-permute-start(bf16[2,16,1024]{2,1,0:T(8,128)(2,1)S(1)} %fusion.20), channel_id=1, source_target_pairs={{0,96},{8,104},{16,112},{24,120},{32,64},{40,72},{48,80},{56,88},{... | collective-permute-start | bytes 196616 | tf_op jit(solution)/shard_map/ppermute | solution.py:45
  243.7 17.7 %copy-start.9 = (bf16[8,2,16,1024]{3,2,1,0:T(8,128)(2,1)S(1)}, bf16[8,2,16,1024]{3,2,1,0:T(8,128)(2,1)}, u32[]{:S(2)}) copy-start(bf16[8,2,16,1024]{3,2,1,0:T(8,128)(2,1)} %copy-done.8) | copy-start | bytes 1572868
  246.8 39.6 %all-to-all-start.4 = ((bf16[8,2,16,1024]{3,2,1,0:T(8,128)(2,1)}), bf16[8,2,16,1024]{3,2,1,0:T(8,128)(2,1)}, u32[]{:S(2)}, u32[]{:S(2)}) async-start(bf16[8,2,16,1024]{3,2,1,0:T(8,128)(2,1)} %broadcast_in_dim.8), calls=%async_computation.4 | async-start | bytes 1048576 | tf_op jit(solution)/shard_map/all_to_all | solution.py:17
  258.8 3.4 %copy-start.1 = (bf16[8,64,768]{2,1,0:T(8,128)(2,1)S(1)}, bf16[8,64,768]{2,1,0:T(8,128)(2,1)}, u32[]{:S(2)}) copy-start(bf16[8,64,768]{2,1,0:T(8,128)(2,1)} %copy-done) | copy-start | bytes 2359300
  258.8 3.4 %copy-start.3 = (bf16[8,64,768]{2,1,0:T(8,128)(2,1)S(1)}, bf16[8,64,768]{2,1,0:T(8,128)(2,1)}, u32[]{:S(2)}) copy-start(bf16[8,64,768]{2,1,0:T(8,128)(2,1)} %copy-done.2) | copy-start | bytes 2359300
  262.2 3.2 %copy-start.21 = (bf16[1024,1024]{1,0:T(8,128)(2,1)S(1)}, bf16[1024,1024]{1,0:T(8,128)(2,1)}, u32[]{:S(2)}) copy-start(bf16[1024,1024]{1,0:T(8,128)(2,1)} %constant_dynamic-update-slice_fusion) | copy-start | bytes 6291460

commit v3 on v2

--- a/solution.py
+++ b/solution.py
@@ -51,10 +51,9 @@
     return lax.ppermute(block, "zl", [(i, i ^ (1 << bit)) for i in range(lax.axis_size("zl"))])
 
 
-def halved(tiles, bit):
-    pairs = tiles.reshape(-1, 2, *tiles.shape[1:])
-    got = to_bit(pairs[:, 1], bit)
-    return pairs[:, 0].astype(jnp.float32) + got.astype(jnp.float32)
+def halved(keep, send, bit):
+    got = to_bit(send, bit)
+    return keep.astype(jnp.float32) + got.astype(jnp.float32)
 
 
 def contract_rows(left, right):
@@ -73,40 +72,51 @@
     return jnp.dot(left, right, preferred_element_type=jnp.float32)
 
 
-def own_kernel(zl, tokens, grad, out):
-    for r in range(out.shape[0]):
+def own_kernel(zl, tokens, grad, out, thin):
+    for p, r in enumerate((0, 2, 4, 6, 1, 3, 5, 7)):
         s = jnp.bitwise_xor(zl[0], r)
-        out[r, 0] = tokens[s]
-        out[r, 1] = grad[s]
-
-
-def terms_kernel(b0, b1, b2, b3, wide, down, out):
-    n, _, cut, width = b0.shape
-    rows = n * cut
-    for k, b in enumerate((b0, b1, b2, b3)):
-        t = b[:, 0].reshape(rows, width)
-        g = b[:, 1].reshape(rows, width)
-        at = pl.ds(k * rows, rows)
-        out[at, : 2 * LANES] = matmul(t, wide[...]).astype(jnp.bfloat16)
-        out[at, 2 * LANES :] = contract_cols(g, down[...]).astype(jnp.bfloat16)
+        out[p, 0] = tokens[s]
+        out[p, 1] = grad[s]
+    thin[0, 0] = tokens[zl[0]]
+    thin[0, 1] = grad[zl[0]]
+
+
+def terms_kernel(*refs):
+    *blocks, wide, down, out, t, g = refs
+    at = 0
+    for b in blocks:
+        n, _, cut, width = b.shape
+        rows = pl.ds(at, n * cut)
+        t[rows] = b[:, 0].reshape(n * cut, width)
+        g[rows] = b[:, 1].reshape(n * cut, width)
+        at += n * cut
+    out[:, : 2 * LANES] = matmul(t[...], wide[...]).astype(jnp.bfloat16)
+    out[:, 2 * LANES :] = contract_cols(g[...], down[...]).astype(jnp.bfloat16)
 
 
 def leave_kernel(acts, wide, down, *outs):
-    rows = acts.shape[0] // 4
-    n, _, cut, width = outs[0].shape
-    for d, out in enumerate(outs):
-        at = pl.ds(d * rows, rows)
-        o = matmul(acts[at, :LANES], down[...]).astype(jnp.bfloat16)
-        out[:, 0] = o.reshape(n, cut, width)
-        i = contract_cols(acts[at, LANES:], wide[...]).astype(jnp.bfloat16)
-        out[:, 1] = i.reshape(n, cut, width)
-
-
-def sum_kernel(a, b, c, d, out):
-    f32 = jnp.float32
-    out[...] = (
-        a[...].astype(f32) + b[...].astype(f32) + c[...].astype(f32) + d[...].astype(f32)
-    ).astype(jnp.bfloat16)
+    o = matmul(acts[:, :LANES], down[...]).astype(jnp.bfloat16)
+    i = contract_cols(acts[:, LANES:], wide[...]).astype(jnp.bfloat16)
+    at = 0
+    for out in outs:
+        n, _, cut, width = out.shape
+        out[:, 0] = o[at : at + n * cut].reshape(n, cut, width)
+        out[:, 1] = i[at : at + n * cut].reshape(n, cut, width)
+        at += n * cut
+
+
+def sum_kernel(*refs):
+    *terms, even, odd = refs
+    half = even.shape[0]
+    for out, at in ((even, 0), (odd, half)):
+        rows = pl.ds(at, half)
+        out[...] = sum(t[rows].astype(jnp.float32) for t in terms).astype(jnp.bfloat16)
+
+
+def add(*terms):
+    n, *rest = terms[0].shape
+    shape = jax.ShapeDtypeStruct((n // 2, *rest), jnp.bfloat16)
+    return pl.pallas_call(sum_kernel, out_shape=[shape] * 2, name="add")(*terms)
 
 
 def work(tokens, gate_weight, up_weight, down_weight, out_grad):
@@ -117,9 +127,9 @@
     block = jax.ShapeDtypeStruct((zl, 2, cut, width), jnp.bfloat16)
     more = LANES - hid
     vmem = pl.BlockSpec(memory_space=pltpu.VMEM)
-    own = pl.pallas_call(
+    own, thin = pl.pallas_call(
         own_kernel,
-        out_shape=block,
+        out_shape=[block, jax.ShapeDtypeStruct((1, *block.shape[1:]), jnp.bfloat16)],
         in_specs=[pl.BlockSpec(memory_space=pltpu.SMEM), vmem, vmem],
         name="own",
     )(
@@ -130,17 +140,23 @@
         [jnp.pad(w, ((0, 0), (0, more))) for w in (gate_weight, up_weight)], axis=1
     )
     down = jnp.pad(down_weight, ((0, more), (0, 0)))
-    far = across(own[:1])
+    far = across(thin)
     own = of_ys(own)
-    for bit in HALVING[::-1]:
+    for bit in HALVING[:0:-1]:
         got = to_bit(far, bit)
         far = jnp.stack([far, got], axis=1).reshape(-1, *far.shape[1:])
-    far = of_ys(far)
+    odd = to_bit(far, HALVING[0])
+    direct = to_y(far, -2)
+    far = jnp.concatenate([far, odd], axis=0)
+    b1, b3 = to_y(far, -1), to_y(far, 1)
+    passed = to_y(b1[zl // 2 :], -1)
+    far = [far, b1, direct, passed, b3]
 
     def terms(blocks):
         made = pl.pallas_call(
             terms_kernel,
             out_shape=jax.ShapeDtypeStruct((4 * rows, 3 * LANES), jnp.bfloat16),
+            scratch_shapes=[pltpu.VMEM((4 * rows, width), jnp.bfloat16)] * 2,
             name="terms",
         )(*blocks, wide, down)
         made = exchange(made.reshape(8, rows // 2, -1), GZ)
@@ -158,17 +174,26 @@
 
     def leave(acts):
         parts = pl.pallas_call(leave_kernel, out_shape=[block] * 4, name="leave")(acts, wide, down)
-        back = [to_y(parts[d], d) for d in (1, 2, 3)]
-        mine = pl.pallas_call(sum_kernel, out_shape=block, name="add")(parts[0], *back)
-        return mine
+        back = [to_y(parts[d], d) for d in (2, 1, 3)]
+        return add(parts[0], *back)
 
     own_acts = gates(terms(own))
     far_acts = gates(terms(far))
     own_sum = leave(own_acts)
     far_sum = leave(far_acts)
-    for bit in HALVING:
-        own_sum = halved(own_sum.astype(jnp.bfloat16), bit)
-        far_sum = halved(far_sum.astype(jnp.bfloat16), bit)
+    for k, bit in enumerate(HALVING):
+        own_sum, far_sum = (
+            halved(*pair, bit)
+            for pair in (own_sum, far_sum)
+        )
+        if k < 2:
+            own_sum, far_sum = (
+                (a[:, 0], a[:, 1])
+                for a in (
+                    t.astype(jnp.bfloat16).reshape(-1, 2, *t.shape[1:])
+                    for t in (own_sum, far_sum)
+                )
+            )
     own_sum, far_sum = own_sum[0], far_sum[0].astype(jnp.bfloat16)
     far_sum = across(far_sum)
     ends = (own_sum + far_sum.astype(jnp.float32)).astype(jnp.bfloat16)
@@ -176,7 +201,7 @@
     output, input_grad = (ends[:, k].reshape(rows, width) for k in range(2))
 
     all_tokens, all_grad = (
-        jnp.concatenate([b[:, k].reshape(rows, width) for b in own + far], axis=0)
+        jnp.concatenate([b[:, k].reshape(-1, width) for b in own + far], axis=0)
         for k in range(2)
     )
     acts = jnp.concatenate([own_acts, far_acts], axis=0)

time: 290 us -> 289 us (level)
  the two profiles are of different devices: /device:TPU:26 before, /device:TPU:2 now
where the time goes in v3:
time: 289 us; the launch traced here: 287 us
  starting transfers between devices  123 us (43%)
  waiting for transfers between devices  101 us (35%)
  local copies, waits for them, and re-layouts  30.8 us (11%)
  Pallas kernels  22.3 us (8%)
  matrix products  6.08 us (2%)
    ppermute x13, starting transfers between devices, to_y(): return lax.ppermute(block, 'y', [(i, (i + d) % n) for i in range(n)])  43.1 us
    ppermute x9, starting transfers between devices, to_bit(): lax.ppermute(block, 'zl', [(i, i ^ 1 << bit) for i in range(lax.axis_size...  32.4 us
    ppermute x9, waiting for transfers between devices, to_bit(): lax.ppermute(block, 'zl', [(i, i ^ 1 << bit) for i in range(lax.axis_size...  28.6 us
    all_to_all x3, waiting for transfers between devices, give_all(): lax.all_to_all(jnp.broadcast_to(shard[None], (devices, *shard.shape)), ax...  27.3 us
    ppermute x13, waiting for transfers between devices, to_y(): return lax.ppermute(block, 'y', [(i, (i + d) % n) for i in range(n)])  22.8 us
    all_to_all x3, starting transfers between devices, give_all(): lax.all_to_all(jnp.broadcast_to(shard[None], (devices, *shard.shape)), ax...  20.5 us
    ppermute x2, starting transfers between devices, across(): lax.ppermute(shard, Z, [(i, (i - step if i % zl < step else i + step) % n...  17.5 us
    unnamed x66, local copies, waits for them, and re-layouts  17.2 us
  transfers between devices with their start and end apart: 29, of which 15 were waited for; matrix products, arithmetic and copies ran while one was open for 11% of the time, Pallas kernels for 7%

profile of v3, /device:TPU:2, one launch (start us, length us, event | category | flops | bytes accessed | tf_op | source)
XLA Modules:
  0.0 287.1 jit_solution(9501230712798977750)
XLA Ops:
  0.6 1.9 own.1
  2.5 12.9 %collective-permute-start.9 = (bf16[1,2,16,1024]{3,2,1,0:T(8,128)(2,1)}, bf16[1,2,16,1024]{3,2,1,0:T(8,128)(2,1)S(1)}, u32[]{:S(2)}, u32[]{:S(2)}) collective-permute-start(bf16[1,2,16,1024]{3,2,1,0:T(8,128)(2,1)} %get-tuple-element.26), channel_id=1, source_target_pairs={{0,96},{8,104},{16,112},{24,120},{32,64},{40,72},{48,80},{56,88},{... | collective-permute-start | bytes 196616 | tf_op jit(solution)/shard_map/ppermute | solution.py:45
  15.4 5.9 %collective-permute-done.9 = bf16[1,2,16,1024]{3,2,1,0:T(8,128)(2,1)S(1)} collective-permute-done((bf16[1,2,16,1024]{3,2,1,0:T(8,128)(2,1)}, bf16[1,2,16,1024]{3,2,1,0:T(8,128)(2,1)S(1)}, u32[]{:S(2)}, u32[]{:S(2)}) %collective-permute-start.9) | collective-permute-done | bytes 65568 | tf_op jit(solution)/shard_map/ppermute | solution.py:45
  21.3 6.1 %collective-permute-start.10 = (bf16[1,2,16,1024]{3,2,1,0:T(8,128)(2,1)S(1)}, bf16[1,2,16,1024]{3,2,1,0:T(8,128)(2,1)S(1)}, u32[]{:S(2)}, u32[]{:S(2)}) collective-permute-start(bf16[1,2,16,1024]{3,2,1,0:T(8,128)(2,1)S(1)} %collective-permute-done.9), channel_id=1, source_target_pairs={{0,32},{8,40},{16,48},{24,56},{32,0},{40,8},{48,16},{56,24},{1,33}... | collective-permute-start | bytes 196616 | tf_op jit(solution)/shard_map/ppermute | solution.py:51
  27.3 6.3 %collective-permute-done.10 = bf16[1,2,16,1024]{3,2,1,0:T(8,128)(2,1)S(1)} collective-permute-done((bf16[1,2,16,1024]{3,2,1,0:T(8,128)(2,1)S(1)}, bf16[1,2,16,1024]{3,2,1,0:T(8,128)(2,1)S(1)}, u32[]{:S(2)}, u32[]{:S(2)}) %collective-permute-start.10) | collective-permute-done | bytes 65568 | tf_op jit(solution)/shard_map/ppermute | solution.py:51
  33.6 1.9 collective-permute-start.11
  35.6 5.8 %collective-permute-done.11 = bf16[2,2,16,1024]{3,2,1,0:T(8,128)(2,1)S(1)} collective-permute-done((bf16[2,2,16,1024]{3,2,1,0:T(8,128)(2,1)S(1)}, bf16[2,2,16,1024]{3,2,1,0:T(8,128)(2,1)S(1)}, u32[]{:S(2)}, u32[]{:S(2)}) %collective-permute-start.11) | collective-permute-done | bytes 131104 | tf_op jit(solution)/shard_map/ppermute | solution.py:51
  41.4 1.9 collective-permute-start.12
  43.4 4.9 %collective-permute-start = (bf16[8,2,16,1024]{3,2,1,0:T(8,128)(2,1)}, bf16[8,2,16,1024]{3,2,1,0:T(8,128)(2,1)}, u32[]{:S(2)}, u32[]{:S(2)}) collective-permute-start(bf16[8,2,16,1024]{3,2,1,0:T(8,128)(2,1)} %get-tuple-element.19.refs_0_), channel_id=1, source_target_pairs={{0,384},{128,0},{256,128},{384,256},{1,385},{129,1},{257,129},{385... | collective-permute-start | bytes 1572872 | tf_op jit(solution)/shard_map/ppermute | solution.py:32
  48.3 2.5 collective-permute-start.1
  50.8 2.9 %collective-permute-start.2 = (bf16[8,2,16,1024]{3,2,1,0:T(8,128)(2,1)}, bf16[8,2,16,1024]{3,2,1,0:T(8,128)(2,1)S(1)}, u32[]{:S(2)}, u32[]{:S(2)}) collective-permute-start(bf16[8,2,16,1024]{3,2,1,0:T(8,128)(2,1)} %get-tuple-element.19.refs_0_), channel_id=1, source_target_pairs={{0,128},{128,256},{256,384},{384,0},{1,129},{129,257},{257,385},{3... | collective-permute-start | bytes 1572872 | tf_op jit(solution)/shard_map/ppermute | solution.py:32
  53.7 1.8 fusion.29
  56.3 4.2 %collective-permute-start.13 = (bf16[8,2,16,1024]{3,2,1,0:T(8,128)(2,1)S(1)}, bf16[8,2,16,1024]{3,2,1,0:T(8,128)(2,1)S(1)}, u32[]{:S(2)}, u32[]{:S(2)}) collective-permute-start(bf16[8,2,16,1024]{3,2,1,0:T(8,128)(2,1)S(1)} %pad_maximum_fusion.refs_0_), channel_id=1, source_target_pairs={{0,384},{128,0},{256,128},{384,256},{1,385},{129,1},{257,129},{385... | collective-permute-start | bytes 1572872 | tf_op jit(solution)/shard_map/ppermute | solution.py:32
  61.4 1.2 copy.16
  62.6 1.9 pad.13.refs_5_.down.refs_6_
  64.5 1.7 constant_dynamic-update-slice_fusion.17
  66.2 1.2 fusion.2.refs_4_.wide.refs_5_
  67.4 3.6 %collective-permute-start.14 = (bf16[4,2,16,1024]{3,2,1,0:T(8,128)(2,1)S(1)}, bf16[4,2,16,1024]{3,2,1,0:T(8,128)(2,1)}, u32[]{:S(2)}, u32[]{:S(2)}) collective-permute-start(bf16[4,2,16,1024]{3,2,1,0:T(8,128)(2,1)S(1)} %bitcast.98), channel_id=1, source_target_pairs={{0,256},{128,384},{256,0},{384,128},{1,257},{129,385},{257,1},{385... | collective-permute-start | bytes 786440 | tf_op jit(solution)/shard_map/ppermute | solution.py:32
  71.0 1.9 collective-permute-start.16
  72.9 3.3 %collective-permute-done.2.refs_3_ = bf16[8,2,16,1024]{3,2,1,0:T(8,128)(2,1)S(1)} collective-permute-done((bf16[8,2,16,1024]{3,2,1,0:T(8,128)(2,1)}, bf16[8,2,16,1024]{3,2,1,0:T(8,128)(2,1)S(1)}, u32[]{:S(2)}, u32[]{:S(2)}) %collective-permute-start.2) | collective-permute-done | bytes 524320 | tf_op jit(solution)/shard_map/ppermute | solution.py:32
  77.0 3.9 %terms.2 = bf16[512,768]{1,0:T(8,128)(2,1)} custom-call(bf16[8,2,16,1024]{3,2,1,0:T(8,128)(2,1)} %get-tuple-element.19.refs_0_, bf16[8,2,16,1024]{3,2,1,0:T(8,128)(2,1)} %collective-permute-done.refs_1_, bf16[8,2,16,1024]{3,2,1,0:T(8,128)(2,1)} %copy-done.12, bf16[8,2,16,1024]{3,2,1,0:T(8,128)(2,1)} %copy-done.9, ...), custom_call_target="tpu_custom_call" | custom-call | tf_op jit(solution)/shard_map/terms/pallas_call | solution.py:156
  80.9 5.0 %all-to-all-start = ((bf16[8,64,768]{2,1,0:T(8,128)(2,1)}), bf16[8,64,768]{2,1,0:T(8,128)(2,1)S(1)}, u32[]{:S(2)}, u32[]{:S(2)}) async-start(bf16[8,64,768]{2,1,0:T(8,128)(2,1)} %bitcast.94), calls=%async_computation | async-start | bytes 1572864 | tf_op jit(solution)/shard_map/all_to_all | solution.py:23
  85.9 1.8 fusion.28
  87.7 2.9 %collective-permute-start.15 = (bf16[4,2,16,1024]{3,2,1,0:T(8,128)(2,1)S(1)}, bf16[4,2,16,1024]{3,2,1,0:T(8,128)(2,1)}, u32[]{:S(2)}, u32[]{:S(2)}) collective-permute-start(bf16[4,2,16,1024]{3,2,1,0:T(8,128)(2,1)S(1)} %slice.159), channel_id=1, source_target_pairs={{0,384},{128,0},{256,128},{384,256},{1,385},{129,1},{257,129},{385... | collective-permute-start | bytes 786440 | tf_op jit(solution)/shard_map/ppermute | solution.py:32
  92.8 5.2 %collective-permute-done.15.refs_3_ = bf16[4,2,16,1024]{3,2,1,0:T(8,128)(2,1)} collective-permute-done((bf16[4,2,16,1024]{3,2,1,0:T(8,128)(2,1)S(1)}, bf16[4,2,16,1024]{3,2,1,0:T(8,128)(2,1)}, u32[]{:S(2)}, u32[]{:S(2)}) %collective-permute-start.15) | collective-permute-done | bytes 262176 | tf_op jit(solution)/shard_map/ppermute | solution.py:32
  98.0 3.8 %terms.3 = bf16[512,768]{1,0:T(8,128)(2,1)} custom-call(bf16[8,2,16,1024]{3,2,1,0:T(8,128)(2,1)} %copy-done.11, bf16[8,2,16,1024]{3,2,1,0:T(8,128)(2,1)} %copy-done.4, bf16[4,2,16,1024]{3,2,1,0:T(8,128)(2,1)} %collective-permute-done.14.refs_2_, bf16[4,2,16,1024]{3,2,1,0:T(8,128)(2,1)} %collective-permute-done.15.refs_3_, ...), custom_call_target="tpu_custom_call" | custom-call | tf_op jit(solution)/shard_map/terms/pallas_call | solution.py:156
  101.9 4.8 %all-to-all-start.2 = ((bf16[8,64,768]{2,1,0:T(8,128)(2,1)}), bf16[8,64,768]{2,1,0:T(8,128)(2,1)S(1)}, u32[]{:S(2)}, u32[]{:S(2)}) async-start(bf16[8,64,768]{2,1,0:T(8,128)(2,1)} %bitcast.95), calls=%async_computation.2 | async-start | bytes 1572864 | tf_op jit(solution)/shard_map/all_to_all | solution.py:23
  106.9 11.4 %all-to-all-done.2 = bf16[8,64,768]{2,1,0:T(8,128)(2,1)S(1)} async-done(((bf16[8,64,768]{2,1,0:T(8,128)(2,1)}), bf16[8,64,768]{2,1,0:T(8,128)(2,1)S(1)}, u32[]{:S(2)}, u32[]{:S(2)}) %all-to-all-start.2) | async-done | bytes 786464 | tf_op jit(solution)/shard_map/all_to_all | solution.py:23
  118.3 0.9 broadcast_in_dim.6
  119.3 4.9 %all-to-all-start.1 = ((bf16[8,64,768]{2,1,0:T(8,128)(2,1)}), bf16[8,64,768]{2,1,0:T(8,128)(2,1)S(1)}, u32[]{:S(2)}, u32[]{:S(2)}) async-start(bf16[8,64,768]{2,1,0:T(8,128)(2,1)} %broadcast_in_dim.6), calls=%async_computation.1 | async-start | bytes 1572864 | tf_op jit(solution)/shard_map/all_to_all | solution.py:17
  125.1 10.8 %all-to-all-done.1 = bf16[8,64,768]{2,1,0:T(8,128)(2,1)S(1)} async-done(((bf16[8,64,768]{2,1,0:T(8,128)(2,1)}), bf16[8,64,768]{2,1,0:T(8,128)(2,1)S(1)}, u32[]{:S(2)}, u32[]{:S(2)}) %all-to-all-start.1) | async-done | bytes 786464 | tf_op jit(solution)/shard_map/all_to_all | solution.py:17
  135.9 1.0 broadcast_in_dim.7
  136.9 5.0 %all-to-all-start.3 = ((bf16[8,64,768]{2,1,0:T(8,128)(2,1)}), bf16[8,64,768]{2,1,0:T(8,128)(2,1)S(1)}, u32[]{:S(2)}, u32[]{:S(2)}) async-start(bf16[8,64,768]{2,1,0:T(8,128)(2,1)} %broadcast_in_dim.7), calls=%async_computation.3 | async-start | bytes 1572864 | tf_op jit(solution)/shard_map/all_to_all | solution.py:17
  142.7 3.8 %leave.2 = (bf16[8,2,16,1024]{3,2,1,0:T(8,128)(2,1)}, bf16[8,2,16,1024]{3,2,1,0:T(8,128)(2,1)}, bf16[8,2,16,1024]{3,2,1,0:T(8,128)(2,1)}, bf16[8,2,16,1024]{3,2,1,0:T(8,128)(2,1)}) custom-call(bf16[512,768]{1,0:T(8,128)(2,1)} %bitcast.86, bf16[1024,512]{1,0:T(8,128)(2,1)} %fusion.2.refs_4_.wide.refs_5_, bf16[256,1024]{1,0:T(8,128)(2,1)} %pad.13.refs_5_.down.refs_6_), custom_call_target="tpu_custom_call" | custom-call | tf_op jit(solution)/shard_map/leave/pallas_call | solution.py:176
  146.5 4.2 %collective-permute-start.3 = (bf16[8,2,16,1024]{3,2,1,0:T(8,128)(2,1)}, bf16[8,2,16,1024]{3,2,1,0:T(8,128)(2,1)}, u32[]{:S(2)}, u32[]{:S(2)}) collective-permute-start(bf16[8,2,16,1024]{3,2,1,0:T(8,128)(2,1)} %get-tuple-element.21), channel_id=1, source_target_pairs={{0,256},{128,384},{256,0},{384,128},{1,257},{129,385},{257,1},{385... | collective-permute-start | bytes 1572872 | tf_op jit(solution)/shard_map/ppermute | solution.py:32
  151.4 2.6 collective-permute-start.4
  154.1 4.4 %collective-permute-start.5 = (bf16[8,2,16,1024]{3,2,1,0:T(8,128)(2,1)}, bf16[8,2,16,1024]{3,2,1,0:T(8,128)(2,1)}, u32[]{:S(2)}, u32[]{:S(2)}) collective-permute-start(bf16[8,2,16,1024]{3,2,1,0:T(8,128)(2,1)} %get-tuple-element.23), channel_id=1, source_target_pairs={{0,384},{128,0},{256,128},{384,256},{1,385},{129,1},{257,129},{385... | collective-permute-start | bytes 1572872 | tf_op jit(solution)/shard_map/ppermute | solution.py:32
  159.9 1.0 fusion.32
  161.8 3.9 %leave.3 = (bf16[8,2,16,1024]{3,2,1,0:T(8,128)(2,1)}, bf16[8,2,16,1024]{3,2,1,0:T(8,128)(2,1)}, bf16[8,2,16,1024]{3,2,1,0:T(8,128)(2,1)}, bf16[8,2,16,1024]{3,2,1,0:T(8,128)(2,1)}) custom-call(bf16[512,768]{1,0:T(8,128)(2,1)} %bitcast.90, bf16[1024,512]{1,0:T(8,128)(2,1)} %fusion.2.refs_4_.wide.refs_5_, bf16[256,1024]{1,0:T(8,128)(2,1)} %pad.13.refs_5_.down.refs_6_), custom_call_target="tpu_custom_call" | custom-call | tf_op jit(solution)/shard_map/leave/pallas_call | solution.py:176
  165.7 1.9 collective-permute-start.17
  167.7 2.8 collective-permute-start.18
  170.4 4.3 %collective-permute-start.19 = (bf16[8,2,16,1024]{3,2,1,0:T(8,128)(2,1)}, bf16[8,2,16,1024]{3,2,1,0:T(8,128)(2,1)S(1)}, u32[]{:S(2)}, u32[]{:S(2)}) collective-permute-start(bf16[8,2,16,1024]{3,2,1,0:T(8,128)(2,1)} %get-tuple-element.30), channel_id=1, source_target_pairs={{0,384},{128,0},{256,128},{384,256},{1,385},{129,1},{257,129},{385... | collective-permute-start | bytes 1572872 | tf_op jit(solution)/shard_map/ppermute | solution.py:32
  176.3 2.5 add.95
  178.8 4.0 %collective-permute-start.6 = (bf16[4,2,16,1024]{3,2,1,0:T(8,128)(2,1)}, bf16[4,2,16,1024]{3,2,1,0:T(8,128)(2,1)S(1)}, u32[]{:S(2)}, u32[]{:S(2)}) collective-permute-start(bf16[4,2,16,1024]{3,2,1,0:T(8,128)(2,1)} %get-tuple-element.25), channel_id=1, source_target_pairs={{0,8},{8,0},{16,24},{24,16},{32,40},{40,32},{48,56},{56,48},{1,9},... | collective-permute-start | bytes 786440 | tf_op jit(solution)/shard_map/ppermute | solution.py:51
  184.4 3.1 %collective-permute-done.17.refs_1_ = bf16[8,2,16,1024]{3,2,1,0:T(8,128)(2,1)S(1)} collective-permute-done((bf16[8,2,16,1024]{3,2,1,0:T(8,128)(2,1)}, bf16[8,2,16,1024]{3,2,1,0:T(8,128)(2,1)S(1)}, u32[]{:S(2)}, u32[]{:S(2)}) %collective-permute-start.17) | collective-permute-done | bytes 524320 | tf_op jit(solution)/shard_map/ppermute | solution.py:32
  187.4 10.3 %collective-permute-done.18.refs_2_ = bf16[8,2,16,1024]{3,2,1,0:T(8,128)(2,1)S(1)} collective-permute-done((bf16[8,2,16,1024]{3,2,1,0:T(8,128)(2,1)}, bf16[8,2,16,1024]{3,2,1,0:T(8,128)(2,1)S(1)}, u32[]{:S(2)}, u32[]{:S(2)}) %collective-permute-start.18) | collective-permute-done | bytes 524320 | tf_op jit(solution)/shard_map/ppermute | solution.py:32
  198.7 2.5 add.96
  201.2 3.9 %collective-permute-start.20 = (bf16[4,2,16,1024]{3,2,1,0:T(8,128)(2,1)}, bf16[4,2,16,1024]{3,2,1,0:T(8,128)(2,1)S(1)}, u32[]{:S(2)}, u32[]{:S(2)}) collective-permute-start(bf16[4,2,16,1024]{3,2,1,0:T(8,128)(2,1)} %get-tuple-element.32), channel_id=1, source_target_pairs={{0,8},{8,0},{16,24},{24,16},{32,40},{40,32},{48,56},{56,48},{1,9},... | collective-permute-start | bytes 786440 | tf_op jit(solution)/shard_map/ppermute | solution.py:51
  205.2 2.5 collective-permute-start.7
  207.8 6.8 %collective-permute-done.20 = bf16[4,2,16,1024]{3,2,1,0:T(8,128)(2,1)S(1)} collective-permute-done((bf16[4,2,16,1024]{3,2,1,0:T(8,128)(2,1)}, bf16[4,2,16,1024]{3,2,1,0:T(8,128)(2,1)S(1)}, u32[]{:S(2)}, u32[]{:S(2)}) %collective-permute-start.20) | collective-permute-done | bytes 262176 | tf_op jit(solution)/shard_map/ppermute | solution.py:51
  214.6 1.0 add_convert_fusion
  215.7 2.2 collective-permute-start.21
  218.0 6.7 %collective-permute-done.21 = bf16[2,2,16,1024]{3,2,1,0:T(8,128)(2,1)S(1)} collective-permute-done((bf16[2,2,16,1024]{3,2,1,0:T(8,128)(2,1)S(1)}, bf16[2,2,16,1024]{3,2,1,0:T(8,128)(2,1)S(1)}, u32[]{:S(2)}, u32[]{:S(2)}) %collective-permute-start.21) | collective-permute-done | bytes 131104 | tf_op jit(solution)/shard_map/ppermute | solution.py:51
  224.8 6.1 %collective-permute-start.22 = (bf16[1,2,16,1024]{3,2,1,0:T(8,128)(2,1)S(1)}, bf16[1,2,16,1024]{3,2,1,0:T(8,128)(2,1)S(1)}, u32[]{:S(2)}, u32[]{:S(2)}) collective-permute-start(bf16[1,2,16,1024]{3,2,1,0:T(8,128)(2,1)S(1)} %slice_bitcast_fusion.4), channel_id=1, source_target_pairs={{0,32},{8,40},{16,48},{24,56},{32,0},{40,8},{48,16},{56,24},{1,33}... | collective-permute-start | bytes 196616 | tf_op jit(solution)/shard_map/ppermute | solution.py:51
  230.9 3.7 %collective-permute-start.8 = (bf16[1,2,16,1024]{3,2,1,0:T(8,128)(2,1)S(1)}, bf16[1,2,16,1024]{3,2,1,0:T(8,128)(2,1)S(1)}, u32[]{:S(2)}, u32[]{:S(2)}) collective-permute-start(bf16[1,2,16,1024]{3,2,1,0:T(8,128)(2,1)S(1)} %slice_bitcast_fusion.6), channel_id=1, source_target_pairs={{0,32},{8,40},{16,48},{24,56},{32,0},{40,8},{48,16},{56,24},{1,33}... | collective-permute-start | bytes 196616 | tf_op jit(solution)/shard_map/ppermute | solution.py:51
  234.6 2.9 %collective-permute-done.22 = bf16[1,2,16,1024]{3,2,1,0:T(8,128)(2,1)S(1)} collective-permute-done((bf16[1,2,16,1024]{3,2,1,0:T(8,128)(2,1)S(1)}, bf16[1,2,16,1024]{3,2,1,0:T(8,128)(2,1)S(1)}, u32[]{:S(2)}, u32[]{:S(2)}) %collective-permute-start.22) | collective-permute-done | bytes 65568 | tf_op jit(solution)/shard_map/ppermute | solution.py:51
  237.5 4.6 %collective-permute-start.23 = (bf16[2,16,1024]{2,1,0:T(8,128)(2,1)S(1)}, bf16[2,16,1024]{2,1,0:T(8,128)(2,1)S(1)}, u32[]{:S(2)}, u32[]{:S(2)}) collective-permute-start(bf16[2,16,1024]{2,1,0:T(8,128)(2,1)S(1)} %fusion.20), channel_id=1, source_target_pairs={{0,96},{8,104},{16,112},{24,120},{32,64},{40,72},{48,80},{56,88},{... | collective-permute-start | bytes 196616 | tf_op jit(solution)/shard_map/ppermute | solution.py:45
  242.8 4.8 %collective-permute-done.23 = bf16[2,16,1024]{2,1,0:T(8,128)(2,1)S(1)} collective-permute-done((bf16[2,16,1024]{2,1,0:T(8,128)(2,1)S(1)}, bf16[2,16,1024]{2,1,0:T(8,128)(2,1)S(1)}, u32[]{:S(2)}, u32[]{:S(2)}) %collective-permute-start.23) | collective-permute-done | bytes 65568 | tf_op jit(solution)/shard_map/ppermute | solution.py:45
  248.5 10.6 %all-to-all-start.4 = ((bf16[8,2,16,1024]{3,2,1,0:T(8,128)(2,1)}), bf16[8,2,16,1024]{3,2,1,0:T(8,128)(2,1)S(1)}, u32[]{:S(2)}, u32[]{:S(2)}) async-start(bf16[8,2,16,1024]{3,2,1,0:T(8,128)(2,1)} %broadcast_in_dim.8), calls=%async_computation.4 | async-start | bytes 1048576 | tf_op jit(solution)/shard_map/all_to_all | solution.py:17
  259.8 1.0 fusion.31
  263.6 3.2 %convolution_convert_fusion.2 = bf16[1024,224]{0,1:T(8,128)(2,1)} fusion(bf16[1024,1024]{1,0:T(8,128)(2,1)} %constant_dynamic-update-slice_fusion, bf16[512,768]{1,0:T(8,128)(2,1)S(1)} %bitcast.87, bf16[512,768]{1,0:T(8,128)(2,1)S(1)} %bitcast.91), kind=kOutput, calls=%fused_computation.12 | convolution fusion | flops 470908928 | bytes 4128768 | tf_op jit(solution)/shard_map/dot_general | solution.py:60
  266.8 1.5 convolution_convert_fusion.1
  268.4 1.4 convolution_convert_fusion
  269.8 16.5 %all-to-all-done.4 = bf16[8,2,16,1024]{3,2,1,0:T(8,128)(2,1)S(1)} async-done(((bf16[8,2,16,1024]{3,2,1,0:T(8,128)(2,1)}), bf16[8,2,16,1024]{3,2,1,0:T(8,128)(2,1)S(1)}, u32[]{:S(2)}, u32[]{:S(2)}) %all-to-all-start.4) | async-done | bytes 524320 | tf_op jit(solution)/shard_map/all_to_all | solution.py:17
  (108 shorter events, 20.0 us)
Async XLA Ops:
  2.5 58.7 %copy-start.21 = (bf16[1024,224]{0,1:T(8,128)(2,1)S(1)}, bf16[1024,224]{0,1:T(8,128)(2,1)}, u32[]{:S(2)}) copy-start(bf16[1024,224]{0,1:T(8,128)(2,1)} %param.7) | copy-start | bytes 1376260
  2.5 18.8 %collective-permute-start.9 = (bf16[1,2,16,1024]{3,2,1,0:T(8,128)(2,1)}, bf16[1,2,16,1024]{3,2,1,0:T(8,128)(2,1)S(1)}, u32[]{:S(2)}, u32[]{:S(2)}) collective-permute-start(bf16[1,2,16,1024]{3,2,1,0:T(8,128)(2,1)} %get-tuple-element.26), channel_id=1, source_target_pairs={{0,96},{8,104},{16,112},{24,120},{32,64},{40,72},{48,80},{56,88},{... | collective-permute-start | bytes 196616 | tf_op jit(solution)/shard_map/ppermute | solution.py:45
  21.3 12.3 %collective-permute-start.10 = (bf16[1,2,16,1024]{3,2,1,0:T(8,128)(2,1)S(1)}, bf16[1,2,16,1024]{3,2,1,0:T(8,128)(2,1)S(1)}, u32[]{:S(2)}, u32[]{:S(2)}) collective-permute-start(bf16[1,2,16,1024]{3,2,1,0:T(8,128)(2,1)S(1)} %collective-permute-done.9), channel_id=1, source_target_pairs={{0,32},{8,40},{16,48},{24,56},{32,0},{40,8},{48,16},{56,24},{1,33}... | collective-permute-start | bytes 196616 | tf_op jit(solution)/shard_map/ppermute | solution.py:51
  33.6 7.8 %collective-permute-start.11 = (bf16[2,2,16,1024]{3,2,1,0:T(8,128)(2,1)S(1)}, bf16[2,2,16,1024]{3,2,1,0:T(8,128)(2,1)S(1)}, u32[]{:S(2)}, u32[]{:S(2)}) collective-permute-start(bf16[2,2,16,1024]{3,2,1,0:T(8,128)(2,1)S(1)} %get-tuple-element.60), channel_id=1, source_target_pairs={{0,16},{8,24},{16,0},{24,8},{32,48},{40,56},{48,32},{56,40},{1,17}... | collective-permute-start | bytes 393224 | tf_op jit(solution)/shard_map/ppermute | solution.py:51
  41.4 14.1 %collective-permute-start.12 = (bf16[4,2,16,1024]{3,2,1,0:T(8,128)(2,1)S(1)}, bf16[4,2,16,1024]{3,2,1,0:T(8,128)(2,1)S(1)}, u32[]{:S(2)}, u32[]{:S(2)}) collective-permute-start(bf16[4,2,16,1024]{3,2,1,0:T(8,128)(2,1)S(1)} %bitcast.96), channel_id=1, source_target_pairs={{0,8},{8,0},{16,24},{24,16},{32,40},{40,32},{48,56},{56,48},{1,9},... | collective-permute-start | bytes 786440 | tf_op jit(solution)/shard_map/ppermute | solution.py:51
  43.4 27.6 %collective-permute-start = (bf16[8,2,16,1024]{3,2,1,0:T(8,128)(2,1)}, bf16[8,2,16,1024]{3,2,1,0:T(8,128)(2,1)}, u32[]{:S(2)}, u32[]{:S(2)}) collective-permute-start(bf16[8,2,16,1024]{3,2,1,0:T(8,128)(2,1)} %get-tuple-element.19.refs_0_), channel_id=1, source_target_pairs={{0,384},{128,0},{256,128},{384,256},{1,385},{129,1},{257,129},{385... | collective-permute-start | bytes 1572872 | tf_op jit(solution)/shard_map/ppermute | solution.py:32
  48.3 24.6 %collective-permute-start.1 = (bf16[8,2,16,1024]{3,2,1,0:T(8,128)(2,1)}, bf16[8,2,16,1024]{3,2,1,0:T(8,128)(2,1)S(1)}, u32[]{:S(2)}, u32[]{:S(2)}) collective-permute-start(bf16[8,2,16,1024]{3,2,1,0:T(8,128)(2,1)} %get-tuple-element.19.refs_0_), channel_id=1, source_target_pairs={{0,256},{128,384},{256,0},{384,128},{1,257},{129,385},{257,1},{385... | collective-permute-start | bytes 1572872 | tf_op jit(solution)/shard_map/ppermute | solution.py:32
  50.8 25.4 %collective-permute-start.2 = (bf16[8,2,16,1024]{3,2,1,0:T(8,128)(2,1)}, bf16[8,2,16,1024]{3,2,1,0:T(8,128)(2,1)S(1)}, u32[]{:S(2)}, u32[]{:S(2)}) collective-permute-start(bf16[8,2,16,1024]{3,2,1,0:T(8,128)(2,1)} %get-tuple-element.19.refs_0_), channel_id=1, source_target_pairs={{0,128},{128,256},{256,384},{384,0},{1,129},{129,257},{257,385},{3... | collective-permute-start | bytes 1572872 | tf_op jit(solution)/shard_map/ppermute | solution.py:32
  55.5 0.7 copy-start.16
  56.3 14.7 %copy-start.11 = (bf16[8,2,16,1024]{3,2,1,0:T(8,128)(2,1)}, bf16[8,2,16,1024]{3,2,1,0:T(8,128)(2,1)S(1)}, u32[]{:S(2)}) copy-start(bf16[8,2,16,1024]{3,2,1,0:T(8,128)(2,1)S(1)} %pad_maximum_fusion.refs_0_) | copy-start | bytes 1572868
  56.3 31.4 %collective-permute-start.13 = (bf16[8,2,16,1024]{3,2,1,0:T(8,128)(2,1)S(1)}, bf16[8,2,16,1024]{3,2,1,0:T(8,128)(2,1)S(1)}, u32[]{:S(2)}, u32[]{:S(2)}) collective-permute-start(bf16[8,2,16,1024]{3,2,1,0:T(8,128)(2,1)S(1)} %pad_maximum_fusion.refs_0_), channel_id=1, source_target_pairs={{0,384},{128,0},{256,128},{384,256},{1,385},{129,1},{257,129},{385... | collective-permute-start | bytes 1572872 | tf_op jit(solution)/shard_map/ppermute | solution.py:32
  67.4 25.4 %collective-permute-start.14 = (bf16[4,2,16,1024]{3,2,1,0:T(8,128)(2,1)S(1)}, bf16[4,2,16,1024]{3,2,1,0:T(8,128)(2,1)}, u32[]{:S(2)}, u32[]{:S(2)}) collective-permute-start(bf16[4,2,16,1024]{3,2,1,0:T(8,128)(2,1)S(1)} %bitcast.98), channel_id=1, source_target_pairs={{0,256},{128,384},{256,0},{384,128},{1,257},{129,385},{257,1},{385... | collective-permute-start | bytes 786440 | tf_op jit(solution)/shard_map/ppermute | solution.py:32
  71.0 21.8 %collective-permute-start.16 = (bf16[8,2,16,1024]{3,2,1,0:T(8,128)(2,1)S(1)}, bf16[8,2,16,1024]{3,2,1,0:T(8,128)(2,1)S(1)}, u32[]{:S(2)}, u32[]{:S(2)}) collective-permute-start(bf16[8,2,16,1024]{3,2,1,0:T(8,128)(2,1)S(1)} %pad_maximum_fusion.refs_0_), channel_id=1, source_target_pairs={{0,128},{128,256},{256,384},{384,0},{1,129},{129,257},{257,385},{3... | collective-permute-start | bytes 1572872 | tf_op jit(solution)/shard_map/ppermute | solution.py:32
  72.9 3.3 %copy-start.12 = (bf16[8,2,16,1024]{3,2,1,0:T(8,128)(2,1)}, bf16[8,2,16,1024]{3,2,1,0:T(8,128)(2,1)S(1)}, u32[]{:S(2)}) copy-start(bf16[8,2,16,1024]{3,2,1,0:T(8,128)(2,1)S(1)} %collective-permute-done.1.refs_2_) | copy-start | bytes 1572868
  76.3 0.8 copy-start.9
  80.9 9.7 %copy-start.13 = (bf16[8,2,16,1024]{3,2,1,0:T(8,128)(2,1)S(1)}, bf16[8,2,16,1024]{3,2,1,0:T(8,128)(2,1)}, u32[]{:S(2)}) copy-start(bf16[8,2,16,1024]{3,2,1,0:T(8,128)(2,1)} %copy-done.12) | copy-start | bytes 1572868
  80.9 21.0 %all-to-all-start = ((bf16[8,64,768]{2,1,0:T(8,128)(2,1)}), bf16[8,64,768]{2,1,0:T(8,128)(2,1)S(1)}, u32[]{:S(2)}, u32[]{:S(2)}) async-start(bf16[8,64,768]{2,1,0:T(8,128)(2,1)} %bitcast.94), calls=%async_computation | async-start | bytes 1572864 | tf_op jit(solution)/shard_map/all_to_all | solution.py:23
  87.7 10.4 %copy-start.4 = (bf16[8,2,16,1024]{3,2,1,0:T(8,128)(2,1)}, bf16[8,2,16,1024]{3,2,1,0:T(8,128)(2,1)S(1)}, u32[]{:S(2)}) copy-start(bf16[8,2,16,1024]{3,2,1,0:T(8,128)(2,1)S(1)} %collective-permute-done.13.refs_1_) | copy-start | bytes 1572868
  87.7 10.3 %collective-permute-start.15 = (bf16[4,2,16,1024]{3,2,1,0:T(8,128)(2,1)S(1)}, bf16[4,2,16,1024]{3,2,1,0:T(8,128)(2,1)}, u32[]{:S(2)}, u32[]{:S(2)}) collective-permute-start(bf16[4,2,16,1024]{3,2,1,0:T(8,128)(2,1)S(1)} %slice.159), channel_id=1, source_target_pairs={{0,384},{128,0},{256,128},{384,256},{1,385},{129,1},{257,129},{385... | collective-permute-start | bytes 786440 | tf_op jit(solution)/shard_map/ppermute | solution.py:32
  92.8 13.9 %copy-start.10 = (bf16[8,2,16,1024]{3,2,1,0:T(8,128)(2,1)S(1)}, bf16[8,2,16,1024]{3,2,1,0:T(8,128)(2,1)}, u32[]{:S(2)}) copy-start(bf16[8,2,16,1024]{3,2,1,0:T(8,128)(2,1)} %copy-done.9) | copy-start | bytes 1572868
  92.8 5.2 %copy-start.7 = (bf16[8,2,16,1024]{3,2,1,0:T(8,128)(2,1)}, bf16[8,2,16,1024]{3,2,1,0:T(8,128)(2,1)S(1)}, u32[]{:S(2)}) copy-start(bf16[8,2,16,1024]{3,2,1,0:T(8,128)(2,1)S(1)} %collective-permute-done.16.refs_4_) | copy-start | bytes 1572868
  101.9 16.5 %all-to-all-start.2 = ((bf16[8,64,768]{2,1,0:T(8,128)(2,1)}), bf16[8,64,768]{2,1,0:T(8,128)(2,1)S(1)}, u32[]{:S(2)}, u32[]{:S(2)}) async-start(bf16[8,64,768]{2,1,0:T(8,128)(2,1)} %bitcast.95), calls=%async_computation.2 | async-start | bytes 1572864 | tf_op jit(solution)/shard_map/all_to_all | solution.py:23
  106.7 18.2 %copy-start.17 = (bf16[4,2,16,1024]{3,2,1,0:T(8,128)(2,1)S(1)}, bf16[4,2,16,1024]{3,2,1,0:T(8,128)(2,1)}, u32[]{:S(2)}) copy-start(bf16[4,2,16,1024]{3,2,1,0:T(8,128)(2,1)} %copy-done.16) | copy-start | bytes 786436
  119.3 16.6 %all-to-all-start.1 = ((bf16[8,64,768]{2,1,0:T(8,128)(2,1)}), bf16[8,64,768]{2,1,0:T(8,128)(2,1)S(1)}, u32[]{:S(2)}, u32[]{:S(2)}) async-start(bf16[8,64,768]{2,1,0:T(8,128)(2,1)} %broadcast_in_dim.6), calls=%async_computation.1 | async-start | bytes 1572864 | tf_op jit(solution)/shard_map/all_to_all | solution.py:17
  135.9 6.8 %copy-start = (bf16[8,64,768]{2,1,0:T(8,128)(2,1)}, bf16[8,64,768]{2,1,0:T(8,128)(2,1)S(1)}, u32[]{:S(2)}) copy-start(bf16[8,64,768]{2,1,0:T(8,128)(2,1)S(1)} %all-to-all-done.1) | copy-start | bytes 2359300
  136.9 13.8 %copy-start.14 = (bf16[8,1,16,1024]{3,2,1,0:T(8,128)(2,1)S(1)}, bf16[8,1,16,1024]{3,2,1,0:T(8,128)(2,1)}, u32[]{:S(2)}) copy-start(bf16[8,1,16,1024]{3,2,1,0:T(8,128)(2,1)} %get-tuple-element.43) | copy-start | bytes 786436
  136.9 24.0 %all-to-all-start.3 = ((bf16[8,64,768]{2,1,0:T(8,128)(2,1)}), bf16[8,64,768]{2,1,0:T(8,128)(2,1)S(1)}, u32[]{:S(2)}, u32[]{:S(2)}) async-start(bf16[8,64,768]{2,1,0:T(8,128)(2,1)} %broadcast_in_dim.7), calls=%async_computation.3 | async-start | bytes 1572864 | tf_op jit(solution)/shard_map/all_to_all | solution.py:17
  142.0 16.5 %copy-start.15 = (bf16[8,1,16,1024]{3,2,1,0:T(8,128)(2,1)S(1)}, bf16[8,1,16,1024]{3,2,1,0:T(8,128)(2,1)}, u32[]{:S(2)}) copy-start(bf16[8,1,16,1024]{3,2,1,0:T(8,128)(2,1)} %get-tuple-element.41) | copy-start | bytes 786436
  146.5 24.0 %collective-permute-start.3 = (bf16[8,2,16,1024]{3,2,1,0:T(8,128)(2,1)}, bf16[8,2,16,1024]{3,2,1,0:T(8,128)(2,1)}, u32[]{:S(2)}, u32[]{:S(2)}) collective-permute-start(bf16[8,2,16,1024]{3,2,1,0:T(8,128)(2,1)} %get-tuple-element.21), channel_id=1, source_target_pairs={{0,256},{128,384},{256,0},{384,128},{1,257},{129,385},{257,1},{385... | collective-permute-start | bytes 1572872 | tf_op jit(solution)/shard_map/ppermute | solution.py:32
  151.4 24.9 %collective-permute-start.4 = (bf16[8,2,16,1024]{3,2,1,0:T(8,128)(2,1)}, bf16[8,2,16,1024]{3,2,1,0:T(8,128)(2,1)}, u32[]{:S(2)}, u32[]{:S(2)}) collective-permute-start(bf16[8,2,16,1024]{3,2,1,0:T(8,128)(2,1)} %get-tuple-element.22), channel_id=1, source_target_pairs={{0,128},{128,256},{256,384},{384,0},{1,129},{129,257},{257,385},{3... | collective-permute-start | bytes 1572872 | tf_op jit(solution)/shard_map/ppermute | solution.py:32
  154.1 22.2 %collective-permute-start.5 = (bf16[8,2,16,1024]{3,2,1,0:T(8,128)(2,1)}, bf16[8,2,16,1024]{3,2,1,0:T(8,128)(2,1)}, u32[]{:S(2)}, u32[]{:S(2)}) collective-permute-start(bf16[8,2,16,1024]{3,2,1,0:T(8,128)(2,1)} %get-tuple-element.23), channel_id=1, source_target_pairs={{0,384},{128,0},{256,128},{384,256},{1,385},{129,1},{257,129},{385... | collective-permute-start | bytes 1572872 | tf_op jit(solution)/shard_map/ppermute | solution.py:32
  160.9 0.9 copy-start.2
  161.8 21.0 %copy-start.5 = (bf16[8,2,16,1024]{3,2,1,0:T(8,128)(2,1)S(1)}, bf16[8,2,16,1024]{3,2,1,0:T(8,128)(2,1)}, u32[]{:S(2)}) copy-start(bf16[8,2,16,1024]{3,2,1,0:T(8,128)(2,1)} %copy-done.4) | copy-start | bytes 1572868
  165.7 21.7 %collective-permute-start.17 = (bf16[8,2,16,1024]{3,2,1,0:T(8,128)(2,1)}, bf16[8,2,16,1024]{3,2,1,0:T(8,128)(2,1)S(1)}, u32[]{:S(2)}, u32[]{:S(2)}) collective-permute-start(bf16[8,2,16,1024]{3,2,1,0:T(8,128)(2,1)} %get-tuple-element.28), channel_id=1, source_target_pairs={{0,256},{128,384},{256,0},{384,128},{1,257},{129,385},{257,1},{385... | collective-permute-start | bytes 1572872 | tf_op jit(solution)/shard_map/ppermute | solution.py:32
  167.7 30.1 %collective-permute-start.18 = (bf16[8,2,16,1024]{3,2,1,0:T(8,128)(2,1)}, bf16[8,2,16,1024]{3,2,1,0:T(8,128)(2,1)S(1)}, u32[]{:S(2)}, u32[]{:S(2)}) collective-permute-start(bf16[8,2,16,1024]{3,2,1,0:T(8,128)(2,1)} %get-tuple-element.29), channel_id=1, source_target_pairs={{0,128},{128,256},{256,384},{384,0},{1,129},{129,257},{257,385},{3... | collective-permute-start | bytes 1572872 | tf_op jit(solution)/shard_map/ppermute | solution.py:32
  170.4 27.3 %collective-permute-start.19 = (bf16[8,2,16,1024]{3,2,1,0:T(8,128)(2,1)}, bf16[8,2,16,1024]{3,2,1,0:T(8,128)(2,1)S(1)}, u32[]{:S(2)}, u32[]{:S(2)}) collective-permute-start(bf16[8,2,16,1024]{3,2,1,0:T(8,128)(2,1)} %get-tuple-element.30), channel_id=1, source_target_pairs={{0,384},{128,0},{256,128},{384,256},{1,385},{129,1},{257,129},{385... | collective-permute-start | bytes 1572872 | tf_op jit(solution)/shard_map/ppermute | solution.py:32
  178.8 26.3 %copy-start.22 = (bf16[4,2,16,1024]{3,2,1,0:T(8,128)(2,1)S(1)}, bf16[4,2,16,1024]{3,2,1,0:T(8,128)(2,1)}, u32[]{:S(2)}) copy-start(bf16[4,2,16,1024]{3,2,1,0:T(8,128)(2,1)} %get-tuple-element.24) | copy-start | bytes 786436
  178.8 26.3 %collective-permute-start.6 = (bf16[4,2,16,1024]{3,2,1,0:T(8,128)(2,1)}, bf16[4,2,16,1024]{3,2,1,0:T(8,128)(2,1)S(1)}, u32[]{:S(2)}, u32[]{:S(2)}) collective-permute-start(bf16[4,2,16,1024]{3,2,1,0:T(8,128)(2,1)} %get-tuple-element.25), channel_id=1, source_target_pairs={{0,8},{8,0},{16,24},{24,16},{32,40},{40,32},{48,56},{56,48},{1,9},... | collective-permute-start | bytes 786440 | tf_op jit(solution)/shard_map/ppermute | solution.py:51
  187.4 10.3 %copy-start.18 = (bf16[8,2,16,1024]{3,2,1,0:T(8,128)(2,1)}, bf16[8,2,16,1024]{3,2,1,0:T(8,128)(2,1)S(1)}, u32[]{:S(2)}) copy-start(bf16[8,2,16,1024]{3,2,1,0:T(8,128)(2,1)S(1)} %collective-permute-done.17.refs_1_) | copy-start | bytes 1572868
  197.7 0.8 copy-start.19
  197.7 1.0 copy-start.20
  201.2 13.4 %collective-permute-start.20 = (bf16[4,2,16,1024]{3,2,1,0:T(8,128)(2,1)}, bf16[4,2,16,1024]{3,2,1,0:T(8,128)(2,1)S(1)}, u32[]{:S(2)}, u32[]{:S(2)}) collective-permute-start(bf16[4,2,16,1024]{3,2,1,0:T(8,128)(2,1)} %get-tuple-element.32), channel_id=1, source_target_pairs={{0,8},{8,0},{16,24},{24,16},{32,40},{40,32},{48,56},{56,48},{1,9},... | collective-permute-start | bytes 786440 | tf_op jit(solution)/shard_map/ppermute | solution.py:51
  205.2 12.7 %collective-permute-start.7 = (bf16[2,2,16,1024]{3,2,1,0:T(8,128)(2,1)S(1)}, bf16[2,2,16,1024]{3,2,1,0:T(8,128)(2,1)S(1)}, u32[]{:S(2)}, u32[]{:S(2)}) collective-permute-start(bf16[2,2,16,1024]{3,2,1,0:T(8,128)(2,1)S(1)} %slice_bitcast_fusion.2), channel_id=1, source_target_pairs={{0,16},{8,24},{16,0},{24,8},{32,48},{40,56},{48,32},{56,40},{1,17}... | collective-permute-start | bytes 393224 | tf_op jit(solution)/shard_map/ppermute | solution.py:51
  215.6 44.1 %copy-start.8 = (bf16[8,2,16,1024]{3,2,1,0:T(8,128)(2,1)S(1)}, bf16[8,2,16,1024]{3,2,1,0:T(8,128)(2,1)}, u32[]{:S(2)}) copy-start(bf16[8,2,16,1024]{3,2,1,0:T(8,128)(2,1)} %copy-done.7) | copy-start | bytes 1572868
  215.7 9.0 %collective-permute-start.21 = (bf16[2,2,16,1024]{3,2,1,0:T(8,128)(2,1)S(1)}, bf16[2,2,16,1024]{3,2,1,0:T(8,128)(2,1)S(1)}, u32[]{:S(2)}, u32[]{:S(2)}) collective-permute-start(bf16[2,2,16,1024]{3,2,1,0:T(8,128)(2,1)S(1)} %slice_bitcast_fusion), channel_id=1, source_target_pairs={{0,16},{8,24},{16,0},{24,8},{32,48},{40,56},{48,32},{56,40},{1,17}... | collective-permute-start | bytes 393224 | tf_op jit(solution)/shard_map/ppermute | solution.py:51
  224.8 12.7 %collective-permute-start.22 = (bf16[1,2,16,1024]{3,2,1,0:T(8,128)(2,1)S(1)}, bf16[1,2,16,1024]{3,2,1,0:T(8,128)(2,1)S(1)}, u32[]{:S(2)}, u32[]{:S(2)}) collective-permute-start(bf16[1,2,16,1024]{3,2,1,0:T(8,128)(2,1)S(1)} %slice_bitcast_fusion.4), channel_id=1, source_target_pairs={{0,32},{8,40},{16,48},{24,56},{32,0},{40,8},{48,16},{56,24},{1,33}... | collective-permute-start | bytes 196616 | tf_op jit(solution)/shard_map/ppermute | solution.py:51
  230.9 11.9 %collective-permute-start.8 = (bf16[1,2,16,1024]{3,2,1,0:T(8,128)(2,1)S(1)}, bf16[1,2,16,1024]{3,2,1,0:T(8,128)(2,1)S(1)}, u32[]{:S(2)}, u32[]{:S(2)}) collective-permute-start(bf16[1,2,16,1024]{3,2,1,0:T(8,128)(2,1)S(1)} %slice_bitcast_fusion.6), channel_id=1, source_target_pairs={{0,32},{8,40},{16,48},{24,56},{32,0},{40,8},{48,16},{56,24},{1,33}... | collective-permute-start | bytes 196616 | tf_op jit(solution)/shard_map/ppermute | solution.py:51
  237.5 10.1 %collective-permute-start.23 = (bf16[2,16,1024]{2,1,0:T(8,128)(2,1)S(1)}, bf16[2,16,1024]{2,1,0:T(8,128)(2,1)S(1)}, u32[]{:S(2)}, u32[]{:S(2)}) collective-permute-start(bf16[2,16,1024]{2,1,0:T(8,128)(2,1)S(1)} %fusion.20), channel_id=1, source_target_pairs={{0,96},{8,104},{16,112},{24,120},{32,64},{40,72},{48,80},{56,88},{... | collective-permute-start | bytes 196616 | tf_op jit(solution)/shard_map/ppermute | solution.py:45
  248.5 15.1 %copy-start.1 = (bf16[8,64,768]{2,1,0:T(8,128)(2,1)S(1)}, bf16[8,64,768]{2,1,0:T(8,128)(2,1)}, u32[]{:S(2)}) copy-start(bf16[8,64,768]{2,1,0:T(8,128)(2,1)} %copy-done) | copy-start | bytes 2359300
  248.5 15.1 %copy-start.3 = (bf16[8,64,768]{2,1,0:T(8,128)(2,1)S(1)}, bf16[8,64,768]{2,1,0:T(8,128)(2,1)}, u32[]{:S(2)}) copy-start(bf16[8,64,768]{2,1,0:T(8,128)(2,1)} %copy-done.2) | copy-start | bytes 2359300
  248.5 37.8 %all-to-all-start.4 = ((bf16[8,2,16,1024]{3,2,1,0:T(8,128)(2,1)}), bf16[8,2,16,1024]{3,2,1,0:T(8,128)(2,1)S(1)}, u32[]{:S(2)}, u32[]{:S(2)}) async-start(bf16[8,2,16,1024]{3,2,1,0:T(8,128)(2,1)} %broadcast_in_dim.8), calls=%async_computation.4 | async-start | bytes 1048576 | tf_op jit(solution)/shard_map/all_to_all | solution.py:17
  263.6 3.2 %copy-start.23 = (bf16[1024,1024]{1,0:T(8,128)(2,1)S(1)}, bf16[1024,1024]{1,0:T(8,128)(2,1)}, u32[]{:S(2)}) copy-start(bf16[1024,1024]{1,0:T(8,128)(2,1)} %constant_dynamic-update-slice_fusion) | copy-start | bytes 6291460
  266.8 1.6 copy-start.6

commit v4 on v3

--- a/solution.py
+++ b/solution.py
@@ -90,13 +90,13 @@
         t[rows] = b[:, 0].reshape(n * cut, width)
         g[rows] = b[:, 1].reshape(n * cut, width)
         at += n * cut
-    out[:, : 2 * LANES] = matmul(t[...], wide[...]).astype(jnp.bfloat16)
+    out[:, : 2 * LANES] = contract_cols(t[...], wide[...]).astype(jnp.bfloat16)
     out[:, 2 * LANES :] = contract_cols(g[...], down[...]).astype(jnp.bfloat16)
 
 
 def leave_kernel(acts, wide, down, *outs):
     o = matmul(acts[:, :LANES], down[...]).astype(jnp.bfloat16)
-    i = contract_cols(acts[:, LANES:], wide[...]).astype(jnp.bfloat16)
+    i = matmul(acts[:, LANES:], wide[...]).astype(jnp.bfloat16)
     at = 0
     for out in outs:
         n, _, cut, width = out.shape
@@ -137,7 +137,7 @@
         *(a.reshape(zl, cut, width) for a in (tokens, out_grad)),
     )
     wide = jnp.concatenate(
-        [jnp.pad(w, ((0, 0), (0, more))) for w in (gate_weight, up_weight)], axis=1
+        [jnp.pad(w.T, ((0, more), (0, 0))) for w in (gate_weight, up_weight)], axis=0
     )
     down = jnp.pad(down_weight, ((0, more), (0, 0)))
     far = across(thin)

time: 289 us -> 290 us (level)
  the two profiles are of different devices: /device:TPU:2 before, /device:TPU:26 now
where the time goes in v4:
time: 290 us; the launch traced here: 288 us
  waiting for transfers between devices  115 us (40%)
  starting transfers between devices  114 us (39%)
  local copies, waits for them, and re-layouts  26.5 us (9%)
  Pallas kernels  22.4 us (8%)
  matrix products  6.08 us (2%)
    ppermute x13, starting transfers between devices, to_y(): return lax.ppermute(block, 'y', [(i, (i + d) % n) for i in range(n)])  39.1 us
    ppermute x9, waiting for transfers between devices, to_bit(): lax.ppermute(block, 'zl', [(i, i ^ 1 << bit) for i in range(lax.axis_size...  32.7 us
    ppermute x9, starting transfers between devices, to_bit(): lax.ppermute(block, 'zl', [(i, i ^ 1 << bit) for i in range(lax.axis_size...  32 us
    ppermute x13, waiting for transfers between devices, to_y(): return lax.ppermute(block, 'y', [(i, (i + d) % n) for i in range(n)])  31.3 us
    all_to_all x3, waiting for transfers between devices, give_all(): lax.all_to_all(jnp.broadcast_to(shard[None], (devices, *shard.shape)), ax...  27.6 us
    all_to_all x3, starting transfers between devices, give_all(): lax.all_to_all(jnp.broadcast_to(shard[None], (devices, *shard.shape)), ax...  17 us
    ppermute x2, starting transfers between devices, across(): lax.ppermute(shard, Z, [(i, (i - step if i % zl < step else i + step) % n...  15.9 us
    unnamed x68, local copies, waits for them, and re-layouts  14.7 us
  transfers between devices with their start and end apart: 29, of which 17 were waited for; matrix products, arithmetic and copies ran while one was open for 10% of the time, Pallas kernels for 7%

profile of v4, /device:TPU:26, one launch (start us, length us, event | category | flops | bytes accessed | tf_op | source)
XLA Modules:
  0.0 288.1 jit_solution(18157455396582600437)
XLA Ops:
  0.6 1.9 own.1
  2.5 12.9 %collective-permute-start.9 = (bf16[1,2,16,1024]{3,2,1,0:T(8,128)(2,1)}, bf16[1,2,16,1024]{3,2,1,0:T(8,128)(2,1)S(1)}, u32[]{:S(2)}, u32[]{:S(2)}) collective-permute-start(bf16[1,2,16,1024]{3,2,1,0:T(8,128)(2,1)} %get-tuple-element.26), channel_id=1, source_target_pairs={{0,96},{8,104},{16,112},{24,120},{32,64},{40,72},{48,80},{56,88},{... | collective-permute-start | bytes 196616 | tf_op jit(solution)/shard_map/ppermute | solution.py:45
  15.4 5.9 %collective-permute-done.9 = bf16[1,2,16,1024]{3,2,1,0:T(8,128)(2,1)S(1)} collective-permute-done((bf16[1,2,16,1024]{3,2,1,0:T(8,128)(2,1)}, bf16[1,2,16,1024]{3,2,1,0:T(8,128)(2,1)S(1)}, u32[]{:S(2)}, u32[]{:S(2)}) %collective-permute-start.9) | collective-permute-done | bytes 65568 | tf_op jit(solution)/shard_map/ppermute | solution.py:45
  21.3 6.1 %collective-permute-start.10 = (bf16[1,2,16,1024]{3,2,1,0:T(8,128)(2,1)S(1)}, bf16[1,2,16,1024]{3,2,1,0:T(8,128)(2,1)S(1)}, u32[]{:S(2)}, u32[]{:S(2)}) collective-permute-start(bf16[1,2,16,1024]{3,2,1,0:T(8,128)(2,1)S(1)} %collective-permute-done.9), channel_id=1, source_target_pairs={{0,32},{8,40},{16,48},{24,56},{32,0},{40,8},{48,16},{56,24},{1,33}... | collective-permute-start | bytes 196616 | tf_op jit(solution)/shard_map/ppermute | solution.py:51
  27.3 6.3 %collective-permute-done.10 = bf16[1,2,16,1024]{3,2,1,0:T(8,128)(2,1)S(1)} collective-permute-done((bf16[1,2,16,1024]{3,2,1,0:T(8,128)(2,1)S(1)}, bf16[1,2,16,1024]{3,2,1,0:T(8,128)(2,1)S(1)}, u32[]{:S(2)}, u32[]{:S(2)}) %collective-permute-start.10) | collective-permute-done | bytes 65568 | tf_op jit(solution)/shard_map/ppermute | solution.py:51
  33.6 1.9 collective-permute-start.11
  35.5 5.8 %collective-permute-done.11 = bf16[2,2,16,1024]{3,2,1,0:T(8,128)(2,1)S(1)} collective-permute-done((bf16[2,2,16,1024]{3,2,1,0:T(8,128)(2,1)S(1)}, bf16[2,2,16,1024]{3,2,1,0:T(8,128)(2,1)S(1)}, u32[]{:S(2)}, u32[]{:S(2)}) %collective-permute-start.11) | collective-permute-done | bytes 131104 | tf_op jit(solution)/shard_map/ppermute | solution.py:51
  41.5 2.1 collective-permute-start.12
  43.5 2.7 collective-permute-start
  46.2 2.8 collective-permute-start.1
  49.0 4.1 %collective-permute-start.2 = (bf16[8,2,16,1024]{3,2,1,0:T(8,128)(2,1)}, bf16[8,2,16,1024]{3,2,1,0:T(8,128)(2,1)S(1)}, u32[]{:S(2)}, u32[]{:S(2)}) collective-permute-start(bf16[8,2,16,1024]{3,2,1,0:T(8,128)(2,1)} %get-tuple-element.19.refs_0_), channel_id=1, source_target_pairs={{0,128},{128,256},{256,384},{384,0},{1,129},{129,257},{257,385},{3... | collective-permute-start | bytes 1572872 | tf_op jit(solution)/shard_map/ppermute | solution.py:32
  53.1 1.1 fusion.29
  55.0 2.1 collective-permute-start.13
  59.5 1.1 fusion.2.refs_4_.wide.refs_5_
  60.6 4.1 %collective-permute-start.14 = (bf16[4,2,16,1024]{3,2,1,0:T(8,128)(2,1)S(1)}, bf16[4,2,16,1024]{3,2,1,0:T(8,128)(2,1)}, u32[]{:S(2)}, u32[]{:S(2)}) collective-permute-start(bf16[4,2,16,1024]{3,2,1,0:T(8,128)(2,1)S(1)} %bitcast.100), channel_id=1, source_target_pairs={{0,256},{128,384},{256,0},{384,128},{1,257},{129,385},{257,1},{385... | collective-permute-start | bytes 786440 | tf_op jit(solution)/shard_map/ppermute | solution.py:32
  64.7 6.6 %collective-permute-done.refs_1_ = bf16[8,2,16,1024]{3,2,1,0:T(8,128)(2,1)} collective-permute-done((bf16[8,2,16,1024]{3,2,1,0:T(8,128)(2,1)}, bf16[8,2,16,1024]{3,2,1,0:T(8,128)(2,1)}, u32[]{:S(2)}, u32[]{:S(2)}) %collective-permute-start) | collective-permute-done | bytes 524320 | tf_op jit(solution)/shard_map/ppermute | solution.py:32
  71.4 1.9 collective-permute-start.16
  73.3 2.3 collective-permute-done.2.refs_3_
  76.4 3.9 %terms.2 = bf16[512,768]{1,0:T(8,128)(2,1)} custom-call(bf16[8,2,16,1024]{3,2,1,0:T(8,128)(2,1)} %get-tuple-element.19.refs_0_, bf16[8,2,16,1024]{3,2,1,0:T(8,128)(2,1)} %collective-permute-done.refs_1_, bf16[8,2,16,1024]{3,2,1,0:T(8,128)(2,1)} %copy-done.12, bf16[8,2,16,1024]{3,2,1,0:T(8,128)(2,1)} %copy-done.9, ...), custom_call_target="tpu_custom_call" | custom-call | tf_op jit(solution)/shard_map/terms/pallas_call | solution.py:156
  80.3 5.0 %all-to-all-start = ((bf16[8,64,768]{2,1,0:T(8,128)(2,1)}), bf16[8,64,768]{2,1,0:T(8,128)(2,1)S(1)}, u32[]{:S(2)}, u32[]{:S(2)}) async-start(bf16[8,64,768]{2,1,0:T(8,128)(2,1)} %bitcast.96), calls=%async_computation | async-start | bytes 1572864 | tf_op jit(solution)/shard_map/all_to_all | solution.py:23
  85.3 1.8 fusion.28
  87.1 2.4 collective-permute-start.15
  91.7 6.9 %collective-permute-done.15.refs_3_ = bf16[4,2,16,1024]{3,2,1,0:T(8,128)(2,1)} collective-permute-done((bf16[4,2,16,1024]{3,2,1,0:T(8,128)(2,1)S(1)}, bf16[4,2,16,1024]{3,2,1,0:T(8,128)(2,1)}, u32[]{:S(2)}, u32[]{:S(2)}) %collective-permute-start.15) | collective-permute-done | bytes 262176 | tf_op jit(solution)/shard_map/ppermute | solution.py:32
  98.7 3.9 %terms.3 = bf16[512,768]{1,0:T(8,128)(2,1)} custom-call(bf16[8,2,16,1024]{3,2,1,0:T(8,128)(2,1)} %copy-done.11, bf16[8,2,16,1024]{3,2,1,0:T(8,128)(2,1)} %copy-done.4, bf16[4,2,16,1024]{3,2,1,0:T(8,128)(2,1)} %collective-permute-done.14.refs_2_, bf16[4,2,16,1024]{3,2,1,0:T(8,128)(2,1)} %collective-permute-done.15.refs_3_, ...), custom_call_target="tpu_custom_call" | custom-call | tf_op jit(solution)/shard_map/terms/pallas_call | solution.py:156
  102.6 4.8 %all-to-all-start.2 = ((bf16[8,64,768]{2,1,0:T(8,128)(2,1)}), bf16[8,64,768]{2,1,0:T(8,128)(2,1)S(1)}, u32[]{:S(2)}, u32[]{:S(2)}) async-start(bf16[8,64,768]{2,1,0:T(8,128)(2,1)} %bitcast.97), calls=%async_computation.2 | async-start | bytes 1572864 | tf_op jit(solution)/shard_map/all_to_all | solution.py:23
  107.6 11.4 %all-to-all-done.2 = bf16[8,64,768]{2,1,0:T(8,128)(2,1)S(1)} async-done(((bf16[8,64,768]{2,1,0:T(8,128)(2,1)}), bf16[8,64,768]{2,1,0:T(8,128)(2,1)S(1)}, u32[]{:S(2)}, u32[]{:S(2)}) %all-to-all-start.2) | async-done | bytes 786464 | tf_op jit(solution)/shard_map/all_to_all | solution.py:23
  119.0 1.0 broadcast_in_dim.6
  120.0 4.9 %all-to-all-start.1 = ((bf16[8,64,768]{2,1,0:T(8,128)(2,1)}), bf16[8,64,768]{2,1,0:T(8,128)(2,1)S(1)}, u32[]{:S(2)}, u32[]{:S(2)}) async-start(bf16[8,64,768]{2,1,0:T(8,128)(2,1)} %broadcast_in_dim.6), calls=%async_computation.1 | async-start | bytes 1572864 | tf_op jit(solution)/shard_map/all_to_all | solution.py:17
  125.8 10.8 %all-to-all-done.1 = bf16[8,64,768]{2,1,0:T(8,128)(2,1)S(1)} async-done(((bf16[8,64,768]{2,1,0:T(8,128)(2,1)}), bf16[8,64,768]{2,1,0:T(8,128)(2,1)S(1)}, u32[]{:S(2)}, u32[]{:S(2)}) %all-to-all-start.1) | async-done | bytes 786464 | tf_op jit(solution)/shard_map/all_to_all | solution.py:17
  136.6 1.0 broadcast_in_dim.7
  137.6 5.0 %all-to-all-start.3 = ((bf16[8,64,768]{2,1,0:T(8,128)(2,1)}), bf16[8,64,768]{2,1,0:T(8,128)(2,1)S(1)}, u32[]{:S(2)}, u32[]{:S(2)}) async-start(bf16[8,64,768]{2,1,0:T(8,128)(2,1)} %broadcast_in_dim.7), calls=%async_computation.3 | async-start | bytes 1572864 | tf_op jit(solution)/shard_map/all_to_all | solution.py:17
  143.4 3.8 %leave.2 = (bf16[8,2,16,1024]{3,2,1,0:T(8,128)(2,1)}, bf16[8,2,16,1024]{3,2,1,0:T(8,128)(2,1)}, bf16[8,2,16,1024]{3,2,1,0:T(8,128)(2,1)}, bf16[8,2,16,1024]{3,2,1,0:T(8,128)(2,1)}) custom-call(bf16[512,768]{1,0:T(8,128)(2,1)} %bitcast.88, bf16[512,1024]{1,0:T(8,128)(2,1)} %fusion.2.refs_4_.wide.refs_5_, bf16[256,1024]{1,0:T(8,128)(2,1)} %pad.12.refs_5_.down.refs_6_), custom_call_target="tpu_custom_call" | custom-call | tf_op jit(solution)/shard_map/leave/pallas_call | solution.py:176
  147.2 1.9 collective-permute-start.3
  149.8 3.8 %collective-permute-start.4 = (bf16[8,2,16,1024]{3,2,1,0:T(8,128)(2,1)}, bf16[8,2,16,1024]{3,2,1,0:T(8,128)(2,1)}, u32[]{:S(2)}, u32[]{:S(2)}) collective-permute-start(bf16[8,2,16,1024]{3,2,1,0:T(8,128)(2,1)} %get-tuple-element.22), channel_id=1, source_target_pairs={{0,128},{128,256},{256,384},{384,0},{1,129},{129,257},{257,385},{3... | collective-permute-start | bytes 1572872 | tf_op jit(solution)/shard_map/ppermute | solution.py:32
  153.7 2.0 collective-permute-start.5
  157.1 1.0 fusion.32
  159.0 3.9 %leave.3 = (bf16[8,2,16,1024]{3,2,1,0:T(8,128)(2,1)}, bf16[8,2,16,1024]{3,2,1,0:T(8,128)(2,1)}, bf16[8,2,16,1024]{3,2,1,0:T(8,128)(2,1)}, bf16[8,2,16,1024]{3,2,1,0:T(8,128)(2,1)}) custom-call(bf16[512,768]{1,0:T(8,128)(2,1)} %bitcast.92, bf16[512,1024]{1,0:T(8,128)(2,1)} %fusion.2.refs_4_.wide.refs_5_, bf16[256,1024]{1,0:T(8,128)(2,1)} %pad.12.refs_5_.down.refs_6_), custom_call_target="tpu_custom_call" | custom-call | tf_op jit(solution)/shard_map/leave/pallas_call | solution.py:176
  163.0 5.4 %collective-permute-start.17 = (bf16[8,2,16,1024]{3,2,1,0:T(8,128)(2,1)}, bf16[8,2,16,1024]{3,2,1,0:T(8,128)(2,1)S(1)}, u32[]{:S(2)}, u32[]{:S(2)}) collective-permute-start(bf16[8,2,16,1024]{3,2,1,0:T(8,128)(2,1)} %get-tuple-element.28), channel_id=1, source_target_pairs={{0,256},{128,384},{256,0},{384,128},{1,257},{129,385},{257,1},{385... | collective-permute-start | bytes 1572872 | tf_op jit(solution)/shard_map/ppermute | solution.py:32
  168.4 2.5 collective-permute-start.18
  170.9 3.3 %collective-permute-start.19 = (bf16[8,2,16,1024]{3,2,1,0:T(8,128)(2,1)}, bf16[8,2,16,1024]{3,2,1,0:T(8,128)(2,1)S(1)}, u32[]{:S(2)}, u32[]{:S(2)}) collective-permute-start(bf16[8,2,16,1024]{3,2,1,0:T(8,128)(2,1)} %get-tuple-element.30), channel_id=1, source_target_pairs={{0,384},{128,0},{256,128},{384,256},{1,385},{129,1},{257,129},{385... | collective-permute-start | bytes 1572872 | tf_op jit(solution)/shard_map/ppermute | solution.py:32
  175.0 2.1 collective-permute-done.5.refs_3_
  177.0 2.5 add.95
  179.5 4.0 %collective-permute-start.6 = (bf16[4,2,16,1024]{3,2,1,0:T(8,128)(2,1)}, bf16[4,2,16,1024]{3,2,1,0:T(8,128)(2,1)S(1)}, u32[]{:S(2)}, u32[]{:S(2)}) collective-permute-start(bf16[4,2,16,1024]{3,2,1,0:T(8,128)(2,1)} %get-tuple-element.25), channel_id=1, source_target_pairs={{0,8},{8,0},{16,24},{24,16},{32,40},{40,32},{48,56},{56,48},{1,9},... | collective-permute-start | bytes 786440 | tf_op jit(solution)/shard_map/ppermute | solution.py:51
  185.1 3.1 %collective-permute-done.17.refs_1_ = bf16[8,2,16,1024]{3,2,1,0:T(8,128)(2,1)S(1)} collective-permute-done((bf16[8,2,16,1024]{3,2,1,0:T(8,128)(2,1)}, bf16[8,2,16,1024]{3,2,1,0:T(8,128)(2,1)S(1)}, u32[]{:S(2)}, u32[]{:S(2)}) %collective-permute-start.17) | collective-permute-done | bytes 524320 | tf_op jit(solution)/shard_map/ppermute | solution.py:32
  188.1 7.5 %collective-permute-done.18.refs_2_ = bf16[8,2,16,1024]{3,2,1,0:T(8,128)(2,1)S(1)} collective-permute-done((bf16[8,2,16,1024]{3,2,1,0:T(8,128)(2,1)}, bf16[8,2,16,1024]{3,2,1,0:T(8,128)(2,1)S(1)}, u32[]{:S(2)}, u32[]{:S(2)}) %collective-permute-start.18) | collective-permute-done | bytes 524320 | tf_op jit(solution)/shard_map/ppermute | solution.py:32
  195.6 2.8 collective-permute-done.19.refs_3_
  199.3 2.5 add.96
  201.7 3.9 %collective-permute-start.20 = (bf16[4,2,16,1024]{3,2,1,0:T(8,128)(2,1)}, bf16[4,2,16,1024]{3,2,1,0:T(8,128)(2,1)S(1)}, u32[]{:S(2)}, u32[]{:S(2)}) collective-permute-start(bf16[4,2,16,1024]{3,2,1,0:T(8,128)(2,1)} %get-tuple-element.32), channel_id=1, source_target_pairs={{0,8},{8,0},{16,24},{24,16},{32,40},{40,32},{48,56},{56,48},{1,9},... | collective-permute-start | bytes 786440 | tf_op jit(solution)/shard_map/ppermute | solution.py:51
  205.8 2.1 collective-permute-start.7
  207.9 7.2 %collective-permute-done.20 = bf16[4,2,16,1024]{3,2,1,0:T(8,128)(2,1)S(1)} collective-permute-done((bf16[4,2,16,1024]{3,2,1,0:T(8,128)(2,1)}, bf16[4,2,16,1024]{3,2,1,0:T(8,128)(2,1)S(1)}, u32[]{:S(2)}, u32[]{:S(2)}) %collective-permute-start.20) | collective-permute-done | bytes 262176 | tf_op jit(solution)/shard_map/ppermute | solution.py:51
  215.1 1.0 add_convert_fusion
  216.2 2.2 collective-permute-start.21
  218.4 7.3 %collective-permute-done.21 = bf16[2,2,16,1024]{3,2,1,0:T(8,128)(2,1)S(1)} collective-permute-done((bf16[2,2,16,1024]{3,2,1,0:T(8,128)(2,1)S(1)}, bf16[2,2,16,1024]{3,2,1,0:T(8,128)(2,1)S(1)}, u32[]{:S(2)}, u32[]{:S(2)}) %collective-permute-start.21) | collective-permute-done | bytes 131104 | tf_op jit(solution)/shard_map/ppermute | solution.py:51
  225.8 5.3 %collective-permute-start.22 = (bf16[1,2,16,1024]{3,2,1,0:T(8,128)(2,1)S(1)}, bf16[1,2,16,1024]{3,2,1,0:T(8,128)(2,1)S(1)}, u32[]{:S(2)}, u32[]{:S(2)}) collective-permute-start(bf16[1,2,16,1024]{3,2,1,0:T(8,128)(2,1)S(1)} %slice_bitcast_fusion.4), channel_id=1, source_target_pairs={{0,32},{8,40},{16,48},{24,56},{32,0},{40,8},{48,16},{56,24},{1,33}... | collective-permute-start | bytes 196616 | tf_op jit(solution)/shard_map/ppermute | solution.py:51
  231.1 4.4 %collective-permute-start.8 = (bf16[1,2,16,1024]{3,2,1,0:T(8,128)(2,1)S(1)}, bf16[1,2,16,1024]{3,2,1,0:T(8,128)(2,1)S(1)}, u32[]{:S(2)}, u32[]{:S(2)}) collective-permute-start(bf16[1,2,16,1024]{3,2,1,0:T(8,128)(2,1)S(1)} %slice_bitcast_fusion.6), channel_id=1, source_target_pairs={{0,32},{8,40},{16,48},{24,56},{32,0},{40,8},{48,16},{56,24},{1,33}... | collective-permute-start | bytes 196616 | tf_op jit(solution)/shard_map/ppermute | solution.py:51
  235.6 6.1 %collective-permute-done.22 = bf16[1,2,16,1024]{3,2,1,0:T(8,128)(2,1)S(1)} collective-permute-done((bf16[1,2,16,1024]{3,2,1,0:T(8,128)(2,1)S(1)}, bf16[1,2,16,1024]{3,2,1,0:T(8,128)(2,1)S(1)}, u32[]{:S(2)}, u32[]{:S(2)}) %collective-permute-start.22) | collective-permute-done | bytes 65568 | tf_op jit(solution)/shard_map/ppermute | solution.py:51
  241.7 3.0 %collective-permute-start.23 = (bf16[2,16,1024]{2,1,0:T(8,128)(2,1)S(1)}, bf16[2,16,1024]{2,1,0:T(8,128)(2,1)S(1)}, u32[]{:S(2)}, u32[]{:S(2)}) collective-permute-start(bf16[2,16,1024]{2,1,0:T(8,128)(2,1)S(1)} %fusion.20), channel_id=1, source_target_pairs={{0,96},{8,104},{16,112},{24,120},{32,64},{40,72},{48,80},{56,88},{... | collective-permute-start | bytes 196616 | tf_op jit(solution)/shard_map/ppermute | solution.py:45
  245.4 6.3 %collective-permute-done.23 = bf16[2,16,1024]{2,1,0:T(8,128)(2,1)S(1)} collective-permute-done((bf16[2,16,1024]{2,1,0:T(8,128)(2,1)S(1)}, bf16[2,16,1024]{2,1,0:T(8,128)(2,1)S(1)}, u32[]{:S(2)}, u32[]{:S(2)}) %collective-permute-start.23) | collective-permute-done | bytes 65568 | tf_op jit(solution)/shard_map/ppermute | solution.py:45
  252.7 7.0 %all-to-all-start.4 = ((bf16[8,2,16,1024]{3,2,1,0:T(8,128)(2,1)}), bf16[8,2,16,1024]{3,2,1,0:T(8,128)(2,1)S(1)}, u32[]{:S(2)}, u32[]{:S(2)}) async-start(bf16[8,2,16,1024]{3,2,1,0:T(8,128)(2,1)} %broadcast_in_dim.8), calls=%async_computation.4 | async-start | bytes 1048576 | tf_op jit(solution)/shard_map/all_to_all | solution.py:17
  260.4 1.0 fusion.31
  264.2 3.2 %convolution_convert_fusion.2 = bf16[1024,224]{0,1:T(8,128)(2,1)} fusion(bf16[1024,1024]{1,0:T(8,128)(2,1)} %constant_dynamic-update-slice_fusion, bf16[512,768]{1,0:T(8,128)(2,1)S(1)} %bitcast.89, bf16[512,768]{1,0:T(8,128)(2,1)S(1)} %bitcast.93), kind=kOutput, calls=%fused_computation.12 | convolution fusion | flops 470908928 | bytes 4128768 | tf_op jit(solution)/shard_map/dot_general | solution.py:60
  267.4 1.5 convolution_convert_fusion.1
  269.0 1.4 convolution_convert_fusion
  270.4 16.9 %all-to-all-done.4 = bf16[8,2,16,1024]{3,2,1,0:T(8,128)(2,1)S(1)} async-done(((bf16[8,2,16,1024]{3,2,1,0:T(8,128)(2,1)}), bf16[8,2,16,1024]{3,2,1,0:T(8,128)(2,1)S(1)}, u32[]{:S(2)}, u32[]{:S(2)}) %all-to-all-start.4) | async-done | bytes 524320 | tf_op jit(solution)/shard_map/all_to_all | solution.py:17
  (110 shorter events, 20.4 us)
Async XLA Ops:
  2.5 55.4 %copy-start.21 = (bf16[224,1024]{1,0:T(8,128)(2,1)S(1)}, bf16[224,1024]{1,0:T(8,128)(2,1)}, u32[]{:S(2)}) copy-start(bf16[224,1024]{1,0:T(8,128)(2,1)} %param.8) | copy-start | bytes 1376260
  2.5 18.8 %collective-permute-start.9 = (bf16[1,2,16,1024]{3,2,1,0:T(8,128)(2,1)}, bf16[1,2,16,1024]{3,2,1,0:T(8,128)(2,1)S(1)}, u32[]{:S(2)}, u32[]{:S(2)}) collective-permute-start(bf16[1,2,16,1024]{3,2,1,0:T(8,128)(2,1)} %get-tuple-element.26), channel_id=1, source_target_pairs={{0,96},{8,104},{16,112},{24,120},{32,64},{40,72},{48,80},{56,88},{... | collective-permute-start | bytes 196616 | tf_op jit(solution)/shard_map/ppermute | solution.py:45
  21.3 12.3 %collective-permute-start.10 = (bf16[1,2,16,1024]{3,2,1,0:T(8,128)(2,1)S(1)}, bf16[1,2,16,1024]{3,2,1,0:T(8,128)(2,1)S(1)}, u32[]{:S(2)}, u32[]{:S(2)}) collective-permute-start(bf16[1,2,16,1024]{3,2,1,0:T(8,128)(2,1)S(1)} %collective-permute-done.9), channel_id=1, source_target_pairs={{0,32},{8,40},{16,48},{24,56},{32,0},{40,8},{48,16},{56,24},{1,33}... | collective-permute-start | bytes 196616 | tf_op jit(solution)/shard_map/ppermute | solution.py:51
  33.6 7.8 %collective-permute-start.11 = (bf16[2,2,16,1024]{3,2,1,0:T(8,128)(2,1)S(1)}, bf16[2,2,16,1024]{3,2,1,0:T(8,128)(2,1)S(1)}, u32[]{:S(2)}, u32[]{:S(2)}) collective-permute-start(bf16[2,2,16,1024]{3,2,1,0:T(8,128)(2,1)S(1)} %get-tuple-element.60), channel_id=1, source_target_pairs={{0,16},{8,24},{16,0},{24,8},{32,48},{40,56},{48,32},{56,40},{1,17}... | collective-permute-start | bytes 393224 | tf_op jit(solution)/shard_map/ppermute | solution.py:51
  41.4 18.1 %copy-start.22 = (bf16[1024,224]{0,1:T(8,128)(2,1)S(1)}, bf16[1024,224]{0,1:T(8,128)(2,1)}, u32[]{:S(2)}) copy-start(bf16[1024,224]{0,1:T(8,128)(2,1)} %param.7) | copy-start | bytes 1376260
  41.4 18.1 %copy-start.23 = (bf16[1024,224]{0,1:T(8,128)(2,1)S(1)}, bf16[1024,224]{0,1:T(8,128)(2,1)}, u32[]{:S(2)}) copy-start(bf16[1024,224]{0,1:T(8,128)(2,1)} %param.6) | copy-start | bytes 1376260
  41.5 12.8 %collective-permute-start.12 = (bf16[4,2,16,1024]{3,2,1,0:T(8,128)(2,1)S(1)}, bf16[4,2,16,1024]{3,2,1,0:T(8,128)(2,1)S(1)}, u32[]{:S(2)}, u32[]{:S(2)}) collective-permute-start(bf16[4,2,16,1024]{3,2,1,0:T(8,128)(2,1)S(1)} %bitcast.98), channel_id=1, source_target_pairs={{0,8},{8,0},{16,24},{24,16},{32,40},{40,32},{48,56},{56,48},{1,9},... | collective-permute-start | bytes 786440 | tf_op jit(solution)/shard_map/ppermute | solution.py:51
  43.5 27.8 %collective-permute-start = (bf16[8,2,16,1024]{3,2,1,0:T(8,128)(2,1)}, bf16[8,2,16,1024]{3,2,1,0:T(8,128)(2,1)}, u32[]{:S(2)}, u32[]{:S(2)}) collective-permute-start(bf16[8,2,16,1024]{3,2,1,0:T(8,128)(2,1)} %get-tuple-element.19.refs_0_), channel_id=1, source_target_pairs={{0,384},{128,0},{256,128},{384,256},{1,385},{129,1},{257,129},{385... | collective-permute-start | bytes 1572872 | tf_op jit(solution)/shard_map/ppermute | solution.py:32
  46.2 27.1 %collective-permute-start.1 = (bf16[8,2,16,1024]{3,2,1,0:T(8,128)(2,1)}, bf16[8,2,16,1024]{3,2,1,0:T(8,128)(2,1)S(1)}, u32[]{:S(2)}, u32[]{:S(2)}) collective-permute-start(bf16[8,2,16,1024]{3,2,1,0:T(8,128)(2,1)} %get-tuple-element.19.refs_0_), channel_id=1, source_target_pairs={{0,256},{128,384},{256,0},{384,128},{1,257},{129,385},{257,1},{385... | collective-permute-start | bytes 1572872 | tf_op jit(solution)/shard_map/ppermute | solution.py:32
  49.0 26.6 %collective-permute-start.2 = (bf16[8,2,16,1024]{3,2,1,0:T(8,128)(2,1)}, bf16[8,2,16,1024]{3,2,1,0:T(8,128)(2,1)S(1)}, u32[]{:S(2)}, u32[]{:S(2)}) collective-permute-start(bf16[8,2,16,1024]{3,2,1,0:T(8,128)(2,1)} %get-tuple-element.19.refs_0_), channel_id=1, source_target_pairs={{0,128},{128,256},{256,384},{384,0},{1,129},{129,257},{257,385},{3... | collective-permute-start | bytes 1572872 | tf_op jit(solution)/shard_map/ppermute | solution.py:32
  54.2 0.7 copy-start.16
  55.0 25.4 %copy-start.11 = (bf16[8,2,16,1024]{3,2,1,0:T(8,128)(2,1)}, bf16[8,2,16,1024]{3,2,1,0:T(8,128)(2,1)S(1)}, u32[]{:S(2)}) copy-start(bf16[8,2,16,1024]{3,2,1,0:T(8,128)(2,1)S(1)} %pad_maximum_fusion.refs_0_) | copy-start | bytes 1572868
  55.0 32.1 %collective-permute-start.13 = (bf16[8,2,16,1024]{3,2,1,0:T(8,128)(2,1)S(1)}, bf16[8,2,16,1024]{3,2,1,0:T(8,128)(2,1)S(1)}, u32[]{:S(2)}, u32[]{:S(2)}) collective-permute-start(bf16[8,2,16,1024]{3,2,1,0:T(8,128)(2,1)S(1)} %pad_maximum_fusion.refs_0_), channel_id=1, source_target_pairs={{0,384},{128,0},{256,128},{384,256},{1,385},{129,1},{257,129},{385... | collective-permute-start | bytes 1572872 | tf_op jit(solution)/shard_map/ppermute | solution.py:32
  60.6 31.1 %collective-permute-start.14 = (bf16[4,2,16,1024]{3,2,1,0:T(8,128)(2,1)S(1)}, bf16[4,2,16,1024]{3,2,1,0:T(8,128)(2,1)}, u32[]{:S(2)}, u32[]{:S(2)}) collective-permute-start(bf16[4,2,16,1024]{3,2,1,0:T(8,128)(2,1)S(1)} %bitcast.100), channel_id=1, source_target_pairs={{0,256},{128,384},{256,0},{384,128},{1,257},{129,385},{257,1},{385... | collective-permute-start | bytes 786440 | tf_op jit(solution)/shard_map/ppermute | solution.py:32
  71.4 20.4 %collective-permute-start.16 = (bf16[8,2,16,1024]{3,2,1,0:T(8,128)(2,1)S(1)}, bf16[8,2,16,1024]{3,2,1,0:T(8,128)(2,1)S(1)}, u32[]{:S(2)}, u32[]{:S(2)}) collective-permute-start(bf16[8,2,16,1024]{3,2,1,0:T(8,128)(2,1)S(1)} %pad_maximum_fusion.refs_0_), channel_id=1, source_target_pairs={{0,128},{128,256},{256,384},{384,0},{1,129},{129,257},{257,385},{3... | collective-permute-start | bytes 1572872 | tf_op jit(solution)/shard_map/ppermute | solution.py:32
  73.3 2.4 copy-start.12
  75.6 0.8 copy-start.9
  80.3 9.2 %copy-start.13 = (bf16[8,2,16,1024]{3,2,1,0:T(8,128)(2,1)S(1)}, bf16[8,2,16,1024]{3,2,1,0:T(8,128)(2,1)}, u32[]{:S(2)}) copy-start(bf16[8,2,16,1024]{3,2,1,0:T(8,128)(2,1)} %copy-done.12) | copy-start | bytes 1572868
  80.3 22.2 %all-to-all-start = ((bf16[8,64,768]{2,1,0:T(8,128)(2,1)}), bf16[8,64,768]{2,1,0:T(8,128)(2,1)S(1)}, u32[]{:S(2)}, u32[]{:S(2)}) async-start(bf16[8,64,768]{2,1,0:T(8,128)(2,1)} %bitcast.96), calls=%async_computation | async-start | bytes 1572864 | tf_op jit(solution)/shard_map/all_to_all | solution.py:23
  87.1 11.6 %copy-start.4 = (bf16[8,2,16,1024]{3,2,1,0:T(8,128)(2,1)}, bf16[8,2,16,1024]{3,2,1,0:T(8,128)(2,1)S(1)}, u32[]{:S(2)}) copy-start(bf16[8,2,16,1024]{3,2,1,0:T(8,128)(2,1)S(1)} %collective-permute-done.13.refs_1_) | copy-start | bytes 1572868
  87.1 11.5 %collective-permute-start.15 = (bf16[4,2,16,1024]{3,2,1,0:T(8,128)(2,1)S(1)}, bf16[4,2,16,1024]{3,2,1,0:T(8,128)(2,1)}, u32[]{:S(2)}, u32[]{:S(2)}) collective-permute-start(bf16[4,2,16,1024]{3,2,1,0:T(8,128)(2,1)S(1)} %slice.159), channel_id=1, source_target_pairs={{0,384},{128,0},{256,128},{384,256},{1,385},{129,1},{257,129},{385... | collective-permute-start | bytes 786440 | tf_op jit(solution)/shard_map/ppermute | solution.py:32
  91.7 15.7 %copy-start.10 = (bf16[8,2,16,1024]{3,2,1,0:T(8,128)(2,1)S(1)}, bf16[8,2,16,1024]{3,2,1,0:T(8,128)(2,1)}, u32[]{:S(2)}) copy-start(bf16[8,2,16,1024]{3,2,1,0:T(8,128)(2,1)} %copy-done.9) | copy-start | bytes 1572868
  91.7 6.9 %copy-start.7 = (bf16[8,2,16,1024]{3,2,1,0:T(8,128)(2,1)}, bf16[8,2,16,1024]{3,2,1,0:T(8,128)(2,1)S(1)}, u32[]{:S(2)}) copy-start(bf16[8,2,16,1024]{3,2,1,0:T(8,128)(2,1)S(1)} %collective-permute-done.16.refs_4_) | copy-start | bytes 1572868
  102.6 16.5 %all-to-all-start.2 = ((bf16[8,64,768]{2,1,0:T(8,128)(2,1)}), bf16[8,64,768]{2,1,0:T(8,128)(2,1)S(1)}, u32[]{:S(2)}, u32[]{:S(2)}) async-start(bf16[8,64,768]{2,1,0:T(8,128)(2,1)} %bitcast.97), calls=%async_computation.2 | async-start | bytes 1572864 | tf_op jit(solution)/shard_map/all_to_all | solution.py:23
  107.4 18.2 %copy-start.17 = (bf16[4,2,16,1024]{3,2,1,0:T(8,128)(2,1)S(1)}, bf16[4,2,16,1024]{3,2,1,0:T(8,128)(2,1)}, u32[]{:S(2)}) copy-start(bf16[4,2,16,1024]{3,2,1,0:T(8,128)(2,1)} %copy-done.16) | copy-start | bytes 786436
  120.0 16.6 %all-to-all-start.1 = ((bf16[8,64,768]{2,1,0:T(8,128)(2,1)}), bf16[8,64,768]{2,1,0:T(8,128)(2,1)S(1)}, u32[]{:S(2)}, u32[]{:S(2)}) async-start(bf16[8,64,768]{2,1,0:T(8,128)(2,1)} %broadcast_in_dim.6), calls=%async_computation.1 | async-start | bytes 1572864 | tf_op jit(solution)/shard_map/all_to_all | solution.py:17
  136.6 6.8 %copy-start = (bf16[8,64,768]{2,1,0:T(8,128)(2,1)}, bf16[8,64,768]{2,1,0:T(8,128)(2,1)S(1)}, u32[]{:S(2)}) copy-start(bf16[8,64,768]{2,1,0:T(8,128)(2,1)S(1)} %all-to-all-done.1) | copy-start | bytes 2359300
  137.6 11.5 %copy-start.14 = (bf16[8,1,16,1024]{3,2,1,0:T(8,128)(2,1)S(1)}, bf16[8,1,16,1024]{3,2,1,0:T(8,128)(2,1)}, u32[]{:S(2)}) copy-start(bf16[8,1,16,1024]{3,2,1,0:T(8,128)(2,1)} %get-tuple-element.43) | copy-start | bytes 786436
  137.6 20.5 %all-to-all-start.3 = ((bf16[8,64,768]{2,1,0:T(8,128)(2,1)}), bf16[8,64,768]{2,1,0:T(8,128)(2,1)S(1)}, u32[]{:S(2)}, u32[]{:S(2)}) async-start(bf16[8,64,768]{2,1,0:T(8,128)(2,1)} %broadcast_in_dim.7), calls=%async_computation.3 | async-start | bytes 1572864 | tf_op jit(solution)/shard_map/all_to_all | solution.py:17
  142.7 13.0 %copy-start.15 = (bf16[8,1,16,1024]{3,2,1,0:T(8,128)(2,1)S(1)}, bf16[8,1,16,1024]{3,2,1,0:T(8,128)(2,1)}, u32[]{:S(2)}) copy-start(bf16[8,1,16,1024]{3,2,1,0:T(8,128)(2,1)} %get-tuple-element.41) | copy-start | bytes 786436
  147.2 23.7 %collective-permute-start.3 = (bf16[8,2,16,1024]{3,2,1,0:T(8,128)(2,1)}, bf16[8,2,16,1024]{3,2,1,0:T(8,128)(2,1)}, u32[]{:S(2)}, u32[]{:S(2)}) collective-permute-start(bf16[8,2,16,1024]{3,2,1,0:T(8,128)(2,1)} %get-tuple-element.21), channel_id=1, source_target_pairs={{0,256},{128,384},{256,0},{384,128},{1,257},{129,385},{257,1},{385... | collective-permute-start | bytes 1572872 | tf_op jit(solution)/shard_map/ppermute | solution.py:32
  149.8 25.1 %collective-permute-start.4 = (bf16[8,2,16,1024]{3,2,1,0:T(8,128)(2,1)}, bf16[8,2,16,1024]{3,2,1,0:T(8,128)(2,1)}, u32[]{:S(2)}, u32[]{:S(2)}) collective-permute-start(bf16[8,2,16,1024]{3,2,1,0:T(8,128)(2,1)} %get-tuple-element.22), channel_id=1, source_target_pairs={{0,128},{128,256},{256,384},{384,0},{1,129},{129,257},{257,385},{3... | collective-permute-start | bytes 1572872 | tf_op jit(solution)/shard_map/ppermute | solution.py:32
  153.7 23.4 %collective-permute-start.5 = (bf16[8,2,16,1024]{3,2,1,0:T(8,128)(2,1)}, bf16[8,2,16,1024]{3,2,1,0:T(8,128)(2,1)}, u32[]{:S(2)}, u32[]{:S(2)}) collective-permute-start(bf16[8,2,16,1024]{3,2,1,0:T(8,128)(2,1)} %get-tuple-element.23), channel_id=1, source_target_pairs={{0,384},{128,0},{256,128},{384,256},{1,385},{129,1},{257,129},{385... | collective-permute-start | bytes 1572872 | tf_op jit(solution)/shard_map/ppermute | solution.py:32
  158.1 0.9 copy-start.2
  159.0 24.5 %copy-start.5 = (bf16[8,2,16,1024]{3,2,1,0:T(8,128)(2,1)S(1)}, bf16[8,2,16,1024]{3,2,1,0:T(8,128)(2,1)}, u32[]{:S(2)}) copy-start(bf16[8,2,16,1024]{3,2,1,0:T(8,128)(2,1)} %copy-done.4) | copy-start | bytes 1572868
  163.0 25.2 %collective-permute-start.17 = (bf16[8,2,16,1024]{3,2,1,0:T(8,128)(2,1)}, bf16[8,2,16,1024]{3,2,1,0:T(8,128)(2,1)S(1)}, u32[]{:S(2)}, u32[]{:S(2)}) collective-permute-start(bf16[8,2,16,1024]{3,2,1,0:T(8,128)(2,1)} %get-tuple-element.28), channel_id=1, source_target_pairs={{0,256},{128,384},{256,0},{384,128},{1,257},{129,385},{257,1},{385... | collective-permute-start | bytes 1572872 | tf_op jit(solution)/shard_map/ppermute | solution.py:32
  168.4 27.3 %collective-permute-start.18 = (bf16[8,2,16,1024]{3,2,1,0:T(8,128)(2,1)}, bf16[8,2,16,1024]{3,2,1,0:T(8,128)(2,1)S(1)}, u32[]{:S(2)}, u32[]{:S(2)}) collective-permute-start(bf16[8,2,16,1024]{3,2,1,0:T(8,128)(2,1)} %get-tuple-element.29), channel_id=1, source_target_pairs={{0,128},{128,256},{256,384},{384,0},{1,129},{129,257},{257,385},{3... | collective-permute-start | bytes 1572872 | tf_op jit(solution)/shard_map/ppermute | solution.py:32
  170.9 27.5 %collective-permute-start.19 = (bf16[8,2,16,1024]{3,2,1,0:T(8,128)(2,1)}, bf16[8,2,16,1024]{3,2,1,0:T(8,128)(2,1)S(1)}, u32[]{:S(2)}, u32[]{:S(2)}) collective-permute-start(bf16[8,2,16,1024]{3,2,1,0:T(8,128)(2,1)} %get-tuple-element.30), channel_id=1, source_target_pairs={{0,384},{128,0},{256,128},{384,256},{1,385},{129,1},{257,129},{385... | collective-permute-start | bytes 1572872 | tf_op jit(solution)/shard_map/ppermute | solution.py:32
  179.5 26.2 %copy-start.24 = (bf16[4,2,16,1024]{3,2,1,0:T(8,128)(2,1)S(1)}, bf16[4,2,16,1024]{3,2,1,0:T(8,128)(2,1)}, u32[]{:S(2)}) copy-start(bf16[4,2,16,1024]{3,2,1,0:T(8,128)(2,1)} %get-tuple-element.24) | copy-start | bytes 786436
  179.5 26.2 %collective-permute-start.6 = (bf16[4,2,16,1024]{3,2,1,0:T(8,128)(2,1)}, bf16[4,2,16,1024]{3,2,1,0:T(8,128)(2,1)S(1)}, u32[]{:S(2)}, u32[]{:S(2)}) collective-permute-start(bf16[4,2,16,1024]{3,2,1,0:T(8,128)(2,1)} %get-tuple-element.25), channel_id=1, source_target_pairs={{0,8},{8,0},{16,24},{24,16},{32,40},{40,32},{48,56},{56,48},{1,9},... | collective-permute-start | bytes 786440 | tf_op jit(solution)/shard_map/ppermute | solution.py:51
  188.1 10.3 %copy-start.18 = (bf16[8,2,16,1024]{3,2,1,0:T(8,128)(2,1)}, bf16[8,2,16,1024]{3,2,1,0:T(8,128)(2,1)S(1)}, u32[]{:S(2)}) copy-start(bf16[8,2,16,1024]{3,2,1,0:T(8,128)(2,1)S(1)} %collective-permute-done.17.refs_1_) | copy-start | bytes 1572868
  195.6 2.8 copy-start.19
  198.4 0.8 copy-start.20
  201.7 13.4 %collective-permute-start.20 = (bf16[4,2,16,1024]{3,2,1,0:T(8,128)(2,1)}, bf16[4,2,16,1024]{3,2,1,0:T(8,128)(2,1)S(1)}, u32[]{:S(2)}, u32[]{:S(2)}) collective-permute-start(bf16[4,2,16,1024]{3,2,1,0:T(8,128)(2,1)} %get-tuple-element.32), channel_id=1, source_target_pairs={{0,8},{8,0},{16,24},{24,16},{32,40},{40,32},{48,56},{56,48},{1,9},... | collective-permute-start | bytes 786440 | tf_op jit(solution)/shard_map/ppermute | solution.py:51
  205.8 12.6 %collective-permute-start.7 = (bf16[2,2,16,1024]{3,2,1,0:T(8,128)(2,1)S(1)}, bf16[2,2,16,1024]{3,2,1,0:T(8,128)(2,1)S(1)}, u32[]{:S(2)}, u32[]{:S(2)}) collective-permute-start(bf16[2,2,16,1024]{3,2,1,0:T(8,128)(2,1)S(1)} %slice_bitcast_fusion.2), channel_id=1, source_target_pairs={{0,16},{8,24},{16,0},{24,8},{32,48},{40,56},{48,32},{56,40},{1,17}... | collective-permute-start | bytes 393224 | tf_op jit(solution)/shard_map/ppermute | solution.py:51
  216.1 44.2 %copy-start.8 = (bf16[8,2,16,1024]{3,2,1,0:T(8,128)(2,1)S(1)}, bf16[8,2,16,1024]{3,2,1,0:T(8,128)(2,1)}, u32[]{:S(2)}) copy-start(bf16[8,2,16,1024]{3,2,1,0:T(8,128)(2,1)} %copy-done.7) | copy-start | bytes 1572868
  216.2 9.6 %collective-permute-start.21 = (bf16[2,2,16,1024]{3,2,1,0:T(8,128)(2,1)S(1)}, bf16[2,2,16,1024]{3,2,1,0:T(8,128)(2,1)S(1)}, u32[]{:S(2)}, u32[]{:S(2)}) collective-permute-start(bf16[2,2,16,1024]{3,2,1,0:T(8,128)(2,1)S(1)} %slice_bitcast_fusion), channel_id=1, source_target_pairs={{0,16},{8,24},{16,0},{24,8},{32,48},{40,56},{48,32},{56,40},{1,17}... | collective-permute-start | bytes 393224 | tf_op jit(solution)/shard_map/ppermute | solution.py:51
  225.8 15.9 %collective-permute-start.22 = (bf16[1,2,16,1024]{3,2,1,0:T(8,128)(2,1)S(1)}, bf16[1,2,16,1024]{3,2,1,0:T(8,128)(2,1)S(1)}, u32[]{:S(2)}, u32[]{:S(2)}) collective-permute-start(bf16[1,2,16,1024]{3,2,1,0:T(8,128)(2,1)S(1)} %slice_bitcast_fusion.4), channel_id=1, source_target_pairs={{0,32},{8,40},{16,48},{24,56},{32,0},{40,8},{48,16},{56,24},{1,33}... | collective-permute-start | bytes 196616 | tf_op jit(solution)/shard_map/ppermute | solution.py:51
  231.1 14.3 %collective-permute-start.8 = (bf16[1,2,16,1024]{3,2,1,0:T(8,128)(2,1)S(1)}, bf16[1,2,16,1024]{3,2,1,0:T(8,128)(2,1)S(1)}, u32[]{:S(2)}, u32[]{:S(2)}) collective-permute-start(bf16[1,2,16,1024]{3,2,1,0:T(8,128)(2,1)S(1)} %slice_bitcast_fusion.6), channel_id=1, source_target_pairs={{0,32},{8,40},{16,48},{24,56},{32,0},{40,8},{48,16},{56,24},{1,33}... | collective-permute-start | bytes 196616 | tf_op jit(solution)/shard_map/ppermute | solution.py:51
  241.7 10.1 %collective-permute-start.23 = (bf16[2,16,1024]{2,1,0:T(8,128)(2,1)S(1)}, bf16[2,16,1024]{2,1,0:T(8,128)(2,1)S(1)}, u32[]{:S(2)}, u32[]{:S(2)}) collective-permute-start(bf16[2,16,1024]{2,1,0:T(8,128)(2,1)S(1)} %fusion.20), channel_id=1, source_target_pairs={{0,96},{8,104},{16,112},{24,120},{32,64},{40,72},{48,80},{56,88},{... | collective-permute-start | bytes 196616 | tf_op jit(solution)/shard_map/ppermute | solution.py:45
  252.7 11.5 %copy-start.1 = (bf16[8,64,768]{2,1,0:T(8,128)(2,1)S(1)}, bf16[8,64,768]{2,1,0:T(8,128)(2,1)}, u32[]{:S(2)}) copy-start(bf16[8,64,768]{2,1,0:T(8,128)(2,1)} %copy-done) | copy-start | bytes 2359300
  252.7 11.5 %copy-start.3 = (bf16[8,64,768]{2,1,0:T(8,128)(2,1)S(1)}, bf16[8,64,768]{2,1,0:T(8,128)(2,1)}, u32[]{:S(2)}) copy-start(bf16[8,64,768]{2,1,0:T(8,128)(2,1)} %copy-done.2) | copy-start | bytes 2359300
  252.7 34.6 %all-to-all-start.4 = ((bf16[8,2,16,1024]{3,2,1,0:T(8,128)(2,1)}), bf16[8,2,16,1024]{3,2,1,0:T(8,128)(2,1)S(1)}, u32[]{:S(2)}, u32[]{:S(2)}) async-start(bf16[8,2,16,1024]{3,2,1,0:T(8,128)(2,1)} %broadcast_in_dim.8), calls=%async_computation.4 | async-start | bytes 1048576 | tf_op jit(solution)/shard_map/all_to_all | solution.py:17
  264.2 3.2 %copy-start.25 = (bf16[1024,1024]{1,0:T(8,128)(2,1)S(1)}, bf16[1024,1024]{1,0:T(8,128)(2,1)}, u32[]{:S(2)}) copy-start(bf16[1024,1024]{1,0:T(8,128)(2,1)} %constant_dynamic-update-slice_fusion) | copy-start | bytes 6291460
  267.4 1.6 copy-start.6
